TPU v7x, 32 devices: a whole 2x2x4 slice. The times are simulated.
32 devices in a mesh: sets: 16 (over z, x, core), tp: 2 (over y).
Axes of the slice: x: 2, y: 2, z: 4, core: 2. Of those that a mesh axis runs over, the one named last changes fastest.
Arguments:
- latents: bfloat16 [16384, 1024], P(('sets', 'tp')), may hold values from -6 to 6
- inputs: bfloat16 [16384, 1024], P(('sets', 'tp')), may hold values from -6 to 6
- neighbours: int32 [128, 512], P('sets'), may hold values from 0 to 1023
- key_counts: int32 [128], P('sets'), may hold values from 65 to 512, as said below
- filled: int32 [16], P('sets'), may hold values from 2 to 8, as said below
- cotangent: bfloat16 [16384, 1024], P(('sets', 'tp')), may hold values from -6 to 6
- cross_gain: float32 [1024], replicated, may hold values from 0.1 to 1.9
- cross_query: bfloat16 [1024, 1024], P(None, 'tp'), may hold values from -0.1875 to 0.1875
- cross_key: bfloat16 [1024, 1024], P(None, 'tp'), may hold values from -0.1875 to 0.1875
- cross_value: bfloat16 [1024, 1024], P(None, 'tp'), may hold values from -0.1875 to 0.1875
- cross_output: bfloat16 [1024, 1024], P('tp'), may hold values from -0.75 to 0.75
- self_gain: float32 [1024], replicated, may hold values from 0.1 to 1.9
- self_query: bfloat16 [1024, 1024], P(None, 'tp'), may hold values from -0.1875 to 0.1875
- self_key: bfloat16 [1024, 1024], P(None, 'tp'), may hold values from -0.1875 to 0.1875
- self_value: bfloat16 [1024, 1024], P(None, 'tp'), may hold values from -0.1875 to 0.1875
- self_output: bfloat16 [1024, 1024], P('tp'), may hold values from -0.5 to 0.5
- feed_gain: float32 [1024], replicated, may hold values from 0.1 to 1.9
- feed_up: bfloat16 [1024, 4096], P(None, 'tp'), may hold values from -0.1875 to 0.1875
- feed_down: bfloat16 [4096, 1024], P('tp'), may hold values from -0.09375 to 0.09375
Outputs:
- latents_out: bfloat16 [16384, 1024], P(('sets', 'tp'))
- latent_grad: float32 [16384, 1024], P(('sets', 'tp'))
- input_grad: float32 [16384, 1024], P(('sets', 'tp'))
- grad_cross_gain: float32 [1024], replicated
- grad_cross_query: float32 [1024, 1024], P(None, 'tp')
- grad_cross_key: float32 [1024, 1024], P(None, 'tp')
- grad_cross_value: float32 [1024, 1024], P(None, 'tp')
- grad_cross_output: float32 [1024, 1024], P('tp')
- grad_self_gain: float32 [1024], replicated
- grad_self_query: float32 [1024, 1024], P(None, 'tp')
- grad_self_key: float32 [1024, 1024], P(None, 'tp')
- grad_self_value: float32 [1024, 1024], P(None, 'tp')
- grad_self_output: float32 [1024, 1024], P('tp')
- grad_feed_gain: float32 [1024], replicated
- grad_feed_up: float32 [1024, 4096], P(None, 'tp')
- grad_feed_down: float32 [4096, 1024], P('tp')
- penalty: float32 [], replicated
Inputs may be any that keep to these rules, and one draw needn't show every extreme that they name: `neighbours`: each entry is a row of the group's own point set, counted from that set's first input embedding. Only the first key_counts[g] entries of group g's neighbour list count; some group has all 512. Groups of point set s numbered filled[s] and above are padding; some point set is full.
All inputs are finite; a program needn't handle non-finite values.
Results may differ from a plain program's by a relative error of at most 0.035.
Values may be sent and summed in bfloat16 or wider, within the bound.
No kernel may reach another device: no remote copies, remote signals or barrier semaphores. Data moves between devices by JAX's collectives and lax.ppermute only.
A program may use at most 256 MiB of HBM per device.

v0:
```python
import functools
import math

import jax
import jax.numpy as jnp
from jax import lax
from jax.sharding import PartitionSpec as P

HEAD_DIM = 128
GROUP = 128


epsilon = 1e-05
masked_score = -1e30
gelu_factor = 0.7978845608028654


def gelu_curve(values):
    return (
        0.5
        * values
        * (1.0 + jnp.tanh(gelu_factor * (values + 0.044715 * values * values * values)))
    )


def project(left_rows, right_rows):
    return jnp.dot(left_rows, right_rows, preferred_element_type=jnp.float32)


def times_transposed(left_rows, right_rows):
    return lax.dot_general(
        left_rows, right_rows, (((1,), (1,)), ((), ())), preferred_element_type=jnp.float32
    )


def transposed_times(left_rows, right_rows):
    return lax.dot_general(
        left_rows, right_rows, (((0,), (0,)), ((), ())), preferred_element_type=jnp.float32
    )


def norm_forward(values, gain):
    average = jnp.mean(values, axis=1, keepdims=True)
    centred = values - average
    variance = jnp.mean(centred * centred, axis=1, keepdims=True)
    inverse = lax.rsqrt(variance + epsilon)
    unit_rows = centred * inverse
    return (unit_rows, inverse, (unit_rows * gain).astype(jnp.bfloat16))


def norm_backward(grad_normed, unit_rows, inverse, gain):
    scaled = grad_normed * gain
    first_mean = jnp.mean(scaled, axis=1, keepdims=True)
    second_mean = jnp.mean(scaled * unit_rows, axis=1, keepdims=True)
    grad_rows = inverse * (scaled - first_mean - unit_rows * second_mean)
    return (grad_rows, jnp.sum(grad_normed * unit_rows, axis=0))


def row_terms(pairs, transposed):
    partial_value = []
    for left_rows, weight in pairs:
        if transposed:
            partial_value.append(times_transposed(left_rows, weight))
        else:
            partial_value.append(project(left_rows, weight))
    return functools.reduce(jnp.add, partial_value)


def spread_rows(rows_local):
    return lax.all_gather(rows_local, "tp", axis=0, tiled=True)


def spread_grads(rows_local):
    return lax.all_gather(rows_local, "tp", axis=0, tiled=True)


def collect_branch(left_rows, weight):
    return lax.psum_scatter(
        row_terms(((left_rows, weight),), False).astype(jnp.bfloat16),
        "tp",
        scatter_dimension=0,
        tiled=True,
    ).astype(jnp.float32)


def collect_normed(pairs):
    return lax.psum_scatter(
        row_terms(pairs, True).astype(jnp.bfloat16), "tp", scatter_dimension=0, tiled=True
    ).astype(jnp.float32)


def log_total(scores):
    row_top = jnp.max(scores, axis=-1, keepdims=True)
    return row_top[..., 0] + jnp.log(jnp.sum(jnp.exp(scores - row_top), axis=-1))


def pick_rows(table, chosen, head_count):
    picked = jnp.take(table, chosen.reshape(-1), axis=0)
    return picked.reshape(chosen.shape[0], chosen.shape[1], head_count, HEAD_DIM)


def cross_scores(query_block, key_rows, count_block, score_scale):
    scores = (
        jnp.einsum("gqhd,gkhd->ghqk", query_block, key_rows, preferred_element_type=jnp.float32)
        * score_scale
    )
    valid = (
        jnp.arange(key_rows.shape[1], dtype=jnp.int32)[None, None, None, :]
        < count_block[:, None, None, None]
    )
    return jnp.where(valid, scores, masked_score)


def cross_forward(
    queries, key_table, value_table, chosen, counts, block_groups, head_count, score_scale
):
    query_blocks = queries.reshape(-1, block_groups, GROUP, head_count, HEAD_DIM)
    chosen_blocks = chosen.reshape(-1, block_groups, chosen.shape[1])
    count_blocks = counts.reshape(-1, block_groups)

    def one_block(block_parts):
        query_block, chosen_block, count_block = block_parts
        key_rows = pick_rows(key_table, chosen_block, head_count)
        value_rows = pick_rows(value_table, chosen_block, head_count)
        scores = cross_scores(query_block, key_rows, count_block, score_scale)
        total_log = log_total(scores)
        attention_weights = jnp.exp(scores - total_log[..., None]).astype(jnp.bfloat16)
        attended = jnp.einsum(
            "ghqk,gkhd->gqhd", attention_weights, value_rows, preferred_element_type=jnp.float32
        )
        return (attended.astype(jnp.bfloat16), total_log)

    attended, total_logs = lax.map(one_block, (query_blocks, chosen_blocks, count_blocks))
    return (attended.reshape(queries.shape), total_logs)


def cross_backward(
    queries,
    key_table,
    value_table,
    chosen,
    counts,
    total_logs,
    grad_attended,
    block_groups,
    head_count,
    score_scale,
):
    query_blocks = queries.reshape(-1, block_groups, GROUP, head_count, HEAD_DIM)
    grad_blocks = grad_attended.reshape(-1, block_groups, GROUP, head_count, HEAD_DIM)
    chosen_blocks = chosen.reshape(-1, block_groups, chosen.shape[1])
    count_blocks = counts.reshape(-1, block_groups)
    row_width = key_table.shape[1]

    def one_block(accumulated, block_parts):
        grad_keys, grad_values = accumulated
        query_block, chosen_block, count_block, log_block, grad_block = block_parts
        key_rows = pick_rows(key_table, chosen_block, head_count)
        value_rows = pick_rows(value_table, chosen_block, head_count)
        scores = cross_scores(query_block, key_rows, count_block, score_scale)
        attention_weights = jnp.exp(scores - log_block[..., None])
        grad_weights = jnp.einsum(
            "gqhd,gkhd->ghqk", grad_block, value_rows, preferred_element_type=jnp.float32
        )
        inner_sum = jnp.sum(grad_weights * attention_weights, axis=-1, keepdims=True)
        grad_scores = (attention_weights * (grad_weights - inner_sum)).astype(jnp.bfloat16)
        grad_query = (
            jnp.einsum("ghqk,gkhd->gqhd", grad_scores, key_rows, preferred_element_type=jnp.float32)
            * score_scale
        )
        grad_key_rows = (
            jnp.einsum(
                "ghqk,gqhd->gkhd", grad_scores, query_block, preferred_element_type=jnp.float32
            )
            * score_scale
        )
        grad_value_rows = jnp.einsum(
            "ghqk,gqhd->gkhd",
            attention_weights.astype(jnp.bfloat16),
            grad_block,
            preferred_element_type=jnp.float32,
        )
        flat_index = chosen_block.reshape(-1)
        grad_keys = grad_keys.at[flat_index].add(grad_key_rows.reshape(-1, row_width))
        grad_values = grad_values.at[flat_index].add(grad_value_rows.reshape(-1, row_width))
        return ((grad_keys, grad_values), grad_query.astype(jnp.bfloat16))

    zero_table = jnp.zeros(key_table.shape, jnp.float32)
    (grad_keys, grad_values), grad_queries = lax.scan(
        one_block,
        (zero_table, zero_table),
        (query_blocks, chosen_blocks, count_blocks, total_logs, grad_blocks),
    )
    return (grad_queries.reshape(queries.shape), grad_keys, grad_values)


def self_forward(queries, keys_rows, values_rows, block_groups, head_count, score_scale):
    block_shape = (-1, block_groups, GROUP, head_count, HEAD_DIM)

    def one_block(block_parts):
        query_block, key_block, value_block = block_parts
        scores = (
            jnp.einsum(
                "gqhd,gkhd->ghqk", query_block, key_block, preferred_element_type=jnp.float32
            )
            * score_scale
        )
        total_log = log_total(scores)
        attention_weights = jnp.exp(scores - total_log[..., None]).astype(jnp.bfloat16)
        attended = jnp.einsum(
            "ghqk,gkhd->gqhd", attention_weights, value_block, preferred_element_type=jnp.float32
        )
        return (attended.astype(jnp.bfloat16), total_log)

    attended, total_logs = lax.map(
        one_block,
        (
            queries.reshape(block_shape),
            keys_rows.reshape(block_shape),
            values_rows.reshape(block_shape),
        ),
    )
    return (attended.reshape(queries.shape), total_logs)


def self_backward(
    queries,
    keys_rows,
    values_rows,
    total_logs,
    grad_attended,
    block_groups,
    head_count,
    score_scale,
):
    block_shape = (-1, block_groups, GROUP, head_count, HEAD_DIM)

    def one_block(block_parts):
        query_block, key_block, value_block, log_block, grad_block = block_parts
        scores = (
            jnp.einsum(
                "gqhd,gkhd->ghqk", query_block, key_block, preferred_element_type=jnp.float32
            )
            * score_scale
        )
        attention_weights = jnp.exp(scores - log_block[..., None])
        grad_weights = jnp.einsum(
            "gqhd,gkhd->ghqk", grad_block, value_block, preferred_element_type=jnp.float32
        )
        inner_sum = jnp.sum(grad_weights * attention_weights, axis=-1, keepdims=True)
        grad_scores = (attention_weights * (grad_weights - inner_sum)).astype(jnp.bfloat16)
        grad_query = (
            jnp.einsum(
                "ghqk,gkhd->gqhd", grad_scores, key_block, preferred_element_type=jnp.float32
            )
            * score_scale
        )
        grad_key = (
            jnp.einsum(
                "ghqk,gqhd->gkhd", grad_scores, query_block, preferred_element_type=jnp.float32
            )
            * score_scale
        )
        grad_value = jnp.einsum(
            "ghqk,gqhd->gkhd",
            attention_weights.astype(jnp.bfloat16),
            grad_block,
            preferred_element_type=jnp.float32,
        )
        return (
            grad_query.astype(jnp.bfloat16),
            grad_key.astype(jnp.bfloat16),
            grad_value.astype(jnp.bfloat16),
        )

    results = lax.map(
        one_block,
        (
            queries.reshape(block_shape),
            keys_rows.reshape(block_shape),
            values_rows.reshape(block_shape),
            total_logs,
            grad_attended.reshape(block_shape),
        ),
    )
    return tuple((result.reshape(queries.shape) for result in results))


def local(
    latents,
    inputs,
    neighbours,
    key_counts,
    filled,
    cotangent,
    cross_gain,
    cross_query,
    cross_key,
    cross_value,
    cross_output,
    self_gain,
    self_query,
    self_key,
    self_value,
    self_output,
    feed_gain,
    feed_up,
    feed_down,
):
    rows_dev = latents.shape[0]
    group_count = neighbours.shape[0]
    score_scale = 1.0 / math.sqrt(HEAD_DIM)
    local_groups = rows_dev // GROUP
    first_group = lax.axis_index("tp") * local_groups
    group_alive = (first_group + jnp.arange(local_groups, dtype=jnp.int32) < filled[0]).astype(
        jnp.float32
    )
    alive_rows = jnp.repeat(group_alive, GROUP)[:, None]
    (
        query_cross_all,
        key_cross_all,
        value_cross_all,
        query_self_all,
        key_self_all,
        value_self_all,
        up_all,
        output_cross_all,
        output_self_all,
        down_all,
    ) = (
        cross_query,
        cross_key,
        cross_value,
        self_query,
        self_key,
        self_value,
        feed_up,
        cross_output,
        self_output,
        feed_down,
    )
    head_count = query_cross_all.shape[1] // HEAD_DIM
    block_groups = math.gcd(neighbours.shape[0], max(1, 512 // GROUP))
    state_rows = latents.astype(jnp.float32)
    unit_cross, inverse_cross, normed_cross = norm_forward(state_rows, cross_gain)
    rows_cross = spread_rows(normed_cross)
    embedded = lax.all_gather(inputs, "tp", axis=0, tiled=True)
    key_table = project(embedded, key_cross_all).astype(jnp.bfloat16)
    value_table = project(embedded, value_cross_all).astype(jnp.bfloat16)
    queries_cross = project(rows_cross, query_cross_all).astype(jnp.bfloat16)
    attended_cross, logs_cross = cross_forward(
        queries_cross,
        key_table,
        value_table,
        neighbours,
        key_counts,
        block_groups,
        head_count,
        score_scale,
    )
    after_cross = state_rows + alive_rows * collect_branch(attended_cross, output_cross_all)
    unit_self, inverse_self, normed_self = norm_forward(after_cross, self_gain)
    rows_self = spread_rows(normed_self)
    queries_self = project(rows_self, query_self_all).astype(jnp.bfloat16)
    keys_self = project(rows_self, key_self_all).astype(jnp.bfloat16)
    values_self = project(rows_self, value_self_all).astype(jnp.bfloat16)
    attended_self, logs_self = self_forward(
        queries_self, keys_self, values_self, block_groups, head_count, score_scale
    )
    after_self = after_cross + alive_rows * collect_branch(attended_self, output_self_all)
    unit_feed, inverse_feed, normed_feed = norm_forward(after_self, feed_gain)
    rows_feed = spread_rows(normed_feed)
    hidden = project(rows_feed, up_all)
    activated = gelu_curve(hidden).astype(jnp.bfloat16)
    final_rows = after_self + alive_rows * collect_branch(activated, down_all)
    group_rms = jnp.sqrt(jnp.mean((final_rows * final_rows).reshape(local_groups, -1), axis=1))
    penalty_term = jnp.sum(group_rms * group_alive)
    grad_final = cotangent.astype(jnp.float32)
    grad_branch = spread_grads((alive_rows * grad_final).astype(jnp.bfloat16))
    grad_feed_down = transposed_times(activated, grad_branch)
    grad_activated = times_transposed(grad_branch, down_all)
    gelu_value, gelu_pull = jax.vjp(gelu_curve, hidden)
    grad_hidden = gelu_pull(grad_activated)[0].astype(jnp.bfloat16)
    grad_feed_up = transposed_times(rows_feed, grad_hidden)
    grad_normed_feed = collect_normed(((grad_hidden, up_all),))
    grad_rows, grad_feed_gain = norm_backward(grad_normed_feed, unit_feed, inverse_feed, feed_gain)
    grad_after_self = grad_final + grad_rows
    grad_branch = spread_grads((alive_rows * grad_after_self).astype(jnp.bfloat16))
    grad_self_output = transposed_times(attended_self, grad_branch)
    grad_attended = times_transposed(grad_branch, output_self_all).astype(jnp.bfloat16)
    grad_queries, grad_keys, grad_values = self_backward(
        queries_self,
        keys_self,
        values_self,
        logs_self,
        grad_attended,
        block_groups,
        head_count,
        score_scale,
    )
    grad_self_query = transposed_times(rows_self, grad_queries)
    grad_self_key = transposed_times(rows_self, grad_keys)
    grad_self_value = transposed_times(rows_self, grad_values)
    grad_normed_self = collect_normed(
        ((grad_queries, query_self_all), (grad_keys, key_self_all), (grad_values, value_self_all))
    )
    grad_rows, grad_self_gain = norm_backward(grad_normed_self, unit_self, inverse_self, self_gain)
    grad_after_cross = grad_after_self + grad_rows
    grad_branch = spread_grads((alive_rows * grad_after_cross).astype(jnp.bfloat16))
    grad_cross_output = transposed_times(attended_cross, grad_branch)
    grad_attended = times_transposed(grad_branch, output_cross_all).astype(jnp.bfloat16)
    grad_queries, grad_key_sum, grad_value_sum = cross_backward(
        queries_cross,
        key_table,
        value_table,
        neighbours,
        key_counts,
        logs_cross,
        grad_attended,
        block_groups,
        head_count,
        score_scale,
    )
    grad_cross_query = transposed_times(rows_cross, grad_queries)
    grad_key_table = grad_key_sum.astype(jnp.bfloat16)
    grad_value_table = grad_value_sum.astype(jnp.bfloat16)
    grad_cross_key = transposed_times(embedded, grad_key_table)
    grad_cross_value = transposed_times(embedded, grad_value_table)
    input_grad = lax.psum_scatter(
        row_terms(
            ((grad_key_table, key_cross_all), (grad_value_table, value_cross_all)), True
        ).astype(jnp.bfloat16),
        "tp",
        scatter_dimension=0,
        tiled=True,
    ).astype(jnp.float32)
    grad_normed_cross = collect_normed(((grad_queries, query_cross_all),))
    grad_rows, grad_cross_gain = norm_backward(
        grad_normed_cross, unit_cross, inverse_cross, cross_gain
    )
    latent_grad = grad_after_cross + grad_rows
    penalty_sum, grad_cross_gain, grad_self_gain, grad_feed_gain = lax.psum(
        (penalty_term, grad_cross_gain, grad_self_gain, grad_feed_gain), ("sets", "tp")
    )
    penalty = penalty_sum / (group_count * lax.axis_size("sets"))
    (
        grad_cross_query,
        grad_cross_key,
        grad_cross_value,
        grad_cross_output,
        grad_self_query,
        grad_self_key,
        grad_self_value,
        grad_self_output,
        grad_feed_up,
        grad_feed_down,
    ) = (
        lax.psum(grad_cross_query.astype(jnp.bfloat16), "sets").astype(jnp.float32),
        lax.psum(grad_cross_key.astype(jnp.bfloat16), "sets").astype(jnp.float32),
        lax.psum(grad_cross_value.astype(jnp.bfloat16), "sets").astype(jnp.float32),
        lax.psum(grad_cross_output.astype(jnp.bfloat16), "sets").astype(jnp.float32),
        lax.psum(grad_self_query.astype(jnp.bfloat16), "sets").astype(jnp.float32),
        lax.psum(grad_self_key.astype(jnp.bfloat16), "sets").astype(jnp.float32),
        lax.psum(grad_self_value.astype(jnp.bfloat16), "sets").astype(jnp.float32),
        lax.psum(grad_self_output.astype(jnp.bfloat16), "sets").astype(jnp.float32),
        lax.psum(grad_feed_up.astype(jnp.bfloat16), "sets").astype(jnp.float32),
        lax.psum(grad_feed_down.astype(jnp.bfloat16), "sets").astype(jnp.float32),
    )
    return (
        final_rows.astype(jnp.bfloat16),
        latent_grad,
        input_grad,
        grad_cross_gain,
        grad_cross_query,
        grad_cross_key,
        grad_cross_value,
        grad_cross_output,
        grad_self_gain,
        grad_self_query,
        grad_self_key,
        grad_self_value,
        grad_self_output,
        grad_feed_gain,
        grad_feed_up,
        grad_feed_down,
        penalty,
    )


def solution(mesh):
    return jax.shard_map(
        local,
        mesh=mesh,
        in_specs=(
            P(("sets", "tp"), None),
            P(("sets", "tp"), None),
            P("sets", None),
            P("sets"),
            P("sets"),
            P(("sets", "tp"), None),
            P(),
            P(None, "tp"),
            P(None, "tp"),
            P(None, "tp"),
            P("tp", None),
            P(),
            P(None, "tp"),
            P(None, "tp"),
            P(None, "tp"),
            P("tp", None),
            P(),
            P(None, "tp"),
            P("tp", None),
        ),
        out_specs=(
            P(("sets", "tp"), None),
            P(("sets", "tp"), None),
            P(("sets", "tp"), None),
            P(),
            P(None, "tp"),
            P(None, "tp"),
            P(None, "tp"),
            P("tp", None),
            P(),
            P(None, "tp"),
            P(None, "tp"),
            P(None, "tp"),
            P("tp", None),
            P(),
            P(None, "tp"),
            P("tp", None),
            P(),
        ),
        check_vma=False,
    )
```

profile of v0, /device:TPU:0, one launch (start us, length us, event | category | flops | bytes accessed | tf_op | source)
XLA Modules:
  0.0 1273.5 jit_solution(4469460067764060761)
XLA Ops:
  12.9 35.0 %all-gather.10.cloned.1.call-done = bf16[1024,1024]{1,0:T(8,128)(2,1)} async-done(((bf16[512,1024]{1,0:T(8,128)(2,1)}), bf16[1024,1024]{1,0:T(8,128)(2,1)}) %all-gather.10.cloned.1.call-update) | async-done | bytes 2097168 | tf_op jit(solution)/shard_map/all_gather | solution.py:70
  54.4 28.2 %all-gather.8.cloned.1.call-done = bf16[1024,1024]{1,0:T(8,128)(2,1)} async-done(((bf16[512,1024]{1,0:T(8,128)(2,1)}), bf16[1024,1024]{1,0:T(8,128)(2,1)}) %all-gather.8.cloned.1.call-update) | async-done | bytes 2097168 | tf_op jit(solution)/shard_map/all_gather | solution.py:347
  88.1 82.3 %while.52 = (s32[]{:T(128)}, bf16[2,4,128,4,128]{4,3,2,1,0:T(4,128)(2,1)}, f32[2,4,4,128]{3,2,1,0:T(4,128)S(1)}, s32[2,4,512]{2,1,0:T(4,128)S(1)}, bf16[1024,512...) while((s32[]{:T(128)}, ...), condition=%wide.region_5.7_spmd, body=%wide.region_2.6_spmd.sunk | while | flops 550785024 | bytes 53629124 | solution.py:133
  88.2 9.2 gather_fusion.1
  97.5 9.2 gather_fusion
  129.4 9.2 gather_fusion.1
  138.6 9.2 gather_fusion
  175.6 31.0 %reduce-scatter.8.cloned.1.call-done = bf16[512,1024]{1,0:T(8,128)(2,1)} async-done(((bf16[1024,1024]{1,0:T(8,128)(2,1)}), bf16[512,1024]{1,0:T(8,128)(2,1)}) %reduce-scatter.8.cloned.1.call-update) | async-done | bytes 1048592 | tf_op jit(solution)/shard_map/reduce_scatter | solution.py:78
  211.5 33.2 %all-gather.12.cloned.1.call-done = bf16[1024,1024]{1,0:T(8,128)(2,1)} async-done(((bf16[512,1024]{1,0:T(8,128)(2,1)}), bf16[1024,1024]{1,0:T(8,128)(2,1)}) %all-gather.12.cloned.1.call-update) | async-done | bytes 2097168 | tf_op jit(solution)/shard_map/all_gather | solution.py:70
  268.9 22.5 %while.53 = (s32[]{:T(128)}, bf16[2,4,128,4,128]{4,3,2,1,0:T(4,128)(2,1)}, f32[2,4,4,128]{3,2,1,0:T(4,128)S(1)}, bf16[2,4,128,4,128]{4,3,2,1,0:T(4,128)(2,1)}, b...) while((s32[]{:T(128)}, ...), condition=%wide.region_12.14_spmd, body=%wide.region_9.13_spmd.sunk | while | flops 136050688 | bytes 11601021 | solution.py:215
  295.8 31.4 %reduce-scatter.10.cloned.1.call-done = bf16[512,1024]{1,0:T(8,128)(2,1)} async-done(((bf16[1024,1024]{1,0:T(8,128)(2,1)}), bf16[512,1024]{1,0:T(8,128)(2,1)}) %reduce-scatter.10.cloned.1.call-update) | async-done | bytes 1048592 | tf_op jit(solution)/shard_map/reduce_scatter | solution.py:78
  332.8 29.5 %all-gather.16.cloned.1.call-done = bf16[1024,1024]{1,0:T(8,128)(2,1)} async-done(((bf16[512,1024]{1,0:T(8,128)(2,1)}), bf16[1024,1024]{1,0:T(8,128)(2,1)}) %all-gather.16.cloned.1.call-update) | async-done | bytes 2097168 | tf_op jit(solution)/shard_map/all_gather | solution.py:74
  362.3 10.9 fusion.152
  373.2 24.3 %all-gather.14.cloned.1.call-done = bf16[1024,1024]{1,0:T(8,128)(2,1)} async-done(((bf16[512,1024]{1,0:T(8,128)(2,1)}), bf16[1024,1024]{1,0:T(8,128)(2,1)}) %all-gather.14.cloned.1.call-update) | async-done | bytes 2097168 | tf_op jit(solution)/shard_map/all_gather | solution.py:70
  397.6 15.7 %fusion.80 = (bf16[1024,2048]{1,0:T(8,128)(2,1)S(1)}, f32[1024,2048]{1,0:T(8,128)}) fusion(f32[1024,2048]{1,0:T(8,128)} %fusion.152, bf16[1024,1024]{1,0:T(8,128)(2,1)} %all-gather.14.cloned.1.call-done, bf16[1024,2048]{1,0:T(8,128)(2,1)} %param.46), kind=kOutput, calls=%fused_computation.139 | convolution fusion | flops 4345298944 | bytes 27262976 | tf_op jit(solution)/shard_map/dot_general | solution.py:27
  415.3 5.7 convolution_convert_fusion.5
  421.3 11.0 convolution_convert_fusion.6
  432.3 20.7 %reduce-scatter.14.cloned.1.call-done = bf16[512,1024]{1,0:T(8,128)(2,1)} async-done(((bf16[1024,1024]{1,0:T(8,128)(2,1)}), bf16[512,1024]{1,0:T(8,128)(2,1)}) %reduce-scatter.14.cloned.1.call-update) | async-done | bytes 1048592 | tf_op jit(solution)/shard_map/reduce_scatter | solution.py:87
  453.0 34.8 %reduce-scatter.12.cloned.1.call-done = bf16[512,1024]{1,0:T(8,128)(2,1)} async-done(((bf16[1024,1024]{1,0:T(8,128)(2,1)}), bf16[512,1024]{1,0:T(8,128)(2,1)}) %reduce-scatter.12.cloned.1.call-update) | async-done | bytes 1048592 | tf_op jit(solution)/shard_map/reduce_scatter | solution.py:78
  487.8 5.1 fusion.105
  495.8 33.0 %all-gather.18.cloned.1.call-done = bf16[1024,1024]{1,0:T(8,128)(2,1)} async-done(((bf16[512,1024]{1,0:T(8,128)(2,1)}), bf16[1024,1024]{1,0:T(8,128)(2,1)}) %all-gather.18.cloned.1.call-update) | async-done | bytes 2097168 | tf_op jit(solution)/shard_map/all_gather | solution.py:74
  538.6 29.6 %while.54 = (s32[]{:T(128)}, bf16[2,4,128,4,128]{4,3,2,1,0:T(4,128)(2,1)}, bf16[2,4,128,4,128]{4,3,2,1,0:T(4,128)(2,1)}, bf16[2,4,128,4,128]{4,3,2,1,0:T(4,128)(...) while((s32[]{:T(128)}, ...), condition=%wide.region_22.24_spmd, body=%wide.region_20.23_spmd.sunk | while | flops 338950144 | bytes 65578456 | solution.py:276
  575.5 31.9 %reduce-scatter.16.cloned.1.call-done = bf16[512,1024]{1,0:T(8,128)(2,1)} async-done(((bf16[1024,1024]{1,0:T(8,128)(2,1)}), bf16[512,1024]{1,0:T(8,128)(2,1)}) %reduce-scatter.16.cloned.1.call-update) | async-done | bytes 1048592 | tf_op jit(solution)/shard_map/reduce_scatter | solution.py:87
  614.6 33.2 %all-gather.20.cloned.1.call-done = bf16[1024,1024]{1,0:T(8,128)(2,1)} async-done(((bf16[512,1024]{1,0:T(8,128)(2,1)}), bf16[1024,1024]{1,0:T(8,128)(2,1)}) %all-gather.20.cloned.1.call-update) | async-done | bytes 2097168 | tf_op jit(solution)/shard_map/all_gather | solution.py:74
  656.5 200.0 %while.55 = (s32[]{:T(128)}, f32[1024,512]{1,0:T(8,128)}, f32[1024,512]{1,0:T(8,128)}, bf16[2,4,128,4,128]{4,3,2,1,0:T(4,128)(2,1)}, s32[2,4,512]{2,1,0:T(4,128)...) while((s32[]{:T(128)}, f32[1024,512]{1,0:T(8,128)}, ...), condition=%wide.region_30.32_spmd, body=%wide.region_26.31_spmd.sunk | while | flops 1363699712 | bytes 140169520 | solution.py:189
  658.3 9.2 gather_fusion.3
  667.5 9.2 gather_fusion.2
  684.5 4.3 copy.306
  703.3 5.3 copy.308
  708.5 17.2 %scatter_custom_fusion.11 = f32[1024,512]{1,0:T(8,128)} fusion(f32[1024,512]{1,0:T(8,128)} %get-tuple-element.830, s32[2048]{0:T(1024)S(1)} %bitcast.321, f32[256,8,4,128]{3,2,1,0:T(4,128)} %bitcast.303), kind=kCustom, calls=%fused_computation.87.clone.1 | custom fusion | flops 1048576 | bytes 6291456 | tf_op jit(solution)/shard_map/while/body/eval_jaxpr/scatter-add | solution.py:185
  729.9 4.3 multiply_bitcast_fusion.2
  734.2 5.3 copy.307
  739.5 17.2 %scatter_custom_fusion.10 = f32[1024,512]{1,0:T(8,128)} fusion(f32[1024,512]{1,0:T(8,128)} %get-tuple-element.829, s32[2048]{0:T(1024)S(1)} %bitcast.322, f32[256,8,4,128]{3,2,1,0:T(4,128)} %bitcast.302), kind=kCustom, calls=%fused_computation.90.clone.1 | custom fusion | flops 1048576 | bytes 6291456 | tf_op jit(solution)/shard_map/while/body/eval_jaxpr/scatter-add | solution.py:184
  758.1 9.2 gather_fusion.3
  767.3 9.2 gather_fusion.2
  784.3 4.3 copy.306
  803.0 5.3 copy.308
  808.3 17.2 %scatter_custom_fusion.11 = f32[1024,512]{1,0:T(8,128)} fusion(f32[1024,512]{1,0:T(8,128)} %get-tuple-element.830, s32[2048]{0:T(1024)S(1)} %bitcast.321, f32[256,8,4,128]{3,2,1,0:T(4,128)} %bitcast.303), kind=kCustom, calls=%fused_computation.87.clone.1 | custom fusion | flops 1048576 | bytes 6291456 | tf_op jit(solution)/shard_map/while/body/eval_jaxpr/scatter-add | solution.py:185
  829.7 4.3 multiply_bitcast_fusion.2
  834.0 5.3 copy.307
  839.3 17.2 %scatter_custom_fusion.10 = f32[1024,512]{1,0:T(8,128)} fusion(f32[1024,512]{1,0:T(8,128)} %get-tuple-element.829, s32[2048]{0:T(1024)S(1)} %bitcast.322, f32[256,8,4,128]{3,2,1,0:T(4,128)} %bitcast.302), kind=kCustom, calls=%fused_computation.90.clone.1 | custom fusion | flops 1048576 | bytes 6291456 | tf_op jit(solution)/shard_map/while/body/eval_jaxpr/scatter-add | solution.py:184
  856.6 4.1 convolution_convert_fusion.4
  860.8 9.5 convolution_convert_fusion.3
  875.1 12.1 convolution_convert_fusion.2
  909.4 40.0 %all-reduce = (f32[1024]{0:T(1024)}, f32[1024]{0:T(1024)}, f32[1024]{0:T(1024)}, f32[]{:T(128)}) all-reduce(f32[1024]{0:T(1024)S(1)} %get-tuple-element.369, f32[1024]{0:T(1024)S(1)} %copy-done.70, f32[1024]{0:T(1024)S(1)} %copy-done.72, f32[]{:T(128)} %fusion.147), channel_id=1, replica_groups=mesh['sets'=16,'tp'=2] {'sets','tp'}, use_global_device_ids=true, to_apply=%region_36.38 | all-reduce | flops 3073 | bytes 24584 | tf_op jit(solution)/shard_map/psum | solution.py:442
  955.1 286.7 %all-reduce.4.cloned.1.call-done = (bf16[1024,512]{0,1:T(8,128)(2,1)}, bf16[1024,512]{0,1:T(8,128)(2,1)}, bf16[1024,512]{1,0:T(8,128)(2,1)}, bf16[512,1024]{1,0:...) async-done(((bf16[1024,512]{0,1:T(8,128)(2,1)}, ...) | async-done | bytes 16777232 | tf_op jit(solution)/shard_map/psum | solution.py:459
  1256.6 4.4 convert_element_type.283
  1261.0 4.4 convert_element_type.285
  (428 shorter events, 298.5 us)
Async XLA Ops:
  7.2 284.1 %copy-start = (bf16[512,1024]{1,0:T(8,128)(2,1)S(1)}, bf16[512,1024]{1,0:T(8,128)(2,1)}, u32[]{:S(2)}) copy-start(bf16[512,1024]{1,0:T(8,128)(2,1)} %param.44) | copy-start | bytes 3145732
  7.2 3.3 copy-start.5
  7.2 3.3 copy-start.66
  7.2 40.7 %all-gather.10.cloned.1.call-start = ((), (), s32[]{:S(2)}) async-start(), calls=%async_computation.8 | async-start | bytes 3145728 | tf_op jit(solution)/shard_map/all_gather | solution.py:70
  8.9 3.1 copy-start.62
  11.9 36.0 %copy-start.81 = (bf16[1024,512]{1,0:T(8,128)(2,1)S(1)}, bf16[1024,512]{1,0:T(8,128)(2,1)}, u32[]{:S(2)}) copy-start(bf16[1024,512]{1,0:T(8,128)(2,1)} %param.36) | copy-start | bytes 3145732
  11.9 70.7 %all-gather.8.cloned.1.call-start = ((), (), s32[]{:S(2)}) async-start(), calls=%async_computation.7 | async-start | bytes 3145728 | tf_op jit(solution)/shard_map/all_gather | solution.py:347
  12.7 193.8 %reduce-scatter.8.cloned.1.call-start = ((), (), s32[]{:S(2)}) async-start(), calls=%async_computation.9 | async-start | bytes 3145728 | tf_op jit(solution)/shard_map/reduce_scatter | solution.py:78
  51.7 30.9 %copy-start.43 = (bf16[1024,512]{1,0:T(8,128)(2,1)S(1)}, bf16[1024,512]{1,0:T(8,128)(2,1)}, u32[]{:S(2)}) copy-start(bf16[1024,512]{1,0:T(8,128)(2,1)} %param.37) | copy-start | bytes 3145732
  82.6 3.0 copy-start.45
  82.6 3.0 copy-start.76
  174.6 70.2 %all-gather.12.cloned.1.call-start = ((), (), s32[]{:S(2)}) async-start(), calls=%async_computation.10 | async-start | bytes 3145728 | tf_op jit(solution)/shard_map/all_gather | solution.py:70
  175.6 33.9 %copy-start.64 = (f32[1024]{0:T(1024)S(1)}, f32[1024]{0:T(1024)}, u32[]{:S(2)}) copy-start(f32[1024]{0:T(1024)} %param.40) | copy-start | bytes 12292
  211.4 115.7 %reduce-scatter.10.cloned.1.call-start = ((), (), s32[]{:S(2)}) async-start(), calls=%async_computation.11 | async-start | bytes 3145728 | tf_op jit(solution)/shard_map/reduce_scatter | solution.py:78
  295.1 67.1 %all-gather.16.cloned.1.call-start = ((), (), s32[]{:S(2)}) async-start(), calls=%async_computation.14 | async-start | bytes 3145728 | tf_op jit(solution)/shard_map/all_gather | solution.py:74
  295.7 101.8 %all-gather.14.cloned.1.call-start = ((), (), s32[]{:S(2)}) async-start(), calls=%async_computation.12 | async-start | bytes 3145728 | tf_op jit(solution)/shard_map/all_gather | solution.py:70
  332.3 120.7 %reduce-scatter.14.cloned.1.call-start = ((), (), s32[]{:S(2)}) async-start(), calls=%async_computation.15 | async-start | bytes 3145728 | tf_op jit(solution)/shard_map/reduce_scatter | solution.py:87
  397.6 17.8 %copy-start.74 = (bf16[1024,2048]{1,0:T(8,128)(2,1)S(1)}, bf16[1024,2048]{1,0:T(8,128)(2,1)}, u32[]{:S(2)}) copy-start(bf16[1024,2048]{1,0:T(8,128)(2,1)} %param.46) | copy-start | bytes 12582916
  421.1 66.8 %reduce-scatter.12.cloned.1.call-start = ((), (), s32[]{:S(2)}) async-start(), calls=%async_computation.13 | async-start | bytes 3145728 | tf_op jit(solution)/shard_map/reduce_scatter | solution.py:78
  432.3 96.6 %all-gather.18.cloned.1.call-start = ((), (), s32[]{:S(2)}) async-start(), calls=%async_computation.16 | async-start | bytes 3145728 | tf_op jit(solution)/shard_map/all_gather | solution.py:74
  487.8 5.1 copy-start.16
  487.8 5.1 copy-start.34
  487.8 5.1 copy-start.38
  495.6 111.8 %reduce-scatter.16.cloned.1.call-start = ((), (), s32[]{:S(2)}) async-start(), calls=%async_computation.17 | async-start | bytes 3145728 | tf_op jit(solution)/shard_map/reduce_scatter | solution.py:87
  538.6 3.6 copy-start.11
  538.6 3.6 copy-start.13
  553.4 3.6 copy-start.11
  553.4 3.6 copy-start.13
  568.2 3.0 copy-start.80
  575.4 32.0 %copy-start.7 = (bf16[512,1024]{1,0:T(8,128)(2,1)S(1)}, bf16[512,1024]{1,0:T(8,128)(2,1)}, u32[]{:S(2)}) copy-start(bf16[512,1024]{1,0:T(8,128)(2,1)} %param.29) | copy-start | bytes 3145732
  575.4 72.4 %all-gather.20.cloned.1.call-start = ((), (), s32[]{:S(2)}) async-start(), calls=%async_computation.18 | async-start | bytes 3145728 | tf_op jit(solution)/shard_map/all_gather | solution.py:74
  607.4 3.7 copy-start.21
  607.4 3.7 copy-start.23
  614.6 292.6 %reduce-scatter.18.cloned.1.call-start = ((), (), s32[]{:S(2)}) async-start(), calls=%async_computation.19 | async-start | bytes 3145728 | tf_op jit(solution)/shard_map/reduce_scatter | solution.py:87
  725.7 4.2 copy-start.10
  825.5 4.2 copy-start.10
  860.8 9.6 copy-start.22
  860.8 9.6 copy-start.44
  860.8 89.3 %reduce-scatter.20.cloned.1.call-start = ((), (), s32[]{:S(2)}) async-start(), calls=%async_computation.20 | async-start | bytes 3145728 | tf_op jit(solution)/shard_map/reduce_scatter | solution.py:429
  874.8 12.4 copy-start.37
  874.8 367.0 %all-reduce.4.cloned.1.call-start = ((), (), s32[]{:S(2)}) async-start(), calls=%async_computation.21 | async-start | bytes 33554432 | tf_op jit(solution)/shard_map/psum | solution.py:459
  875.1 12.1 copy-start.39
  905.8 3.6 copy-start.70
  905.8 3.6 copy-start.72
  909.4 43.6 %copy-start.24 = (f32[512,1024]{1,0:T(8,128)S(1)}, f32[512,1024]{1,0:T(8,128)}, u32[]{:S(2)}) copy-start(f32[512,1024]{1,0:T(8,128)} %get-tuple-element.462) | copy-start | bytes 6291460
  1252.5 4.0 copy-start.28
  1256.6 4.5 copy-start.27
  1261.0 4.4 copy-start.1
  (69 other events, 126.8 us)
Sparse Core Ops, SparseCore 0:
  12.1 35.8 all-gather.9
  49.5 33.1 all-gather.7
  174.7 31.8 reduce-scatter.7
  211.6 33.1 all-gather.11
  295.3 31.8 reduce-scatter.9
  329.1 33.1 all-gather.15
  364.4 33.1 all-gather.13
  421.2 31.8 reduce-scatter.13
  455.9 31.8 reduce-scatter.11
  495.7 33.1 all-gather.17
  575.5 31.8 reduce-scatter.15
  614.7 33.1 all-gather.19
  860.9 31.8 reduce-scatter.17
  895.4 32.5 reduce-scatter.19
  936.5 305.2 all-reduce.3
where the time goes:
time: 1280 us; the launch traced here: 1270 us
  waiting for transfers between devices  655 us (51%)
  local copies, waits for them, and re-layouts  230 us (18%)
  matrix products  183 us (14%)
  other arithmetic  145 us (11%)
  blocking collectives  40 us (3%)
  between operations  17.4 us (1%)
    psum x1, waiting for transfers between devices, local(): lax.psum(grad_cross_key.astype(jnp.bfloat16), 'sets').astype(jnp.float32)  287 us
    reduce_scatter x3, waiting for transfers between devices, collect_branch(): lax.psum_scatter(row_terms(((left_rows, weight),), False).astype(jnp.bflo...  97.1 us
    all_gather x3, waiting for transfers between devices, spread_grads(): return lax.all_gather(rows_local, 'tp', axis=0, tiled=True)  95.8 us
    all_gather x3, waiting for transfers between devices, spread_rows(): return lax.all_gather(rows_local, 'tp', axis=0, tiled=True)  92.6 us
    gather x8, local copies, waits for them, and re-layouts, pick_rows(): picked = jnp.take(table, chosen.reshape(-1), axis=0)  73.6 us
    dot_general x10, matrix products, project(): return jnp.dot(left_rows, right_rows, preferred_element_type=jnp.float32)  54 us
    reduce_scatter x3, waiting for transfers between devices, collect_normed(): lax.psum_scatter(row_terms(pairs, True).astype(jnp.bfloat16), 'tp', scatt...  52.6 us
    reshape x10, local copies, waits for them, and re-layouts, pick_rows(): picked.reshape(chosen.shape[0], chosen.shape[1], head_count, HEAD_DIM)  40.1 us
  transfers between devices with their start and end apart: 15, of which 13 were waited for; matrix products, arithmetic and copies ran while one was open for 7% of the time, Pallas kernels for 0%

commit v1 on v0

v1 whole, which is shorter than its diff:
```python
import functools
import math

import jax
import jax.numpy as jnp
from jax import lax
from jax.experimental import pallas as pl
from jax.experimental.pallas import tpu as pltpu
from jax.sharding import PartitionSpec as P

HEAD_DIM = 128
GROUP = 128

epsilon = 1e-05
masked_score = -1e30
gelu_factor = 0.7978845608028654
gelu_cubic = 0.044715
log2_e = 1.4426950408889634
vmem_bytes = 60 * 1024 * 1024


def project(left_rows, right_rows):
    return jnp.dot(left_rows, right_rows, preferred_element_type=jnp.float32)


def times_transposed(left_rows, right_rows):
    return lax.dot_general(
        left_rows, right_rows, (((1,), (1,)), ((), ())), preferred_element_type=jnp.float32
    )


def transposed_times(left_rows, right_rows):
    return lax.dot_general(
        left_rows, right_rows, (((0,), (0,)), ((), ())), preferred_element_type=jnp.float32
    )


def norm_forward(values, gain):
    average = jnp.mean(values, axis=1, keepdims=True)
    centred = values - average
    variance = jnp.mean(centred * centred, axis=1, keepdims=True)
    inverse = lax.rsqrt(variance + epsilon)
    unit_rows = centred * inverse
    return (unit_rows, inverse, (unit_rows * gain).astype(jnp.bfloat16))


def norm_backward(grad_normed, unit_rows, inverse, gain):
    scaled = grad_normed * gain
    first_mean = jnp.mean(scaled, axis=1, keepdims=True)
    second_mean = jnp.mean(scaled * unit_rows, axis=1, keepdims=True)
    grad_rows = inverse * (scaled - first_mean - unit_rows * second_mean)
    return (grad_rows, jnp.sum(grad_normed * unit_rows, axis=0))


def from_peer(block, step):
    count = lax.axis_size("tp")
    return lax.ppermute(block, "tp", [(source, (source - step) % count) for source in range(count)])


def to_peer(block, step):
    count = lax.axis_size("tp")
    return lax.ppermute(block, "tp", [(source, (source + step) % count) for source in range(count)])


def gather_blocks(block):
    return [block] + [from_peer(block, step) for step in range(1, lax.axis_size("tp"))]


def sum_blocks(make_partial):
    received = [
        to_peer(make_partial(step).astype(jnp.bfloat16), step)
        for step in range(1, lax.axis_size("tp"))
    ]
    total = make_partial(0)
    for term in received:
        total = total + term.astype(jnp.float32)
    return total


def swap_sets(block, bit):
    count = lax.axis_size("sets")
    return lax.ppermute(block, "sets", [(source, source ^ (1 << bit)) for source in range(count)])


def set_bit(bit):
    return (lax.axis_index("sets") >> bit) & 1


def halves(block, bit):
    half = block.shape[0] // 2
    mine = set_bit(bit)
    kept = lax.dynamic_slice_in_dim(block, mine * half, half, 0)
    sent = lax.dynamic_slice_in_dim(block, (1 - mine) * half, half, 0)
    return (kept, sent)


def add_pair(kept, received):
    return (kept.astype(jnp.float32) + received.astype(jnp.float32)).astype(jnp.bfloat16)


def scatter_sets(block, bits):
    for bit in bits:
        kept, sent = halves(block, bit)
        block = add_pair(kept, swap_sets(sent, bit))
    return block


def spread_sets(block, bits):
    for bit in reversed(bits):
        received = swap_sets(block, bit)
        first = set_bit(bit) == 0
        block = jnp.concatenate(
            [jnp.where(first, block, received), jnp.where(first, received, block)], axis=0
        )
    return block


def all_bits():
    return list(range(int(math.log2(lax.axis_size("sets")))))


def sum_sets(block, bits):
    return spread_sets(scatter_sets(block.astype(jnp.bfloat16), bits), bits).astype(jnp.float32)


def sum_everywhere(block):
    for bit in all_bits():
        block = block + swap_sets(block, bit)
    count = lax.axis_size("tp")
    step = 1
    while step < count:
        block = block + lax.ppermute(
            block, "tp", [(source, source ^ step) for source in range(count)]
        )
        step *= 2
    return block


def multiplicity_kernel(chosen_ref, out_ref):
    row_count = out_ref.shape[0]
    group_count, key_count = chosen_ref.shape
    row_ids = lax.broadcasted_iota(jnp.int32, (row_count, key_count), 0) + (
        pl.program_id(0) * row_count
    )
    lanes = lax.broadcasted_iota(jnp.int32, (key_count, 128), 1)

    def one_group(group, total):
        picked = chosen_ref[pl.ds(group, 1), :]
        hits = jnp.where(row_ids == picked, 1.0, 0.0).astype(jnp.bfloat16)
        place = jnp.where(lanes == group, 1.0, 0.0).astype(jnp.bfloat16)
        return total + project(hits, place)

    total = lax.fori_loop(0, group_count, one_group, jnp.zeros((row_count, 128), jnp.float32))
    out_ref[...] = jnp.where(total > 0.0, jnp.log2(jnp.maximum(total, 1.0)), masked_score)


def log_multiplicity(chosen, counts, table_rows):
    group_count, key_count = chosen.shape
    valid = jnp.arange(key_count, dtype=jnp.int32)[None, :] < counts[:, None]
    chosen = jnp.where(valid, chosen, -1)
    block = math.gcd(table_rows, 512)
    return pl.pallas_call(
        multiplicity_kernel,
        grid=(table_rows // block,),
        in_specs=[pl.BlockSpec((group_count, key_count), lambda i: (0, 0))],
        out_specs=pl.BlockSpec((block, 128), lambda i: (i, 0)),
        out_shape=jax.ShapeDtypeStruct((table_rows, 128), jnp.float32),
        name="multiplicity",
    )(chosen)


def fill_bias(counts_ref, bias_ref, span):
    row_count = bias_ref.shape[0]
    lanes = lax.broadcasted_iota(jnp.int32, (row_count, 128), 1)
    counts = counts_ref[...]
    for part in range(span):
        group = pl.program_id(0) * span + part
        column = jnp.sum(jnp.where(lanes == group, counts, 0.0), axis=1, keepdims=True)
        bias_ref[:, part * GROUP : (part + 1) * GROUP] = jnp.broadcast_to(
            column, (row_count, GROUP)
        )


def cross_forward_kernel(
    counts_ref, query_ref, key_ref, value_t_ref, out_ref, log_ref, bias_ref, *, heads, span, scale
):
    fill_bias(counts_ref, bias_ref, span)
    for head in range(heads):
        cols = slice(head * HEAD_DIM, (head + 1) * HEAD_DIM)
        scores = times_transposed(key_ref[:, cols], query_ref[:, cols])
        scores = scores * (scale * log2_e) + bias_ref[...]
        top = jnp.max(scores, axis=0, keepdims=True)
        raised = jnp.exp2(scores - top)
        total = jnp.sum(raised, axis=0, keepdims=True)
        mixed = project(value_t_ref[cols, :], raised.astype(jnp.bfloat16)) / total
        out_ref[:, cols] = mixed.T.astype(jnp.bfloat16)
        log_ref[0, head : head + 1, :] = top + jnp.log2(total)


def cross_forward(log_counts, queries, key_table, value_table_t, scale):
    row_count, width = queries.shape
    table_rows = key_table.shape[0]
    heads = width // HEAD_DIM
    groups = row_count // GROUP
    span = 2 if groups % 2 == 0 else 1
    rows = span * GROUP
    work = row_count * table_rows * width
    return pl.pallas_call(
        functools.partial(cross_forward_kernel, heads=heads, span=span, scale=scale),
        grid=(groups // span,),
        in_specs=[
            pl.BlockSpec((table_rows, 128), lambda i: (0, 0)),
            pl.BlockSpec((rows, width), lambda i: (i, 0)),
            pl.BlockSpec((table_rows, width), lambda i: (0, 0)),
            pl.BlockSpec((width, table_rows), lambda i: (0, 0)),
        ],
        out_specs=[
            pl.BlockSpec((rows, width), lambda i: (i, 0)),
            pl.BlockSpec((1, heads, rows), lambda i: (i, 0, 0)),
        ],
        out_shape=[
            jax.ShapeDtypeStruct((row_count, width), jnp.bfloat16),
            jax.ShapeDtypeStruct((groups // span, heads, rows), jnp.float32),
        ],
        scratch_shapes=[pltpu.VMEM((table_rows, rows), jnp.float32)],
        compiler_params=pltpu.CompilerParams(vmem_limit_bytes=vmem_bytes),
        cost_estimate=pl.CostEstimate(
            flops=8 * work, transcendentals=work // HEAD_DIM, bytes_accessed=4 * queries.size * 2
        ),
        name="cross_forward",
    )(log_counts, queries, key_table, value_table_t)


def cross_backward_kernel(
    counts_ref,
    query_ref,
    grad_ref,
    log_ref,
    key_ref,
    key_t_ref,
    value_ref,
    grad_query_ref,
    grad_key_ref,
    grad_value_ref,
    bias_ref,
    key_sum_ref,
    value_sum_ref,
    *,
    heads,
    span,
    scale,
):
    step = pl.program_id(0)

    @pl.when(step == 0)
    def _():
        key_sum_ref[...] = jnp.zeros_like(key_sum_ref)
        value_sum_ref[...] = jnp.zeros_like(value_sum_ref)

    fill_bias(counts_ref, bias_ref, span)
    for head in range(heads):
        cols = slice(head * HEAD_DIM, (head + 1) * HEAD_DIM)
        query = query_ref[:, cols]
        grad = grad_ref[:, cols]
        scores = times_transposed(key_ref[:, cols], query)
        weights = jnp.exp2(
            scores * (scale * log2_e) + bias_ref[...] - log_ref[0, head : head + 1, :]
        )
        grad_weights = times_transposed(value_ref[:, cols], grad)
        inner = jnp.sum(weights * grad_weights, axis=0, keepdims=True)
        grad_scores = (weights * (grad_weights - inner)).astype(jnp.bfloat16)
        value_sum_ref[:, cols] += project(weights.astype(jnp.bfloat16), grad)
        key_sum_ref[:, cols] += project(grad_scores, query)
        grad_query = project(key_t_ref[cols, :], grad_scores) * scale
        grad_query_ref[:, cols] = grad_query.T.astype(jnp.bfloat16)

    @pl.when(step == pl.num_programs(0) - 1)
    def _():
        grad_key_ref[...] = (key_sum_ref[...] * scale).astype(jnp.bfloat16)
        grad_value_ref[...] = value_sum_ref[...].astype(jnp.bfloat16)


def cross_backward(
    log_counts, queries, grad_attended, logs, key_table, key_table_t, value_table, scale
):
    row_count, width = queries.shape
    table_rows = key_table.shape[0]
    heads = width // HEAD_DIM
    groups = row_count // GROUP
    span = 2 if groups % 2 == 0 else 1
    rows = span * GROUP
    work = row_count * table_rows * width
    whole = pl.BlockSpec((table_rows, width), lambda i: (0, 0))
    block = pl.BlockSpec((rows, width), lambda i: (i, 0))
    return pl.pallas_call(
        functools.partial(cross_backward_kernel, heads=heads, span=span, scale=scale),
        grid=(groups // span,),
        in_specs=[
            pl.BlockSpec((table_rows, 128), lambda i: (0, 0)),
            block,
            block,
            pl.BlockSpec((1, heads, rows), lambda i: (i, 0, 0)),
            whole,
            pl.BlockSpec((width, table_rows), lambda i: (0, 0)),
            whole,
        ],
        out_specs=[block, whole, whole],
        out_shape=[
            jax.ShapeDtypeStruct((row_count, width), jnp.bfloat16),
            jax.ShapeDtypeStruct((table_rows, width), jnp.bfloat16),
            jax.ShapeDtypeStruct((table_rows, width), jnp.bfloat16),
        ],
        scratch_shapes=[
            pltpu.VMEM((table_rows, rows), jnp.float32),
            pltpu.VMEM((table_rows, width), jnp.float32),
            pltpu.VMEM((table_rows, width), jnp.float32),
        ],
        compiler_params=pltpu.CompilerParams(vmem_limit_bytes=vmem_bytes),
        cost_estimate=pl.CostEstimate(
            flops=20 * work, transcendentals=work // HEAD_DIM, bytes_accessed=8 * queries.size * 2
        ),
        name="cross_backward",
    )(log_counts, queries, grad_attended, logs, key_table, key_table_t, value_table)


def head_columns(head, heads_block):
    base = (head // heads_block) * 3 * heads_block + head % heads_block
    return [
        slice((base + kind * heads_block) * HEAD_DIM, (base + kind * heads_block + 1) * HEAD_DIM)
        for kind in range(3)
    ]


def self_forward_kernel(rows_ref, out_ref, log_ref, *, heads, heads_block, scale):
    for head in range(heads):
        query_cols, key_cols, value_cols = head_columns(head, heads_block)
        scores = times_transposed(rows_ref[:, key_cols], rows_ref[:, query_cols])
        scores = scores * (scale * log2_e)
        top = jnp.max(scores, axis=0, keepdims=True)
        raised = jnp.exp2(scores - top)
        total = jnp.sum(raised, axis=0, keepdims=True)
        weights = (raised / total).astype(jnp.bfloat16)
        mixed = transposed_times(weights, rows_ref[:, value_cols])
        out_ref[:, head * HEAD_DIM : (head + 1) * HEAD_DIM] = mixed.astype(jnp.bfloat16)
        log_ref[0, head : head + 1, :] = top + jnp.log2(total)


def self_forward(mixed_rows, heads, heads_block, scale):
    row_count, width = mixed_rows.shape
    groups = row_count // GROUP
    return pl.pallas_call(
        functools.partial(
            self_forward_kernel, heads=heads, heads_block=heads_block, scale=scale
        ),
        grid=(groups,),
        in_specs=[pl.BlockSpec((GROUP, width), lambda i: (i, 0))],
        out_specs=[
            pl.BlockSpec((GROUP, heads * HEAD_DIM), lambda i: (i, 0)),
            pl.BlockSpec((1, heads, GROUP), lambda i: (i, 0, 0)),
        ],
        out_shape=[
            jax.ShapeDtypeStruct((row_count, heads * HEAD_DIM), jnp.bfloat16),
            jax.ShapeDtypeStruct((groups, heads, GROUP), jnp.float32),
        ],
        cost_estimate=pl.CostEstimate(
            flops=8 * row_count * GROUP * heads * HEAD_DIM,
            transcendentals=row_count * GROUP * heads,
            bytes_accessed=3 * mixed_rows.size,
        ),
        name="self_forward",
    )(mixed_rows)


def self_backward_kernel(rows_ref, grad_ref, log_ref, out_ref, *, heads, heads_block, scale):
    for head in range(heads):
        query_cols, key_cols, value_cols = head_columns(head, heads_block)
        query = rows_ref[:, query_cols]
        key = rows_ref[:, key_cols]
        grad = grad_ref[:, head * HEAD_DIM : (head + 1) * HEAD_DIM]
        scores = times_transposed(key, query) * (scale * log2_e)
        weights = jnp.exp2(scores - log_ref[0, head : head + 1, :])
        grad_weights = times_transposed(rows_ref[:, value_cols], grad)
        inner = jnp.sum(weights * grad_weights, axis=0, keepdims=True)
        grad_scores = (weights * (grad_weights - inner)).astype(jnp.bfloat16)
        out_ref[:, value_cols] = project(weights.astype(jnp.bfloat16), grad).astype(jnp.bfloat16)
        out_ref[:, key_cols] = (project(grad_scores, query) * scale).astype(jnp.bfloat16)
        out_ref[:, query_cols] = (transposed_times(grad_scores, key) * scale).astype(jnp.bfloat16)


def self_backward(mixed_rows, grad_attended, logs, heads, heads_block, scale):
    row_count, width = mixed_rows.shape
    groups = row_count // GROUP
    return pl.pallas_call(
        functools.partial(
            self_backward_kernel, heads=heads, heads_block=heads_block, scale=scale
        ),
        grid=(groups,),
        in_specs=[
            pl.BlockSpec((GROUP, width), lambda i: (i, 0)),
            pl.BlockSpec((GROUP, heads * HEAD_DIM), lambda i: (i, 0)),
            pl.BlockSpec((1, heads, GROUP), lambda i: (i, 0, 0)),
        ],
        out_specs=pl.BlockSpec((GROUP, width), lambda i: (i, 0)),
        out_shape=jax.ShapeDtypeStruct((row_count, width), jnp.bfloat16),
        cost_estimate=pl.CostEstimate(
            flops=20 * row_count * GROUP * heads * HEAD_DIM,
            transcendentals=row_count * GROUP * heads,
            bytes_accessed=5 * mixed_rows.size,
        ),
        name="self_backward",
    )(mixed_rows, grad_attended, logs)


def feed_kernel(rows_ref, grad_ref, up_ref, down_ref, *rest):
    active_ref, grad_hidden_ref = rest[-2:]
    hidden = project(rows_ref[...], up_ref[...])
    grad_active = times_transposed(grad_ref[...], down_ref[...])
    square = hidden * hidden
    bend = jnp.tanh(gelu_factor * hidden * (1.0 + gelu_cubic * square))
    half_sum = 0.5 * (1.0 + bend)
    slope = half_sum + (0.5 * gelu_factor) * hidden * (1.0 - bend * bend) * (
        1.0 + (3.0 * gelu_cubic) * square
    )
    active_ref[...] = (hidden * half_sum).astype(jnp.bfloat16)
    grad_hidden_ref[...] = (slope * grad_active).astype(jnp.bfloat16)


def feed_block(step, total, rows, grads, up, down, earlier):
    row_count, width = rows.shape
    hidden_width = up.shape[1]
    tile = math.gcd(hidden_width, 256)
    result = jax.ShapeDtypeStruct((total * row_count, hidden_width), jnp.bfloat16)
    block = pl.BlockSpec((row_count, tile), lambda i: (step, i))
    whole = pl.BlockSpec((row_count, width), lambda i: (0, 0))
    return pl.pallas_call(
        feed_kernel,
        grid=(hidden_width // tile,),
        in_specs=[
            whole,
            whole,
            pl.BlockSpec((width, tile), lambda i: (0, i)),
            pl.BlockSpec((tile, width), lambda i: (i, 0)),
        ]
        + [pl.BlockSpec(memory_space=pl.ANY)] * len(earlier),
        out_specs=[block, block],
        out_shape=[result, result],
        input_output_aliases={4: 0, 5: 1} if earlier else {},
        compiler_params=pltpu.CompilerParams(vmem_limit_bytes=vmem_bytes),
        cost_estimate=pl.CostEstimate(
            flops=4 * row_count * width * hidden_width,
            transcendentals=row_count * hidden_width,
            bytes_accessed=4 * (width * hidden_width + row_count * (width + hidden_width)),
        ),
        name="feed_hidden",
    )(rows, grads, up, down, *earlier)


def local(
    latents,
    inputs,
    neighbours,
    key_counts,
    filled,
    cotangent,
    cross_gain,
    cross_query,
    cross_key,
    cross_value,
    cross_output,
    self_gain,
    self_query,
    self_key,
    self_value,
    self_output,
    feed_gain,
    feed_up,
    feed_down,
):
    tp_count = lax.axis_size("tp")
    tp_index = lax.axis_index("tp")
    bits = all_bits()
    rows_dev = latents.shape[0]
    table_dev = inputs.shape[0]
    table_rows = table_dev * tp_count
    group_count = neighbours.shape[0]
    local_groups = rows_dev // GROUP
    scale = 1.0 / math.sqrt(HEAD_DIM)
    first_group = tp_index * local_groups
    group_alive = (first_group + jnp.arange(local_groups, dtype=jnp.int32) < filled[0]).astype(
        jnp.float32
    )
    alive_rows = jnp.repeat(group_alive, GROUP)[:, None]

    chosen = jnp.roll(neighbours, -first_group, axis=0)
    counts = jnp.roll(key_counts, -first_group, axis=0)
    chosen = (chosen - tp_index * table_dev) % table_rows
    log_counts = log_multiplicity(chosen, counts, table_rows)

    def block_rows(array, step):
        return array[step * rows_dev : (step + 1) * rows_dev]

    state_rows = latents.astype(jnp.float32)
    unit_cross, inverse_cross, normed_cross = norm_forward(state_rows, cross_gain)
    embedded = jnp.concatenate(gather_blocks(inputs), axis=0)
    rows_cross = jnp.concatenate(gather_blocks(normed_cross), axis=0)
    key_table = project(embedded, cross_key).astype(jnp.bfloat16)
    value_table = project(embedded, cross_value).astype(jnp.bfloat16)
    key_table_t = key_table.T
    value_table_t = value_table.T
    queries_cross = project(rows_cross, cross_query).astype(jnp.bfloat16)
    attended_cross, logs_cross = cross_forward(
        log_counts, queries_cross, key_table, value_table_t, scale
    )
    after_cross = state_rows + alive_rows * sum_blocks(
        lambda step: project(block_rows(attended_cross, step), cross_output)
    )

    own_mixed = jnp.concatenate([self_query, self_key, self_value], axis=1)
    heads_block = self_query.shape[1] // HEAD_DIM
    heads = heads_block * tp_count

    def fetch(weight):
        kept, _ = halves(weight, 0)
        parts = [weight]
        for step in range(1, tp_count):
            part = from_peer(kept, step)
            parts.append(spread_sets(part, [0]))
        return parts

    mixed_weight = jnp.concatenate(fetch(own_mixed), axis=1)
    output_weight = jnp.concatenate(fetch(self_output), axis=0)

    unit_self, inverse_self, normed_self = norm_forward(after_cross, self_gain)
    mixed_rows = project(normed_self, mixed_weight).astype(jnp.bfloat16)
    attended_self, logs_self = self_forward(mixed_rows, heads, heads_block, scale)
    after_self = after_cross + alive_rows * project(attended_self, output_weight)

    grad_final = cotangent.astype(jnp.float32)
    grad_blocks = gather_blocks((alive_rows * grad_final).astype(jnp.bfloat16))
    unit_feed, inverse_feed, normed_feed = norm_forward(after_self, feed_gain)
    feed_blocks = gather_blocks(normed_feed)
    filled_parts = ()
    for step in range(tp_count):
        filled_parts = feed_block(
            step, tp_count, feed_blocks[step], grad_blocks[step], feed_up, feed_down, filled_parts
        )
    activated, grad_hidden = filled_parts
    grad_normed_feed = sum_blocks(
        lambda step: times_transposed(block_rows(grad_hidden, step), feed_up)
    )
    final_rows = after_self + alive_rows * sum_blocks(
        lambda step: project(block_rows(activated, step), feed_down)
    )
    grad_feed_up = transposed_times(jnp.concatenate(feed_blocks, axis=0), grad_hidden)
    grad_feed_down = transposed_times(activated, jnp.concatenate(grad_blocks, axis=0))
    grad_feed_up = sum_sets(grad_feed_up, bits)
    grad_feed_down = sum_sets(grad_feed_down, bits)
    group_rms = jnp.sqrt(jnp.mean((final_rows * final_rows).reshape(local_groups, -1), axis=1))
    penalty_term = jnp.sum(group_rms * group_alive)
    grad_rows, grad_feed_gain = norm_backward(grad_normed_feed, unit_feed, inverse_feed, feed_gain)
    grad_after_self = grad_final + grad_rows

    grad_branch = (alive_rows * grad_after_self).astype(jnp.bfloat16)
    grad_output_full = transposed_times(attended_self, grad_branch).astype(jnp.bfloat16)
    grad_attended = times_transposed(grad_branch, output_weight).astype(jnp.bfloat16)
    grad_mixed = self_backward(mixed_rows, grad_attended, logs_self, heads, heads_block, scale)
    grad_normed_self = times_transposed(grad_mixed, mixed_weight)
    grad_mixed_full = transposed_times(normed_self, grad_mixed).astype(jnp.bfloat16)
    grad_rows, grad_self_gain = norm_backward(grad_normed_self, unit_self, inverse_self, self_gain)
    grad_after_cross = grad_after_self + grad_rows

    def own_share(parts):
        shares = [scatter_sets(part, bits[:1]) for part in parts]
        total = shares[0].astype(jnp.float32)
        for step in range(1, tp_count):
            total = total + to_peer(shares[step], step).astype(jnp.float32)
        part = scatter_sets(total.astype(jnp.bfloat16), bits[1:])
        return spread_sets(part, bits).astype(jnp.float32)

    grad_self_mixed = own_share(jnp.split(grad_mixed_full, tp_count, axis=1))
    grad_self_output = own_share(jnp.split(grad_output_full, tp_count, axis=0))
    grad_self_query, grad_self_key, grad_self_value = jnp.split(grad_self_mixed, 3, axis=1)

    grad_branch = jnp.concatenate(
        gather_blocks((alive_rows * grad_after_cross).astype(jnp.bfloat16)), axis=0
    )
    grad_cross_output = sum_sets(transposed_times(attended_cross, grad_branch), bits)
    grad_attended = times_transposed(grad_branch, cross_output).astype(jnp.bfloat16)
    grad_queries, grad_key_table, grad_value_table = cross_backward(
        log_counts,
        queries_cross,
        grad_attended,
        logs_cross,
        key_table,
        key_table_t,
        value_table,
        scale,
    )
    grad_cross_mixed = jnp.concatenate(
        [
            transposed_times(rows_cross, grad_queries).astype(jnp.bfloat16),
            transposed_times(embedded, grad_key_table).astype(jnp.bfloat16),
            transposed_times(embedded, grad_value_table).astype(jnp.bfloat16),
        ],
        axis=1,
    )
    grad_cross_mixed = sum_sets(grad_cross_mixed, bits)
    grad_cross_query, grad_cross_key, grad_cross_value = jnp.split(grad_cross_mixed, 3, axis=1)
    input_grad = sum_blocks(
        lambda step: times_transposed(
            grad_key_table[step * table_dev : (step + 1) * table_dev], cross_key
        )
        + times_transposed(
            grad_value_table[step * table_dev : (step + 1) * table_dev], cross_value
        )
    )
    grad_normed_cross = sum_blocks(
        lambda step: times_transposed(block_rows(grad_queries, step), cross_query)
    )
    grad_rows, grad_cross_gain = norm_backward(
        grad_normed_cross, unit_cross, inverse_cross, cross_gain
    )
    latent_grad = grad_after_cross + grad_rows

    early = jnp.stack(
        [grad_feed_gain, grad_self_gain, jnp.full_like(grad_feed_gain, penalty_term)], axis=0
    )
    early = sum_everywhere(early)
    grad_cross_gain = sum_everywhere(grad_cross_gain[None])[0]
    penalty = early[2, 0] / (group_count * lax.axis_size("sets"))
    return (
        final_rows.astype(jnp.bfloat16),
        latent_grad,
        input_grad,
        grad_cross_gain,
        grad_cross_query,
        grad_cross_key,
        grad_cross_value,
        grad_cross_output,
        early[1],
        grad_self_query,
        grad_self_key,
        grad_self_value,
        grad_self_output,
        early[0],
        grad_feed_up,
        grad_feed_down,
        penalty,
    )


def solution(mesh):
    return jax.shard_map(
        local,
        mesh=mesh,
        in_specs=(
            P(("sets", "tp"), None),
            P(("sets", "tp"), None),
            P("sets", None),
            P("sets"),
            P("sets"),
            P(("sets", "tp"), None),
            P(),
            P(None, "tp"),
            P(None, "tp"),
            P(None, "tp"),
            P("tp", None),
            P(),
            P(None, "tp"),
            P(None, "tp"),
            P(None, "tp"),
            P("tp", None),
            P(),
            P(None, "tp"),
            P("tp", None),
        ),
        out_specs=(
            P(("sets", "tp"), None),
            P(("sets", "tp"), None),
            P(("sets", "tp"), None),
            P(),
            P(None, "tp"),
            P(None, "tp"),
            P(None, "tp"),
            P("tp", None),
            P(),
            P(None, "tp"),
            P(None, "tp"),
            P(None, "tp"),
            P("tp", None),
            P(),
            P(None, "tp"),
            P("tp", None),
            P(),
        ),
        check_vma=False,
    )
```

time: 1280 us -> 728 us (0.57)
  waiting for transfers between devices: 655 us -> 342 us
  local copies, waits for them, and re-layouts: 230 us -> 59.1 us
  Pallas kernels: 0 us -> 84.5 us
  matrix products: 183 us -> 101 us
  other arithmetic: 145 us -> 64.6 us
  starting transfers between devices: 1.83 us -> 62.5 us
  blocking collectives: 40 us -> 0 us
    ppermute x0 -> x76, waiting for transfers between devices: none -> 342 us  [the longest x60 247 us: swap_sets(): lax.ppermute(block, 'sets', [(source, source ^ 1 << bit) for source in ra...]
    psum x1 -> x0, waiting for transfers between devices: 287 us -> none  [local(): lax.psum(grad_cross_key.astype(jnp.bfloat16), 'sets').astype(jnp.float32)]
    all_gather x7 -> x0, waiting for transfers between devices: 217 us -> none  [the longest x3 95.8 us: spread_grads(): return lax.all_gather(rows_local, 'tp', axis=0, tiled=True)]
    reduce_scatter x7 -> x0, waiting for transfers between devices: 150 us -> none  [the longest x3 97.1 us: collect_branch(): lax.psum_scatter(row_terms(((left_rows, weight),), False).astype(jnp.bflo...]
    pallas_call x0 -> x7, Pallas kernels: none -> 84.5 us  [the longest x2 23.7 us: feed_block(): pl.pallas_call(feed_kernel, grid=(hidden_width // tile,), in_specs=[whole...]
    gather x8 -> x0, local copies, waits for them, and re-layouts: 73.6 us -> none  [pick_rows(): picked = jnp.take(table, chosen.reshape(-1), axis=0)]
    scatter-add x4 -> x0, other arithmetic: 68.6 us -> none  [the longest x2 34.3 us: one_block(): grad_keys.at[flat_index].add(grad_key_rows.reshape(-1, row_width))]
    ppermute x0 -> x76, starting transfers between devices: none -> 62.5 us  [the longest x60 39.9 us: swap_sets(): lax.ppermute(block, 'sets', [(source, source ^ 1 << bit) for source in ra...]
  transfers between devices with their start and end apart: 15 -> 76, of which waited for: 13 -> 39; matrix products, arithmetic and copies ran while one was open for 7% -> 27% of each run, Pallas kernels for 0% -> 10%
where the time goes in v1:
time: 728 us; the launch traced here: 718 us
  waiting for transfers between devices  342 us (47%)
  matrix products  101 us (14%)
  Pallas kernels  84.5 us (12%)
  other arithmetic  64.6 us (9%)
  starting transfers between devices  62.5 us (9%)
  local copies, waits for them, and re-layouts  59.1 us (8%)
    ppermute x60, waiting for transfers between devices, swap_sets(): lax.ppermute(block, 'sets', [(source, source ^ 1 << bit) for source in ra...  247 us
    ppermute x7, waiting for transfers between devices, from_peer(): lax.ppermute(block, 'tp', [(source, (source - step) % count) for source i...  50.2 us
    dot_general x9, matrix products, project(): return jnp.dot(left_rows, right_rows, preferred_element_type=jnp.float32)  47.2 us
    ppermute x60, starting transfers between devices, swap_sets(): lax.ppermute(block, 'sets', [(source, source ^ 1 << bit) for source in ra...  39.9 us
    ppermute x7, waiting for transfers between devices, to_peer(): lax.ppermute(block, 'tp', [(source, (source + step) % count) for source i...  36.8 us
    unnamed x148, local copies, waits for them, and re-layouts  34.4 us
    dot_general x11, matrix products, times_transposed(): lax.dot_general(left_rows, right_rows, (((1,), (1,)), ((), ())), preferre...  26.7 us
    dot_general x8, matrix products, transposed_times(): lax.dot_general(left_rows, right_rows, (((0,), (0,)), ((), ())), preferre...  26.6 us
  transfers between devices with their start and end apart: 76, of which 39 were waited for; matrix products, arithmetic and copies ran while one was open for 27% of the time, Pallas kernels for 10%

profile of v1, /device:TPU:0, one launch (start us, length us, event | category | flops | bytes accessed | tf_op | source)
XLA Modules:
  0.0 718.2 jit_solution(13703649015873855787)
XLA Ops:
  22.0 6.6 multiplicity.1.counts_ref
  40.3 10.2 %collective-permute-done = bf16[512,1024]{1,0:T(8,128)(2,1)} collective-permute-done((bf16[512,1024]{1,0:T(8,128)(2,1)}, bf16[512,1024]{1,0:T(8,128)(2,1)}, u32[]{:S(2)}, u32[]{:S(2)}) %collective-permute-start) | collective-permute-done | bytes 1048608 | tf_op jit(solution)/shard_map/ppermute | solution.py:57
  50.5 3.8 convolution_convert_fusion.13.query_ref
  54.3 14.3 %cross_forward.1 = (bf16[1024,512]{1,0:T(8,128)(2,1)}, f32[4,4,256]{2,1,0:T(4,128)}) custom-call(f32[1024,128]{1,0:T(8,128)} %multiplicity.1.counts_ref, bf16[1024,512]{1,0:T(8,128)(2,1)} %convolution_convert_fusion.13.query_ref, bf16[1024,512]{1,0:T(8,128)(2,1)} %copy.56.key_ref, bf16[512,1024]{1,0:T(8,128)(2,1)} %copy.57.value_t_ref), custom_call_target="tpu_custom_call" | custom-call | flops 4294967296 | bytes 4194304 | tf_op jit(solution)/shard_map/cross_forward/pallas_call | solution.py:208
  68.5 3.2 convolution_convert_fusion.15
  74.4 21.0 %collective-permute-done.5 = bf16[256,1024]{1,0:T(8,128)(2,1)} collective-permute-done((bf16[256,1024]{1,0:T(8,128)(2,1)}, bf16[256,1024]{1,0:T(8,128)(2,1)}, u32[]{:S(2)}, u32[]{:S(2)}) %collective-permute-start.5) | collective-permute-done | bytes 524320 | tf_op jit(solution)/shard_map/ppermute | solution.py:57
  101.7 16.2 %collective-permute-done.2 = bf16[512,1024]{1,0:T(8,128)(2,1)} collective-permute-done((bf16[512,1024]{1,0:T(8,128)(2,1)}, bf16[512,1024]{1,0:T(8,128)(2,1)}, u32[]{:S(2)}, u32[]{:S(2)}) %collective-permute-start.2) | collective-permute-done | bytes 1048608 | tf_op jit(solution)/shard_map/ppermute | solution.py:62
  124.6 18.7 %convolution_convert_fusion.1.rows_ref = bf16[512,3072]{1,0:T(8,128)(2,1)} fusion(bf16[512,1536]{0,1:T(8,128)(2,1)S(1)} %get-tuple-element.101, bf16[512,1536]{0,1:T(8,128)(2,1)S(1)} %get-tuple-element.100, bf16[1024,512]{0,1:T(8,128)(2,1)S(1)} %copy-done.27, bf16[1024,512]{0,1:T(8,128)(2,1)S(1)} %copy-done.26, bf16[1024,512]{0,1:T(8,128)(2,1)S(1)} %copy.61, ...), kind=kOutput, calls=%fused_computation.2 | convolution fusion | flops 3256352768 | bytes 11542528 | tf_op jit(solution)/shard_map/dot_general | solution.py:23
  143.4 11.1 %self_forward.1 = (bf16[512,1024]{1,0:T(8,128)(2,1)}, f32[4,8,128]{2,1,0:T(8,128)}) custom-call(bf16[512,3072]{1,0:T(8,128)(2,1)} %convolution_convert_fusion.1.rows_ref), custom_call_target="tpu_custom_call" | custom-call | flops 536870912 | bytes 4718592 | tf_op jit(solution)/shard_map/self_forward/pallas_call | solution.py:351
  154.5 3.2 fusion.77
  161.7 12.0 %feed_hidden.2 = (bf16[1024,2048]{1,0:T(8,128)(2,1)}, bf16[1024,2048]{1,0:T(8,128)(2,1)}) custom-call(bf16[512,1024]{1,0:T(8,128)(2,1)} %multiply_convert_fusion.2.rows_ref, bf16[512,1024]{1,0:T(8,128)(2,1)} %fusion.13.grad_ref, bf16[1024,2048]{1,0:T(8,128)(2,1)} %up_ref.3, bf16[2048,1024]{1,0:T(8,128)(2,1)} %down_ref.3), custom_call_target="tpu_custom_call" | custom-call | flops 4294967296 | bytes 14680064 | tf_op jit(solution)/shard_map/feed_hidden/pallas_call | solution.py:435
  173.8 9.7 %collective-permute-done.7.rows_ref = bf16[512,1024]{1,0:T(8,128)(2,1)} collective-permute-done((bf16[512,1024]{1,0:T(8,128)(2,1)}, bf16[512,1024]{1,0:T(8,128)(2,1)}, u32[]{:S(2)}, u32[]{:S(2)}) %collective-permute-start.7) | collective-permute-done | bytes 1048608 | tf_op jit(solution)/shard_map/ppermute | solution.py:57
  183.5 11.6 %feed_hidden.3 = (bf16[1024,2048]{1,0:T(8,128)(2,1)}, bf16[1024,2048]{1,0:T(8,128)(2,1)}) custom-call(bf16[512,1024]{1,0:T(8,128)(2,1)} %collective-permute-done.7.rows_ref, bf16[512,1024]{1,0:T(8,128)(2,1)} %collective-permute-done.8.grad_ref, bf16[1024,2048]{1,0:T(8,128)(2,1)} %up_ref.3, ...), custom_call_target="tpu_custom_call", output_to_operand_aliasing={{0}: (4, {}), {1}: (5, {})} | custom-call | flops 4294967296 | bytes 14680064 | tf_op jit(solution)/shard_map/feed_hidden/pallas_call | solution.py:435
  195.2 6.3 fusion.32
  206.0 6.4 convolution_convert_fusion.3
  216.8 6.6 convolution_convert_fusion.2
  226.2 20.5 %collective-permute-done.10 = bf16[512,1024]{1,0:T(8,128)(2,1)S(1)} collective-permute-done((bf16[512,1024]{1,0:T(8,128)(2,1)S(1)}, bf16[512,1024]{1,0:T(8,128)(2,1)S(1)}, u32[]{:S(2)}, u32[]{:S(2)}) %collective-permute-start.10) | collective-permute-done | bytes 1048608 | tf_op jit(solution)/shard_map/ppermute | solution.py:62
  253.6 10.3 %self_backward.1 = bf16[512,3072]{1,0:T(8,128)(2,1)} custom-call(bf16[512,3072]{1,0:T(8,128)(2,1)} %convolution_convert_fusion.1.rows_ref, bf16[512,1024]{1,0:T(8,128)(2,1)} %convolution_convert_fusion.10.grad_ref, f32[4,8,128]{2,1,0:T(8,128)} %get-tuple-element.34.log_ref), custom_call_target="tpu_custom_call" | custom-call | flops 1342177280 | bytes 7864320 | tf_op jit(solution)/shard_map/self_backward/pallas_call | solution.py:393
  263.9 9.0 %multiply_reduce_fusion.1 = (f32[1024]{0:T(1024)S(1)}, f32[512]{0:T(512)S(1)}, f32[512]{0:T(512)S(1)}, f32[512,1024]{1,0:T(8,128)}) fusion(f32[512,1024]{1,0:T(8,128)S(1)} %copy-done.4, f32[512]{0:T(512)S(1)} %add_rsqrt_fusion.1, f32[512]{0:T(512)S(1)} %broadcast_multiply_fusion.7, f32[1024]{0:T(1024)S(1)} %copy-done.63, ...), kind=kOutput, calls=%fused_computation.52 | convolution fusion | flops 3256875008 | bytes 13647872 | tf_op jit(solution)/shard_map/dot_general | solution.py:27
  275.6 4.2 convolution_convert_fusion
  279.9 5.4 multiply_reduce_fusion
  303.3 8.2 %collective-permute-done.39 = f32[3,1024]{1,0:T(4,128)S(1)} collective-permute-done((f32[3,1024]{1,0:T(4,128)S(1)}, f32[3,1024]{1,0:T(4,128)S(1)}, u32[]{:S(2)}, u32[]{:S(2)}) %collective-permute-start.39) | collective-permute-done | bytes 12320 | tf_op jit(solution)/shard_map/ppermute | solution.py:132
  325.1 9.3 %collective-permute-done.11 = bf16[512,1024]{1,0:T(8,128)(2,1)S(1)} collective-permute-done((bf16[512,1024]{1,0:T(8,128)(2,1)S(1)}, bf16[512,1024]{1,0:T(8,128)(2,1)S(1)}, u32[]{:S(2)}, u32[]{:S(2)}) %collective-permute-start.11) | collective-permute-done | bytes 1048608 | tf_op jit(solution)/shard_map/ppermute | solution.py:57
  336.6 18.6 %cross_backward.1 = (bf16[1024,512]{1,0:T(8,128)(2,1)}, bf16[1024,512]{1,0:T(8,128)(2,1)}, bf16[1024,512]{1,0:T(8,128)(2,1)}) custom-call(f32[1024,128]{1,0:T(8,128)} %multiplicity.1.counts_ref, bf16[1024,512]{1,0:T(8,128)(2,1)} %convolution_convert_fusion.13.query_ref, bf16[1024,512]{1,0:T(8,128)(2,1)} %convolution_convert_fusion.9.grad_ref, ...), custom_call_target="tpu_custom_call" | custom-call | flops 10737418240 | bytes 8388608 | tf_op jit(solution)/shard_map/cross_backward/pallas_call | solution.py:295
  370.7 5.1 collective-permute-done.54
  376.2 5.4 collective-permute-done.55
  390.8 21.0 %collective-permute-done.28 = bf16[128,1024]{1,0:T(8,128)(2,1)S(1)} collective-permute-done((bf16[128,1024]{1,0:T(8,128)(2,1)S(1)}, bf16[128,1024]{1,0:T(8,128)(2,1)S(1)}, u32[]{:S(2)}, u32[]{:S(2)}) %collective-permute-start.28) | collective-permute-done | bytes 262176 | tf_op jit(solution)/shard_map/ppermute | solution.py:82
  411.9 4.9 collective-permute-done.57
  416.8 4.9 collective-permute-done.29
  423.2 4.8 collective-permute-done.58
  428.2 5.1 collective-permute-done.30
  466.9 10.7 %collective-permute-done.62 = bf16[128,2048]{1,0:T(8,128)(2,1)S(1)} collective-permute-done((bf16[128,2048]{1,0:T(8,128)(2,1)S(1)}, bf16[128,2048]{1,0:T(8,128)(2,1)S(1)}, u32[]{:S(2)}, u32[]{:S(2)}) %collective-permute-start.62) | collective-permute-done | bytes 524320 | tf_op jit(solution)/shard_map/ppermute | solution.py:82
  477.8 9.4 %collective-permute-done.70 = bf16[256,1024]{1,0:T(8,128)(2,1)S(1)} collective-permute-done((bf16[256,1024]{1,0:T(8,128)(2,1)S(1)}, bf16[256,1024]{1,0:T(8,128)(2,1)S(1)}, u32[]{:S(2)}, u32[]{:S(2)}) %collective-permute-start.70) | collective-permute-done | bytes 524320 | tf_op jit(solution)/shard_map/ppermute | solution.py:82
  491.2 15.0 %collective-permute-done.63 = bf16[64,2048]{1,0:T(8,128)(2,1)S(1)} collective-permute-done((bf16[64,2048]{1,0:T(8,128)(2,1)S(1)}, bf16[64,2048]{1,0:T(8,128)(2,1)S(1)}, u32[]{:S(2)}, u32[]{:S(2)}) %collective-permute-start.63) | collective-permute-done | bytes 262176 | tf_op jit(solution)/shard_map/ppermute | solution.py:82
  507.7 4.0 collective-permute-done.71
  521.5 9.1 %collective-permute-done.64 = bf16[64,2048]{1,0:T(8,128)(2,1)S(1)} collective-permute-done((bf16[64,2048]{1,0:T(8,128)(2,1)S(1)}, bf16[64,2048]{1,0:T(8,128)(2,1)S(1)}, u32[]{:S(2)}, u32[]{:S(2)}) %collective-permute-start.64) | collective-permute-done | bytes 262176 | tf_op jit(solution)/shard_map/ppermute | solution.py:82
  530.7 5.5 collective-permute-done.72
  538.8 8.7 %collective-permute-done.65 = bf16[128,2048]{1,0:T(8,128)(2,1)S(1)} collective-permute-done((bf16[128,2048]{1,0:T(8,128)(2,1)S(1)}, bf16[128,2048]{1,0:T(8,128)(2,1)S(1)}, u32[]{:S(2)}, u32[]{:S(2)}) %collective-permute-start.65) | collective-permute-done | bytes 524320 | tf_op jit(solution)/shard_map/ppermute | solution.py:82
  548.3 10.4 %collective-permute-done.73 = bf16[256,1024]{1,0:T(8,128)(2,1)S(1)} collective-permute-done((bf16[256,1024]{1,0:T(8,128)(2,1)S(1)}, bf16[256,1024]{1,0:T(8,128)(2,1)S(1)}, u32[]{:S(2)}, u32[]{:S(2)}) %collective-permute-start.73) | collective-permute-done | bytes 524320 | tf_op jit(solution)/shard_map/ppermute | solution.py:82
  559.5 7.5 %collective-permute-done.21 = bf16[128,1536]{0,1:T(8,128)(2,1)S(1)} collective-permute-done((bf16[128,1536]{0,1:T(8,128)(2,1)S(1)}, bf16[128,1536]{0,1:T(8,128)(2,1)S(1)}, u32[]{:S(2)}, u32[]{:S(2)}) %collective-permute-start.21) | collective-permute-done | bytes 393248 | tf_op jit(solution)/shard_map/ppermute | solution.py:82
  568.5 19.4 %collective-permute-done.22 = bf16[64,1536]{0,1:T(8,128)(2,1)S(1)} collective-permute-done((bf16[64,1536]{0,1:T(8,128)(2,1)S(1)}, bf16[64,1536]{0,1:T(8,128)(2,1)S(1)}, u32[]{:S(2)}, u32[]{:S(2)}) %collective-permute-start.22) | collective-permute-done | bytes 196640 | tf_op jit(solution)/shard_map/ppermute | solution.py:82
  590.5 17.2 %collective-permute-done.23 = bf16[64,1536]{0,1:T(8,128)(2,1)S(1)} collective-permute-done((bf16[64,1536]{0,1:T(8,128)(2,1)S(1)}, bf16[64,1536]{0,1:T(8,128)(2,1)S(1)}, u32[]{:S(2)}, u32[]{:S(2)}) %collective-permute-start.23) | collective-permute-done | bytes 196640 | tf_op jit(solution)/shard_map/ppermute | solution.py:82
  611.3 16.7 %collective-permute-done.45 = bf16[64,1536]{0,1:T(8,128)(2,1)S(1)} collective-permute-done((bf16[64,1536]{0,1:T(8,128)(2,1)S(1)}, bf16[64,1536]{0,1:T(8,128)(2,1)S(1)}, u32[]{:S(2)}, u32[]{:S(2)}) %collective-permute-start.45) | collective-permute-done | bytes 196640 | tf_op jit(solution)/shard_map/ppermute | solution.py:82
  630.3 17.2 %collective-permute-done.46 = bf16[64,1536]{0,1:T(8,128)(2,1)S(1)} collective-permute-done((bf16[64,1536]{0,1:T(8,128)(2,1)S(1)}, bf16[64,1536]{0,1:T(8,128)(2,1)S(1)}, u32[]{:S(2)}, u32[]{:S(2)}) %collective-permute-start.46) | collective-permute-done | bytes 196640 | tf_op jit(solution)/shard_map/ppermute | solution.py:82
  648.8 10.2 %collective-permute-done.47 = bf16[128,1536]{0,1:T(8,128)(2,1)S(1)} collective-permute-done((bf16[128,1536]{0,1:T(8,128)(2,1)S(1)}, bf16[128,1536]{0,1:T(8,128)(2,1)S(1)}, u32[]{:S(2)}, u32[]{:S(2)}) %collective-permute-start.47) | collective-permute-done | bytes 393248 | tf_op jit(solution)/shard_map/ppermute | solution.py:82
  660.5 17.6 %collective-permute-done.48 = bf16[256,1536]{0,1:T(8,128)(2,1)S(1)} collective-permute-done((bf16[256,1536]{0,1:T(8,128)(2,1)S(1)}, bf16[256,1536]{0,1:T(8,128)(2,1)S(1)}, u32[]{:S(2)}, u32[]{:S(2)}) %collective-permute-start.48) | collective-permute-done | bytes 786464 | tf_op jit(solution)/shard_map/ppermute | solution.py:82
  682.5 4.3 maximum_convert_fusion
  686.8 4.5 maximum_convert_fusion.1
  (441 shorter events, 228.2 us)
Async XLA Ops:
  0.7 29.3 %collective-permute-start.1 = (bf16[512,1024]{1,0:T(8,128)(2,1)}, bf16[512,1024]{1,0:T(8,128)(2,1)}, u32[]{:S(2)}, u32[]{:S(2)}) collective-permute-start(bf16[512,1024]{1,0:T(8,128)(2,1)} %param.20), channel_id=1, source_target_pairs={{0,1},{1,0},{2,3},{3,2},{4,5},{5,4},{6,7},{7,6},{8,9},{9,8},{10,11... | collective-permute-start | bytes 3145736 | tf_op jit(solution)/shard_map/ppermute | solution.py:57
  8.2 42.3 %collective-permute-start = (bf16[512,1024]{1,0:T(8,128)(2,1)}, bf16[512,1024]{1,0:T(8,128)(2,1)}, u32[]{:S(2)}, u32[]{:S(2)}) collective-permute-start(bf16[512,1024]{1,0:T(8,128)(2,1)} %fusion.6), channel_id=1, source_target_pairs={{0,1},{1,0},{2,3},{3,2},{4,5},{5,4},{6,7},{7,6},{8,9},{9,8},{10,11... | collective-permute-start | bytes 3145736 | tf_op jit(solution)/shard_map/ppermute | solution.py:57
  17.3 78.2 %collective-permute-start.3 = (bf16[512,1536]{0,1:T(8,128)(2,1)}, bf16[512,1536]{0,1:T(8,128)(2,1)}, u32[]{:S(2)}, u32[]{:S(2)}) collective-permute-start(bf16[512,1536]{0,1:T(8,128)(2,1)} %fusion.29), channel_id=1, source_target_pairs={{0,1},{1,0},{2,3},{3,2},{4,5},{5,4},{6,7},{7,6},{8,9},{9,8},{10,11... | collective-permute-start | bytes 4718600 | tf_op jit(solution)/shard_map/ppermute | solution.py:57
  21.0 74.4 %collective-permute-start.5 = (bf16[256,1024]{1,0:T(8,128)(2,1)}, bf16[256,1024]{1,0:T(8,128)(2,1)}, u32[]{:S(2)}, u32[]{:S(2)}) collective-permute-start(bf16[256,1024]{1,0:T(8,128)(2,1)} %constant_dynamic-slice_fusion.26), channel_id=1, source_target_pairs={{0,1},{1,0},{2,3},{3,2},{4,5},{5,4},{6,7},{7,6},{8,9},{9,8},{10,11... | collective-permute-start | bytes 1572872 | tf_op jit(solution)/shard_map/ppermute | solution.py:57
  71.7 46.2 %collective-permute-start.2 = (bf16[512,1024]{1,0:T(8,128)(2,1)}, bf16[512,1024]{1,0:T(8,128)(2,1)}, u32[]{:S(2)}, u32[]{:S(2)}) collective-permute-start(bf16[512,1024]{1,0:T(8,128)(2,1)} %convolution_convert_fusion.15), channel_id=1, source_target_pairs={{0,1},{1,0},{2,3},{3,2},{4,5},{5,4},{6,7},{7,6},{8,9},{9,8},{10,11... | collective-permute-start | bytes 3145736 | tf_op jit(solution)/shard_map/ppermute | solution.py:62
  95.5 25.0 %collective-permute-start.4 = (bf16[512,1536]{0,1:T(8,128)(2,1)}, bf16[512,1536]{0,1:T(8,128)(2,1)}, u32[]{:S(2)}, u32[]{:S(2)}) collective-permute-start(bf16[512,1536]{0,1:T(8,128)(2,1)} %collective-permute-done.3), channel_id=1, source_target_pairs={{0,2},{2,0},{4,6},{6,4},{8,10},{10,8},{12,14},{14,12},{16,18},{18,... | collective-permute-start | bytes 4718600 | tf_op jit(solution)/shard_map/ppermute | solution.py:82
  97.2 76.5 %collective-permute-start.8 = (bf16[512,1024]{1,0:T(8,128)(2,1)}, bf16[512,1024]{1,0:T(8,128)(2,1)}, u32[]{:S(2)}, u32[]{:S(2)}) collective-permute-start(bf16[512,1024]{1,0:T(8,128)(2,1)} %fusion.13.grad_ref), channel_id=1, source_target_pairs={{0,1},{1,0},{2,3},{3,2},{4,5},{5,4},{6,7},{7,6},{8,9},{9,8},{10,11... | collective-permute-start | bytes 3145736 | tf_op jit(solution)/shard_map/ppermute | solution.py:57
  159.7 23.8 %collective-permute-start.7 = (bf16[512,1024]{1,0:T(8,128)(2,1)}, bf16[512,1024]{1,0:T(8,128)(2,1)}, u32[]{:S(2)}, u32[]{:S(2)}) collective-permute-start(bf16[512,1024]{1,0:T(8,128)(2,1)} %multiply_convert_fusion.2.rows_ref), channel_id=1, source_target_pairs={{0,1},{1,0},{2,3},{3,2},{4,5},{5,4},{6,7},{7,6},{8,9},{9,8},{10,11... | collective-permute-start | bytes 3145736 | tf_op jit(solution)/shard_map/ppermute | solution.py:57
  201.5 78.3 %collective-permute-start.9 = (bf16[512,1024]{1,0:T(8,128)(2,1)}, bf16[512,1024]{1,0:T(8,128)(2,1)}, u32[]{:S(2)}, u32[]{:S(2)}) collective-permute-start(bf16[512,1024]{1,0:T(8,128)(2,1)} %fusion.32), channel_id=1, source_target_pairs={{0,1},{1,0},{2,3},{3,2},{4,5},{5,4},{6,7},{7,6},{8,9},{9,8},{10,11... | collective-permute-start | bytes 3145736 | tf_op jit(solution)/shard_map/ppermute | solution.py:62
  205.3 41.4 %collective-permute-start.10 = (bf16[512,1024]{1,0:T(8,128)(2,1)S(1)}, bf16[512,1024]{1,0:T(8,128)(2,1)S(1)}, u32[]{:S(2)}, u32[]{:S(2)}) collective-permute-start(bf16[512,1024]{1,0:T(8,128)(2,1)S(1)} %fusion.35), channel_id=1, source_target_pairs={{0,1},{1,0},{2,3},{3,2},{4,5},{5,4},{6,7},{7,6},{8,9},{9,8},{10,11... | collective-permute-start | bytes 3145736 | tf_op jit(solution)/shard_map/ppermute | solution.py:62
  215.6 100.1 %collective-permute-start.60 = (bf16[512,2048]{1,0:T(8,128)(2,1)}, bf16[512,2048]{1,0:T(8,128)(2,1)}, u32[]{:S(2)}, u32[]{:S(2)}) collective-permute-start(bf16[512,2048]{1,0:T(8,128)(2,1)} %constant_dynamic-slice_fusion.7), channel_id=1, source_target_pairs={{0,2},{2,0},{4,6},{6,4},{8,10},{10,8},{12,14},{14,12},{16,18},{18,... | collective-permute-start | bytes 6291464 | tf_op jit(solution)/shard_map/ppermute | solution.py:82
  226.2 94.6 %collective-permute-start.68 = (bf16[1024,1024]{1,0:T(8,128)(2,1)}, bf16[1024,1024]{1,0:T(8,128)(2,1)}, u32[]{:S(2)}, u32[]{:S(2)}) collective-permute-start(bf16[1024,1024]{1,0:T(8,128)(2,1)} %constant_dynamic-slice_fusion.3), channel_id=1, source_target_pairs={{0,2},{2,0},{4,6},{6,4},{8,10},{10,8},{12,14},{14,12},{16,18},{18,... | collective-permute-start | bytes 6291464 | tf_op jit(solution)/shard_map/ppermute | solution.py:82
  289.6 25.2 %collective-permute-start.50 = (bf16[256,1024]{1,0:T(8,128)(2,1)S(1)}, bf16[256,1024]{1,0:T(8,128)(2,1)S(1)}, u32[]{:S(2)}, u32[]{:S(2)}) collective-permute-start(bf16[256,1024]{1,0:T(8,128)(2,1)S(1)} %constant_dynamic-slice_fusion.12), channel_id=1, source_target_pairs={{0,2},{2,0},{4,6},{6,4},{8,10},{10,8},{12,14},{14,12},{16,18},{18,... | collective-permute-start | bytes 1572872 | tf_op jit(solution)/shard_map/ppermute | solution.py:82
  311.5 22.9 %collective-permute-start.11 = (bf16[512,1024]{1,0:T(8,128)(2,1)S(1)}, bf16[512,1024]{1,0:T(8,128)(2,1)S(1)}, u32[]{:S(2)}, u32[]{:S(2)}) collective-permute-start(bf16[512,1024]{1,0:T(8,128)(2,1)S(1)} %get-tuple-element.82), channel_id=1, source_target_pairs={{0,1},{1,0},{2,3},{3,2},{4,5},{5,4},{6,7},{7,6},{8,9},{9,8},{10,11... | collective-permute-start | bytes 3145736 | tf_op jit(solution)/shard_map/ppermute | solution.py:57
  314.8 70.3 %collective-permute-start.41 = (bf16[512,1536]{0,1:T(8,128)(2,1)}, bf16[512,1536]{0,1:T(8,128)(2,1)}, u32[]{:S(2)}, u32[]{:S(2)}) collective-permute-start(bf16[512,1536]{0,1:T(8,128)(2,1)} %constant_dynamic-slice_fusion.16), channel_id=1, source_target_pairs={{0,2},{2,0},{4,6},{6,4},{8,10},{10,8},{12,14},{14,12},{16,18},{18,... | collective-permute-start | bytes 4718600 | tf_op jit(solution)/shard_map/ppermute | solution.py:82
  314.8 201.8 %collective-permute-start.40 = (bf16[512,1536]{0,1:T(8,128)(2,1)}, bf16[512,1536]{0,1:T(8,128)(2,1)}, u32[]{:S(2)}, u32[]{:S(2)}) collective-permute-start(bf16[512,1536]{0,1:T(8,128)(2,1)} %constant_dynamic-slice_fusion.17), channel_id=1, source_target_pairs={{0,2},{2,0},{4,6},{6,4},{8,10},{10,8},{12,14},{14,12},{16,18},{18,... | collective-permute-start | bytes 4718600 | tf_op jit(solution)/shard_map/ppermute | solution.py:82
  315.6 53.1 %collective-permute-start.53 = (bf16[128,1024]{1,0:T(8,128)(2,1)S(1)}, bf16[128,1024]{1,0:T(8,128)(2,1)}, u32[]{:S(2)}, u32[]{:S(2)}) collective-permute-start(bf16[128,1024]{1,0:T(8,128)(2,1)S(1)} %constant_dynamic-slice_fusion.10), channel_id=1, source_target_pairs={{0,4},{2,6},{4,0},{6,2},{8,12},{10,14},{12,8},{14,10},{16,20},{18,... | collective-permute-start | bytes 786440 | tf_op jit(solution)/shard_map/ppermute | solution.py:82
  320.8 114.7 %collective-permute-start.61 = (bf16[256,2048]{1,0:T(8,128)(2,1)}, bf16[256,2048]{1,0:T(8,128)(2,1)}, u32[]{:S(2)}, u32[]{:S(2)}) collective-permute-start(bf16[256,2048]{1,0:T(8,128)(2,1)} %constant_dynamic-slice_fusion.6), channel_id=1, source_target_pairs={{0,4},{2,6},{4,0},{6,2},{8,12},{10,14},{12,8},{14,10},{16,20},{18,... | collective-permute-start | bytes 3145736 | tf_op jit(solution)/shard_map/ppermute | solution.py:82
  381.6 53.3 %collective-permute-start.69 = (bf16[512,1024]{1,0:T(8,128)(2,1)S(1)}, bf16[512,1024]{1,0:T(8,128)(2,1)S(1)}, u32[]{:S(2)}, u32[]{:S(2)}) collective-permute-start(bf16[512,1024]{1,0:T(8,128)(2,1)S(1)} %copy-done.44), channel_id=1, source_target_pairs={{0,4},{2,6},{4,0},{6,2},{8,12},{10,14},{12,8},{14,10},{16,20},{18,... | collective-permute-start | bytes 3145736 | tf_op jit(solution)/shard_map/ppermute | solution.py:82
  383.1 54.4 %collective-permute-start.12 = (bf16[512,1024]{1,0:T(8,128)(2,1)S(1)}, bf16[512,1024]{1,0:T(8,128)(2,1)S(1)}, u32[]{:S(2)}, u32[]{:S(2)}) collective-permute-start(bf16[512,1024]{1,0:T(8,128)(2,1)S(1)} %convolution_convert_fusion.14), channel_id=1, source_target_pairs={{0,1},{1,0},{2,3},{3,2},{4,5},{5,4},{6,7},{7,6},{8,9},{9,8},{10,11... | collective-permute-start | bytes 3145736 | tf_op jit(solution)/shard_map/ppermute | solution.py:62
  390.3 21.5 %collective-permute-start.28 = (bf16[128,1024]{1,0:T(8,128)(2,1)S(1)}, bf16[128,1024]{1,0:T(8,128)(2,1)S(1)}, u32[]{:S(2)}, u32[]{:S(2)}) collective-permute-start(bf16[128,1024]{1,0:T(8,128)(2,1)S(1)} %constant_dynamic-slice_fusion.20), channel_id=1, source_target_pairs={{0,4},{2,6},{4,0},{6,2},{8,12},{10,14},{12,8},{14,10},{16,20},{18,... | collective-permute-start | bytes 786440 | tf_op jit(solution)/shard_map/ppermute | solution.py:82
  433.4 20.9 %collective-permute-start.13 = (bf16[512,1024]{1,0:T(8,128)(2,1)S(1)}, bf16[512,1024]{1,0:T(8,128)(2,1)S(1)}, u32[]{:S(2)}, u32[]{:S(2)}) collective-permute-start(bf16[512,1024]{1,0:T(8,128)(2,1)S(1)} %add_convert_fusion.8), channel_id=1, source_target_pairs={{0,1},{1,0},{2,3},{3,2},{4,5},{5,4},{6,7},{7,6},{8,9},{9,8},{10,11... | collective-permute-start | bytes 3145736 | tf_op jit(solution)/shard_map/ppermute | solution.py:62
  435.0 53.6 %collective-permute-start.19 = (bf16[512,1536]{0,1:T(8,128)(2,1)S(1)}, bf16[512,1536]{0,1:T(8,128)(2,1)S(1)}, u32[]{:S(2)}, u32[]{:S(2)}) collective-permute-start(bf16[512,1536]{0,1:T(8,128)(2,1)S(1)} %constant_dynamic-slice_fusion.25), channel_id=1, source_target_pairs={{0,2},{2,0},{4,6},{6,4},{8,10},{10,8},{12,14},{14,12},{16,18},{18,... | collective-permute-start | bytes 4718600 | tf_op jit(solution)/shard_map/ppermute | solution.py:82
  457.8 58.7 %collective-permute-start.42 = (bf16[512,1536]{0,1:T(8,128)(2,1)S(1)}, bf16[512,1536]{0,1:T(8,128)(2,1)S(1)}, u32[]{:S(2)}, u32[]{:S(2)}) collective-permute-start(bf16[512,1536]{0,1:T(8,128)(2,1)S(1)} %add_convert_fusion.3), channel_id=1, source_target_pairs={{0,1},{1,0},{2,3},{3,2},{4,5},{5,4},{6,7},{7,6},{8,9},{9,8},{10,11... | collective-permute-start | bytes 4718600 | tf_op jit(solution)/shard_map/ppermute | solution.py:62
  462.9 24.3 %collective-permute-start.70 = (bf16[256,1024]{1,0:T(8,128)(2,1)S(1)}, bf16[256,1024]{1,0:T(8,128)(2,1)S(1)}, u32[]{:S(2)}, u32[]{:S(2)}) collective-permute-start(bf16[256,1024]{1,0:T(8,128)(2,1)S(1)} %constant_dynamic-slice_fusion.1), channel_id=1, source_target_pairs={{0,8},{2,10},{4,12},{6,14},{8,0},{10,2},{12,4},{14,6},{16,24},{18,... | collective-permute-start | bytes 1572872 | tf_op jit(solution)/shard_map/ppermute | solution.py:82
  477.6 34.1 %collective-permute-start.34 = (bf16[256,1024]{1,0:T(8,128)(2,1)S(1)}, bf16[256,1024]{1,0:T(8,128)(2,1)S(1)}, u32[]{:S(2)}, u32[]{:S(2)}) collective-permute-start(bf16[256,1024]{1,0:T(8,128)(2,1)S(1)} %pad_maximum_fusion.18), channel_id=1, source_target_pairs={{0,2},{2,0},{4,6},{6,4},{8,10},{10,8},{12,14},{14,12},{16,18},{18,... | collective-permute-start | bytes 1572872 | tf_op jit(solution)/shard_map/ppermute | solution.py:82
  487.2 18.9 %collective-permute-start.63 = (bf16[64,2048]{1,0:T(8,128)(2,1)S(1)}, bf16[64,2048]{1,0:T(8,128)(2,1)S(1)}, u32[]{:S(2)}, u32[]{:S(2)}) collective-permute-start(bf16[64,2048]{1,0:T(8,128)(2,1)S(1)} %constant_dynamic-slice_fusion.4), channel_id=1, source_target_pairs={{0,16},{2,18},{4,20},{6,22},{8,24},{10,26},{12,28},{14,30},{16,0},... | collective-permute-start | bytes 786440 | tf_op jit(solution)/shard_map/ppermute | solution.py:82
  488.6 23.1 %collective-permute-start.71 = (bf16[128,1024]{1,0:T(8,128)(2,1)S(1)}, bf16[128,1024]{1,0:T(8,128)(2,1)S(1)}, u32[]{:S(2)}, u32[]{:S(2)}) collective-permute-start(bf16[128,1024]{1,0:T(8,128)(2,1)S(1)} %constant_dynamic-slice_fusion), channel_id=1, source_target_pairs={{0,16},{2,18},{4,20},{6,22},{8,24},{10,26},{12,28},{14,30},{16,0},... | collective-permute-start | bytes 786440 | tf_op jit(solution)/shard_map/ppermute | solution.py:82
  506.2 30.2 %collective-permute-start.20 = (bf16[256,1536]{0,1:T(8,128)(2,1)S(1)}, bf16[256,1536]{0,1:T(8,128)(2,1)S(1)}, u32[]{:S(2)}, u32[]{:S(2)}) collective-permute-start(bf16[256,1536]{0,1:T(8,128)(2,1)S(1)} %constant_dynamic-slice_fusion.24), channel_id=1, source_target_pairs={{0,4},{2,6},{4,0},{6,2},{8,12},{10,14},{12,8},{14,10},{16,20},{18,... | collective-permute-start | bytes 2359304 | tf_op jit(solution)/shard_map/ppermute | solution.py:82
  511.7 18.9 %collective-permute-start.64 = (bf16[64,2048]{1,0:T(8,128)(2,1)S(1)}, bf16[64,2048]{1,0:T(8,128)(2,1)S(1)}, u32[]{:S(2)}, u32[]{:S(2)}) collective-permute-start(bf16[64,2048]{1,0:T(8,128)(2,1)S(1)} %add_convert_fusion.22), channel_id=1, source_target_pairs={{0,16},{2,18},{4,20},{6,22},{8,24},{10,26},{12,28},{14,30},{16,0},... | collective-permute-start | bytes 786440 | tf_op jit(solution)/shard_map/ppermute | solution.py:82
  511.7 24.5 %collective-permute-start.72 = (bf16[128,1024]{1,0:T(8,128)(2,1)S(1)}, bf16[128,1024]{1,0:T(8,128)(2,1)S(1)}, u32[]{:S(2)}, u32[]{:S(2)}) collective-permute-start(bf16[128,1024]{1,0:T(8,128)(2,1)S(1)} %add_convert_fusion.21), channel_id=1, source_target_pairs={{0,16},{2,18},{4,20},{6,22},{8,24},{10,26},{12,28},{14,30},{16,0},... | collective-permute-start | bytes 786440 | tf_op jit(solution)/shard_map/ppermute | solution.py:82
  520.0 48.3 %collective-permute-start.43 = (bf16[256,1536]{0,1:T(8,128)(2,1)S(1)}, bf16[256,1536]{0,1:T(8,128)(2,1)S(1)}, u32[]{:S(2)}, u32[]{:S(2)}) collective-permute-start(bf16[256,1536]{0,1:T(8,128)(2,1)S(1)} %constant_dynamic-slice_fusion.15), channel_id=1, source_target_pairs={{0,4},{2,6},{4,0},{6,2},{8,12},{10,14},{12,8},{14,10},{16,20},{18,... | collective-permute-start | bytes 2359304 | tf_op jit(solution)/shard_map/ppermute | solution.py:82
  536.3 22.4 %collective-permute-start.73 = (bf16[256,1024]{1,0:T(8,128)(2,1)S(1)}, bf16[256,1024]{1,0:T(8,128)(2,1)S(1)}, u32[]{:S(2)}, u32[]{:S(2)}) collective-permute-start(bf16[256,1024]{1,0:T(8,128)(2,1)S(1)} %pad_maximum_fusion.21), channel_id=1, source_target_pairs={{0,8},{2,10},{4,12},{6,14},{8,0},{10,2},{12,4},{14,6},{16,24},{18,... | collective-permute-start | bytes 1572872 | tf_op jit(solution)/shard_map/ppermute | solution.py:82
  536.7 30.3 %collective-permute-start.21 = (bf16[128,1536]{0,1:T(8,128)(2,1)S(1)}, bf16[128,1536]{0,1:T(8,128)(2,1)S(1)}, u32[]{:S(2)}, u32[]{:S(2)}) collective-permute-start(bf16[128,1536]{0,1:T(8,128)(2,1)S(1)} %constant_dynamic-slice_fusion.23), channel_id=1, source_target_pairs={{0,8},{2,10},{4,12},{6,14},{8,0},{10,2},{12,4},{14,6},{16,24},{18,... | collective-permute-start | bytes 1179656 | tf_op jit(solution)/shard_map/ppermute | solution.py:82
  547.8 81.7 %collective-permute-start.66 = (bf16[256,2048]{1,0:T(8,128)(2,1)S(1)}, bf16[256,2048]{1,0:T(8,128)(2,1)S(1)}, u32[]{:S(2)}, u32[]{:S(2)}) collective-permute-start(bf16[256,2048]{1,0:T(8,128)(2,1)S(1)} %pad_maximum_fusion.12), channel_id=1, source_target_pairs={{0,4},{2,6},{4,0},{6,2},{8,12},{10,14},{12,8},{14,10},{16,20},{18,... | collective-permute-start | bytes 3145736 | tf_op jit(solution)/shard_map/ppermute | solution.py:82
  559.0 88.9 %collective-permute-start.74 = (bf16[512,1024]{1,0:T(8,128)(2,1)S(1)}, bf16[512,1024]{1,0:T(8,128)(2,1)S(1)}, u32[]{:S(2)}, u32[]{:S(2)}) collective-permute-start(bf16[512,1024]{1,0:T(8,128)(2,1)S(1)} %pad_maximum_fusion.13), channel_id=1, source_target_pairs={{0,4},{2,6},{4,0},{6,2},{8,12},{10,14},{12,8},{14,10},{16,20},{18,... | collective-permute-start | bytes 3145736 | tf_op jit(solution)/shard_map/ppermute | solution.py:82
  567.5 20.4 %collective-permute-start.22 = (bf16[64,1536]{0,1:T(8,128)(2,1)S(1)}, bf16[64,1536]{0,1:T(8,128)(2,1)S(1)}, u32[]{:S(2)}, u32[]{:S(2)}) collective-permute-start(bf16[64,1536]{0,1:T(8,128)(2,1)S(1)} %constant_dynamic-slice_fusion.22), channel_id=1, source_target_pairs={{0,16},{2,18},{4,20},{6,22},{8,24},{10,26},{12,28},{14,30},{16,0},... | collective-permute-start | bytes 589832 | tf_op jit(solution)/shard_map/ppermute | solution.py:82
  588.1 19.5 %collective-permute-start.23 = (bf16[64,1536]{0,1:T(8,128)(2,1)S(1)}, bf16[64,1536]{0,1:T(8,128)(2,1)S(1)}, u32[]{:S(2)}, u32[]{:S(2)}) collective-permute-start(bf16[64,1536]{0,1:T(8,128)(2,1)S(1)} %add_convert_fusion.19), channel_id=1, source_target_pairs={{0,16},{2,18},{4,20},{6,22},{8,24},{10,26},{12,28},{14,30},{16,0},... | collective-permute-start | bytes 589832 | tf_op jit(solution)/shard_map/ppermute | solution.py:82
  588.2 19.7 %collective-permute-start.44 = (bf16[128,1536]{0,1:T(8,128)(2,1)S(1)}, bf16[128,1536]{0,1:T(8,128)(2,1)S(1)}, u32[]{:S(2)}, u32[]{:S(2)}) collective-permute-start(bf16[128,1536]{0,1:T(8,128)(2,1)S(1)} %constant_dynamic-slice_fusion.14), channel_id=1, source_target_pairs={{0,8},{2,10},{4,12},{6,14},{8,0},{10,2},{12,4},{14,6},{16,24},{18,... | collective-permute-start | bytes 1179656 | tf_op jit(solution)/shard_map/ppermute | solution.py:82
  608.2 19.8 %collective-permute-start.45 = (bf16[64,1536]{0,1:T(8,128)(2,1)S(1)}, bf16[64,1536]{0,1:T(8,128)(2,1)S(1)}, u32[]{:S(2)}, u32[]{:S(2)}) collective-permute-start(bf16[64,1536]{0,1:T(8,128)(2,1)S(1)} %constant_dynamic-slice_fusion.13), channel_id=1, source_target_pairs={{0,16},{2,18},{4,20},{6,22},{8,24},{10,26},{12,28},{14,30},{16,0},... | collective-permute-start | bytes 589832 | tf_op jit(solution)/shard_map/ppermute | solution.py:82
  608.8 19.7 %collective-permute-start.24 = (bf16[128,1536]{0,1:T(8,128)(2,1)S(1)}, bf16[128,1536]{0,1:T(8,128)(2,1)S(1)}, u32[]{:S(2)}, u32[]{:S(2)}) collective-permute-start(bf16[128,1536]{0,1:T(8,128)(2,1)S(1)} %pad_maximum_fusion.22), channel_id=1, source_target_pairs={{0,8},{2,10},{4,12},{6,14},{8,0},{10,2},{12,4},{14,6},{16,24},{18,... | collective-permute-start | bytes 1179656 | tf_op jit(solution)/shard_map/ppermute | solution.py:82
  628.2 19.4 %collective-permute-start.46 = (bf16[64,1536]{0,1:T(8,128)(2,1)S(1)}, bf16[64,1536]{0,1:T(8,128)(2,1)S(1)}, u32[]{:S(2)}, u32[]{:S(2)}) collective-permute-start(bf16[64,1536]{0,1:T(8,128)(2,1)S(1)} %add_convert_fusion.17), channel_id=1, source_target_pairs={{0,16},{2,18},{4,20},{6,22},{8,24},{10,26},{12,28},{14,30},{16,0},... | collective-permute-start | bytes 589832 | tf_op jit(solution)/shard_map/ppermute | solution.py:82
  628.9 31.0 %collective-permute-start.25 = (bf16[256,1536]{0,1:T(8,128)(2,1)S(1)}, bf16[256,1536]{0,1:T(8,128)(2,1)S(1)}, u32[]{:S(2)}, u32[]{:S(2)}) collective-permute-start(bf16[256,1536]{0,1:T(8,128)(2,1)S(1)} %pad_maximum_fusion.16), channel_id=1, source_target_pairs={{0,4},{2,6},{4,0},{6,2},{8,12},{10,14},{12,8},{14,10},{16,20},{18,... | collective-permute-start | bytes 2359304 | tf_op jit(solution)/shard_map/ppermute | solution.py:82
  630.3 51.0 %collective-permute-start.67 = (bf16[512,2048]{1,0:T(8,128)(2,1)S(1)}, bf16[512,2048]{1,0:T(8,128)(2,1)S(1)}, u32[]{:S(2)}, u32[]{:S(2)}) collective-permute-start(bf16[512,2048]{1,0:T(8,128)(2,1)S(1)} %pad_maximum_fusion.4), channel_id=1, source_target_pairs={{0,2},{2,0},{4,6},{6,4},{8,10},{10,8},{12,14},{14,12},{16,18},{18,... | collective-permute-start | bytes 6291464 | tf_op jit(solution)/shard_map/ppermute | solution.py:82
  648.7 31.4 %collective-permute-start.75 = (bf16[1024,1024]{1,0:T(8,128)(2,1)S(1)}, bf16[1024,1024]{1,0:T(8,128)(2,1)S(1)}, u32[]{:S(2)}, u32[]{:S(2)}) collective-permute-start(bf16[1024,1024]{1,0:T(8,128)(2,1)S(1)} %pad_maximum_fusion.5), channel_id=1, source_target_pairs={{0,2},{2,0},{4,6},{6,4},{8,10},{10,8},{12,14},{14,12},{16,18},{18,... | collective-permute-start | bytes 6291464 | tf_op jit(solution)/shard_map/ppermute | solution.py:82
  659.4 18.7 %collective-permute-start.48 = (bf16[256,1536]{0,1:T(8,128)(2,1)S(1)}, bf16[256,1536]{0,1:T(8,128)(2,1)S(1)}, u32[]{:S(2)}, u32[]{:S(2)}) collective-permute-start(bf16[256,1536]{0,1:T(8,128)(2,1)S(1)} %pad_maximum_fusion.17), channel_id=1, source_target_pairs={{0,4},{2,6},{4,0},{6,2},{8,12},{10,14},{12,8},{14,10},{16,20},{18,... | collective-permute-start | bytes 2359304 | tf_op jit(solution)/shard_map/ppermute | solution.py:82
  660.4 30.9 %collective-permute-start.26 = (bf16[512,1536]{0,1:T(8,128)(2,1)S(1)}, bf16[512,1536]{0,1:T(8,128)(2,1)S(1)}, u32[]{:S(2)}, u32[]{:S(2)}) collective-permute-start(bf16[512,1536]{0,1:T(8,128)(2,1)S(1)} %pad_maximum_fusion.6), channel_id=1, source_target_pairs={{0,2},{2,0},{4,6},{6,4},{8,10},{10,8},{12,14},{14,12},{16,18},{18,... | collective-permute-start | bytes 4718600 | tf_op jit(solution)/shard_map/ppermute | solution.py:82
  679.8 23.3 %collective-permute-start.49 = (bf16[512,1536]{0,1:T(8,128)(2,1)}, bf16[512,1536]{0,1:T(8,128)(2,1)}, u32[]{:S(2)}, u32[]{:S(2)}) collective-permute-start(bf16[512,1536]{0,1:T(8,128)(2,1)} %pad_maximum_fusion.7), channel_id=1, source_target_pairs={{0,2},{2,0},{4,6},{6,4},{8,10},{10,8},{12,14},{14,12},{16,18},{18,... | collective-permute-start | bytes 4718600 | tf_op jit(solution)/shard_map/ppermute | solution.py:82
  (97 other events, 808.5 us)

commit v2 on v1

v2 whole, which is shorter than its diff:
```python
import functools
import math

import jax
import jax.numpy as jnp
from jax import lax
from jax.experimental import pallas as pl
from jax.experimental.pallas import tpu as pltpu
from jax.sharding import PartitionSpec as P

HEAD_DIM = 128
GROUP = 128

epsilon = 1e-05
masked_score = -1e30
gelu_factor = 0.7978845608028654
gelu_cubic = 0.044715
log2_e = 1.4426950408889634
vmem_bytes = 60 * 1024 * 1024
small_cost = pl.CostEstimate(flops=1000000, transcendentals=1000, bytes_accessed=100000)


def project(left_rows, right_rows):
    return jnp.dot(left_rows, right_rows, preferred_element_type=jnp.float32)


def times_transposed(left_rows, right_rows):
    return lax.dot_general(
        left_rows, right_rows, (((1,), (1,)), ((), ())), preferred_element_type=jnp.float32
    )


def transposed_times(left_rows, right_rows):
    return lax.dot_general(
        left_rows, right_rows, (((0,), (0,)), ((), ())), preferred_element_type=jnp.float32
    )


def norm_forward(values, gain):
    average = jnp.mean(values, axis=1, keepdims=True)
    centred = values - average
    variance = jnp.mean(centred * centred, axis=1, keepdims=True)
    inverse = lax.rsqrt(variance + epsilon)
    unit_rows = centred * inverse
    return (unit_rows, inverse, (unit_rows * gain).astype(jnp.bfloat16))


def norm_backward(grad_normed, unit_rows, inverse, gain):
    scaled = grad_normed * gain
    first_mean = jnp.mean(scaled, axis=1, keepdims=True)
    second_mean = jnp.mean(scaled * unit_rows, axis=1, keepdims=True)
    grad_rows = inverse * (scaled - first_mean - unit_rows * second_mean)
    return (grad_rows, jnp.sum(grad_normed * unit_rows, axis=0))


def from_peer(block, step):
    count = lax.axis_size("tp")
    return lax.ppermute(block, "tp", [(source, (source - step) % count) for source in range(count)])


def to_peer(block, step):
    count = lax.axis_size("tp")
    return lax.ppermute(block, "tp", [(source, (source + step) % count) for source in range(count)])


def gather_blocks(block):
    return [block] + [from_peer(block, step) for step in range(1, lax.axis_size("tp"))]


def sum_blocks(make_partial):
    received = [
        to_peer(make_partial(step).astype(jnp.bfloat16), step)
        for step in range(1, lax.axis_size("tp"))
    ]
    total = make_partial(0)
    for term in received:
        total = total + term.astype(jnp.float32)
    return total


def swap_sets(block, bit):
    count = lax.axis_size("sets")
    return lax.ppermute(block, "sets", [(source, source ^ (1 << bit)) for source in range(count)])


def set_bit(bit):
    return (lax.axis_index("sets") >> bit) & 1


def halves(block, bit, before=0):
    rows, columns = block.shape[-2:]
    lead = block.shape[:-2]
    view = block.reshape(lead + (2**before, 2, rows // 2 ** (before + 1), columns))
    axis = view.ndim - 3
    mine = set_bit(bit)
    kept, sent = [
        lax.dynamic_slice_in_dim(view, place, 1, axis).reshape(lead + (rows // 2, columns))
        for place in (mine, 1 - mine)
    ]
    return (kept, sent)


def add_pair(kept, received):
    return (kept.astype(jnp.float32) + received.astype(jnp.float32)).astype(jnp.bfloat16)


class Order:
    def __init__(self):
        self.last = ()

    def hold(self, value):
        if not self.last:
            return value
        return lax.optimization_barrier((value, *self.last))[0]

    def mark(self, *values):
        self.last = values


def join(block, received, bit):
    first = set_bit(bit) == 0
    return jnp.concatenate(
        [jnp.where(first, block, received), jnp.where(first, received, block)],
        axis=block.ndim - 2,
    )


def all_bits():
    return list(range(int(math.log2(lax.axis_size("sets")))))


class SetSum:
    def __init__(self, order, block, halve, layout=None, peers_after=None, double=True):
        self.order = order
        self.block = block.astype(jnp.bfloat16)
        self.layout = list(halve if layout is None else layout)
        self.stages = [("halve", bit) for bit in halve]
        if peers_after is not None:
            self.stages.insert(peers_after, ("peers", None))
        if double:
            self.stages += [("double", bit) for bit in reversed(halve)]
        self.last = None
        self.send()

    def send(self):
        kind, bit = self.stages[0]
        if kind == "halve":
            before = self.layout.index(bit)
            self.layout.remove(bit)
            self.kept, sent = halves(self.block, bit, before)
            self.received = [swap_sets(sent, bit)]
        elif kind == "peers":
            self.kept, sent = self.block[0], self.block[1:]
            self.received = [
                to_peer(sent[step], step + 1) for step in range(sent.shape[0])
            ]
        else:
            self.kept = sent = self.block
            self.received = [swap_sets(sent, bit)]
        self.order.mark(sent)

    def advance(self):
        if not self.stages:
            return
        kind, bit = self.stages.pop(0)
        received = self.order.hold(tuple(self.received))
        if kind == "double" and not self.stages:
            self.last = (self.kept, received[0], bit)
            self.order.mark(received[0])
            return
        if kind == "double":
            self.block = join(self.kept, received[0], bit)
        else:
            total = self.kept.astype(jnp.float32)
            for term in received:
                total = total + term.astype(jnp.float32)
            self.block = total.astype(jnp.bfloat16)
        if self.stages:
            self.send()
        else:
            self.order.mark(self.block)

    def result(self, place=None):
        kept, received, bit = self.last
        if place is not None:
            kept, received = kept[place], received[place]
        return join(kept, received, bit).astype(jnp.float32)


def stack_output(weight):
    width = weight.shape[0]
    return jnp.concatenate(
        [weight[:, start : start + width] for start in range(0, weight.shape[1], width)], axis=0
    )


def unstack_output(stacked):
    width = stacked.shape[1]
    return jnp.concatenate(
        [stacked[start : start + width] for start in range(0, stacked.shape[0], width)], axis=1
    )


def multiplicity_kernel(chosen_ref, out_ref):
    row_count = out_ref.shape[0]
    group_count, key_count = chosen_ref.shape
    row_ids = lax.broadcasted_iota(jnp.int32, (row_count, key_count), 0) + (
        pl.program_id(0) * row_count
    )
    lanes = lax.broadcasted_iota(jnp.int32, (key_count, 128), 1)

    def one_group(group, total):
        picked = chosen_ref[pl.ds(group, 1), :]
        hits = jnp.where(row_ids == picked, 1.0, 0.0).astype(jnp.bfloat16)
        place = jnp.where(lanes == group, 1.0, 0.0).astype(jnp.bfloat16)
        return total + project(hits, place)

    total = lax.fori_loop(0, group_count, one_group, jnp.zeros((row_count, 128), jnp.float32))
    out_ref[...] = jnp.where(total > 0.0, jnp.log2(jnp.maximum(total, 1.0)), masked_score)


def log_multiplicity(chosen, counts, table_rows):
    group_count, key_count = chosen.shape
    valid = jnp.arange(key_count, dtype=jnp.int32)[None, :] < counts[:, None]
    chosen = jnp.where(valid, chosen, -1)
    block = math.gcd(table_rows, 512)
    return pl.pallas_call(
        multiplicity_kernel,
        grid=(table_rows // block,),
        in_specs=[pl.BlockSpec((group_count, key_count), lambda i: (0, 0))],
        out_specs=pl.BlockSpec((block, 128), lambda i: (i, 0)),
        out_shape=jax.ShapeDtypeStruct((table_rows, 128), jnp.float32),
        name="multiplicity",
    )(chosen)


def fill_bias(counts_ref, bias_ref, span, first_group):
    row_count = bias_ref.shape[0]
    lanes = lax.broadcasted_iota(jnp.int32, (row_count, 128), 1)
    counts = counts_ref[...]
    for part in range(span):
        group = first_group + pl.program_id(0) * span + part
        column = jnp.sum(jnp.where(lanes == group, counts, 0.0), axis=1, keepdims=True)
        bias_ref[:, part * GROUP : (part + 1) * GROUP] = jnp.broadcast_to(
            column, (row_count, GROUP)
        )


def cross_forward_kernel(
    counts_ref,
    query_ref,
    key_ref,
    value_t_ref,
    out_ref,
    log_ref,
    bias_ref,
    *,
    heads,
    span,
    scale,
    first_group,
):
    fill_bias(counts_ref, bias_ref, span, first_group)
    for head in range(heads):
        cols = slice(head * HEAD_DIM, (head + 1) * HEAD_DIM)
        scores = times_transposed(key_ref[:, cols], query_ref[:, cols])
        scores = scores * (scale * log2_e) + bias_ref[...]
        top = jnp.max(scores, axis=0, keepdims=True)
        raised = jnp.exp2(scores - top)
        total = jnp.sum(raised, axis=0, keepdims=True)
        mixed = project(value_t_ref[cols, :], raised.astype(jnp.bfloat16)) / total
        out_ref[:, cols] = mixed.T.astype(jnp.bfloat16)
        log_ref[0, head : head + 1, :] = top + jnp.log2(total)


def cross_forward(log_counts, queries, key_table, value_table_t, scale, first_group):
    row_count, width = queries.shape
    table_rows = key_table.shape[0]
    heads = width // HEAD_DIM
    groups = row_count // GROUP
    span = 2 if groups % 2 == 0 else 1
    rows = span * GROUP
    return pl.pallas_call(
        functools.partial(
            cross_forward_kernel, heads=heads, span=span, scale=scale, first_group=first_group
        ),
        grid=(groups // span,),
        in_specs=[
            pl.BlockSpec((table_rows, 128), lambda i: (0, 0)),
            pl.BlockSpec((rows, width), lambda i: (i, 0)),
            pl.BlockSpec((table_rows, width), lambda i: (0, 0)),
            pl.BlockSpec((width, table_rows), lambda i: (0, 0)),
        ],
        out_specs=[
            pl.BlockSpec((rows, width), lambda i: (i, 0)),
            pl.BlockSpec((1, heads, rows), lambda i: (i, 0, 0)),
        ],
        out_shape=[
            jax.ShapeDtypeStruct((row_count, width), jnp.bfloat16),
            jax.ShapeDtypeStruct((groups // span, heads, rows), jnp.float32),
        ],
        scratch_shapes=[pltpu.VMEM((table_rows, rows), jnp.float32)],
        compiler_params=pltpu.CompilerParams(vmem_limit_bytes=vmem_bytes),
        cost_estimate=small_cost,
        name="cross_forward",
    )(log_counts, queries, key_table, value_table_t)


def cross_backward_kernel(*refs, heads, span, scale, first_group, start, finish):
    counts_ref, query_ref, grad_ref, log_ref, key_ref, key_t_ref, value_ref = refs[:7]
    refs = refs[7:]
    if not start:
        key_start_ref, value_start_ref = refs[:2]
        refs = refs[2:]
    grad_query_ref, grad_key_ref, grad_value_ref, bias_ref = refs[:4]
    key_sum_ref, value_sum_ref = refs[4:] if finish else (grad_key_ref, grad_value_ref)
    step = pl.program_id(0)

    @pl.when(step == 0)
    def _():
        if start:
            key_sum_ref[...] = jnp.zeros_like(key_sum_ref)
            value_sum_ref[...] = jnp.zeros_like(value_sum_ref)
        else:
            key_sum_ref[...] = key_start_ref[...]
            value_sum_ref[...] = value_start_ref[...]

    fill_bias(counts_ref, bias_ref, span, first_group)
    for head in range(heads):
        cols = slice(head * HEAD_DIM, (head + 1) * HEAD_DIM)
        query = query_ref[:, cols]
        grad = grad_ref[:, cols]
        scores = times_transposed(key_ref[:, cols], query)
        weights = jnp.exp2(
            scores * (scale * log2_e) + bias_ref[...] - log_ref[0, head : head + 1, :]
        )
        grad_weights = times_transposed(value_ref[:, cols], grad)
        inner = jnp.sum(weights * grad_weights, axis=0, keepdims=True)
        grad_scores = (weights * (grad_weights - inner)).astype(jnp.bfloat16)
        value_sum_ref[:, cols] += project(weights.astype(jnp.bfloat16), grad)
        key_sum_ref[:, cols] += project(grad_scores, query)
        grad_query = project(key_t_ref[cols, :], grad_scores) * scale
        grad_query_ref[:, cols] = grad_query.T.astype(jnp.bfloat16)

    if finish:

        @pl.when(step == pl.num_programs(0) - 1)
        def _():
            grad_key_ref[...] = (key_sum_ref[...] * scale).astype(jnp.bfloat16)
            grad_value_ref[...] = value_sum_ref[...].astype(jnp.bfloat16)


def cross_backward(
    log_counts,
    queries,
    grad_attended,
    logs,
    key_table,
    key_table_t,
    value_table,
    scale,
    first_group,
    earlier,
    finish,
):
    row_count, width = queries.shape
    table_rows = key_table.shape[0]
    heads = width // HEAD_DIM
    groups = row_count // GROUP
    span = 2 if groups % 2 == 0 else 1
    rows = span * GROUP
    whole = pl.BlockSpec((table_rows, width), lambda i: (0, 0))
    block = pl.BlockSpec((rows, width), lambda i: (i, 0))
    table_type = jnp.bfloat16 if finish else jnp.float32
    sums = pltpu.VMEM((table_rows, width), jnp.float32)
    return pl.pallas_call(
        functools.partial(
            cross_backward_kernel,
            heads=heads,
            span=span,
            scale=scale,
            first_group=first_group,
            start=not earlier,
            finish=finish,
        ),
        grid=(groups // span,),
        in_specs=[
            pl.BlockSpec((table_rows, 128), lambda i: (0, 0)),
            block,
            block,
            pl.BlockSpec((1, heads, rows), lambda i: (i, 0, 0)),
            whole,
            pl.BlockSpec((width, table_rows), lambda i: (0, 0)),
            whole,
        ]
        + [whole] * len(earlier),
        out_specs=[block, whole, whole],
        out_shape=[
            jax.ShapeDtypeStruct((row_count, width), jnp.bfloat16),
            jax.ShapeDtypeStruct((table_rows, width), table_type),
            jax.ShapeDtypeStruct((table_rows, width), table_type),
        ],
        scratch_shapes=[pltpu.VMEM((table_rows, rows), jnp.float32)]
        + ([sums, sums] if finish else []),
        compiler_params=pltpu.CompilerParams(vmem_limit_bytes=vmem_bytes),
        cost_estimate=small_cost,
        name="cross_backward",
    )(log_counts, queries, grad_attended, logs, key_table, key_table_t, value_table, *earlier)


def head_columns(head, heads_block):
    base = (head // heads_block) * 3 * heads_block + head % heads_block
    return [
        slice((base + kind * heads_block) * HEAD_DIM, (base + kind * heads_block + 1) * HEAD_DIM)
        for kind in range(3)
    ]


def self_forward_kernel(rows_ref, out_ref, log_ref, *, heads, heads_block, scale):
    columns = [head_columns(head, heads_block) for head in range(heads)]
    scores = [
        times_transposed(rows_ref[:, key_cols], rows_ref[:, query_cols])
        for query_cols, key_cols, _ in columns
    ]
    weights = []
    for head in range(heads):
        scaled = scores[head] * (scale * log2_e)
        top = jnp.max(scaled, axis=0, keepdims=True)
        raised = jnp.exp2(scaled - top)
        total = jnp.sum(raised, axis=0, keepdims=True)
        weights.append((raised * (1.0 / total)).astype(jnp.bfloat16))
        log_ref[0, head : head + 1, :] = top + jnp.log2(total)
    for head in range(heads):
        mixed = transposed_times(weights[head], rows_ref[:, columns[head][2]])
        out_ref[:, head * HEAD_DIM : (head + 1) * HEAD_DIM] = mixed.astype(jnp.bfloat16)


def self_forward(mixed_rows, heads, heads_block, scale):
    row_count, width = mixed_rows.shape
    groups = row_count // GROUP
    return pl.pallas_call(
        functools.partial(
            self_forward_kernel, heads=heads, heads_block=heads_block, scale=scale
        ),
        grid=(groups,),
        in_specs=[pl.BlockSpec((GROUP, width), lambda i: (i, 0))],
        out_specs=[
            pl.BlockSpec((GROUP, heads * HEAD_DIM), lambda i: (i, 0)),
            pl.BlockSpec((1, heads, GROUP), lambda i: (i, 0, 0)),
        ],
        out_shape=[
            jax.ShapeDtypeStruct((row_count, heads * HEAD_DIM), jnp.bfloat16),
            jax.ShapeDtypeStruct((groups, heads, GROUP), jnp.float32),
        ],
        cost_estimate=small_cost,
        name="self_forward",
    )(mixed_rows)


def self_backward_kernel(rows_ref, grad_ref, log_ref, out_ref, *, heads, heads_block, scale):
    columns = [head_columns(head, heads_block) for head in range(heads)]
    grads = [slice(head * HEAD_DIM, (head + 1) * HEAD_DIM) for head in range(heads)]
    scores = [
        times_transposed(rows_ref[:, key_cols], rows_ref[:, query_cols])
        for query_cols, key_cols, _ in columns
    ]
    grad_weights = [
        times_transposed(rows_ref[:, columns[head][2]], grad_ref[:, grads[head]])
        for head in range(heads)
    ]
    weights, grad_scores = [], []
    for head in range(heads):
        soft = jnp.exp2(scores[head] * (scale * log2_e) - log_ref[0, head : head + 1, :])
        inner = jnp.sum(soft * grad_weights[head], axis=0, keepdims=True)
        grad_scores.append((soft * (grad_weights[head] - inner)).astype(jnp.bfloat16))
        weights.append(soft.astype(jnp.bfloat16))
    for head in range(heads):
        query_cols, key_cols, value_cols = columns[head]
        out_ref[:, value_cols] = project(weights[head], grad_ref[:, grads[head]]).astype(
            jnp.bfloat16
        )
        out_ref[:, key_cols] = (project(grad_scores[head], rows_ref[:, query_cols]) * scale).astype(
            jnp.bfloat16
        )
        out_ref[:, query_cols] = (
            transposed_times(grad_scores[head], rows_ref[:, key_cols]) * scale
        ).astype(jnp.bfloat16)


def self_backward(mixed_rows, grad_attended, logs, heads, heads_block, scale):
    row_count, width = mixed_rows.shape
    groups = row_count // GROUP
    return pl.pallas_call(
        functools.partial(
            self_backward_kernel, heads=heads, heads_block=heads_block, scale=scale
        ),
        grid=(groups,),
        in_specs=[
            pl.BlockSpec((GROUP, width), lambda i: (i, 0)),
            pl.BlockSpec((GROUP, heads * HEAD_DIM), lambda i: (i, 0)),
            pl.BlockSpec((1, heads, GROUP), lambda i: (i, 0, 0)),
        ],
        out_specs=pl.BlockSpec((GROUP, width), lambda i: (i, 0)),
        out_shape=jax.ShapeDtypeStruct((row_count, width), jnp.bfloat16),
        cost_estimate=small_cost,
        name="self_backward",
    )(mixed_rows, grad_attended, logs)


def feed_kernel(rows_ref, grad_ref, up_ref, down_ref, *rest):
    active_ref, grad_hidden_ref, grad_rows_ref, sum_ref = rest[-4:]
    step = pl.program_id(0)

    @pl.when(step == 0)
    def _():
        sum_ref[...] = jnp.zeros_like(sum_ref)

    hidden = project(rows_ref[...], up_ref[...])
    grad_active = times_transposed(grad_ref[...], down_ref[...])
    square = hidden * hidden
    bend = jnp.tanh(gelu_factor * hidden * (1.0 + gelu_cubic * square))
    half_sum = 0.5 * (1.0 + bend)
    slope = half_sum + (0.5 * gelu_factor) * hidden * (1.0 - bend * bend) * (
        1.0 + (3.0 * gelu_cubic) * square
    )
    grad_hidden = (slope * grad_active).astype(jnp.bfloat16)
    active_ref[...] = (hidden * half_sum).astype(jnp.bfloat16)
    grad_hidden_ref[...] = grad_hidden
    sum_ref[...] += times_transposed(grad_hidden, up_ref[...])

    @pl.when(step == pl.num_programs(0) - 1)
    def _():
        grad_rows_ref[...] = sum_ref[...].astype(grad_rows_ref.dtype)


def feed_block(first_row, total_rows, rows, grads, up, down, earlier, sum_type):
    row_count, width = rows.shape
    hidden_width = up.shape[1]
    tile = math.gcd(hidden_width, 512)
    place = first_row // row_count
    result = jax.ShapeDtypeStruct((total_rows, hidden_width), jnp.bfloat16)
    block = pl.BlockSpec((row_count, tile), lambda i: (place, i))
    whole = pl.BlockSpec((row_count, width), lambda i: (0, 0))
    return pl.pallas_call(
        feed_kernel,
        grid=(hidden_width // tile,),
        in_specs=[
            whole,
            whole,
            pl.BlockSpec((width, tile), lambda i: (0, i)),
            pl.BlockSpec((tile, width), lambda i: (i, 0)),
        ]
        + [pl.BlockSpec(memory_space=pl.ANY)] * len(earlier),
        out_specs=[block, block, whole],
        out_shape=[result, result, jax.ShapeDtypeStruct((row_count, width), sum_type)],
        scratch_shapes=[pltpu.VMEM((row_count, width), jnp.float32)],
        input_output_aliases={4: 0, 5: 1} if earlier else {},
        compiler_params=pltpu.CompilerParams(vmem_limit_bytes=vmem_bytes),
        cost_estimate=small_cost,
        name="feed_hidden",
    )(rows, grads, up, down, *earlier)


def local(
    latents,
    inputs,
    neighbours,
    key_counts,
    filled,
    cotangent,
    cross_gain,
    cross_query,
    cross_key,
    cross_value,
    cross_output,
    self_gain,
    self_query,
    self_key,
    self_value,
    self_output,
    feed_gain,
    feed_up,
    feed_down,
):
    tp_count = lax.axis_size("tp")
    tp_index = lax.axis_index("tp")
    bits = all_bits()
    rows_dev = latents.shape[0]
    table_dev = inputs.shape[0]
    table_rows = table_dev * tp_count
    group_count = neighbours.shape[0]
    local_groups = rows_dev // GROUP
    scale = 1.0 / math.sqrt(HEAD_DIM)
    first_group = tp_index * local_groups
    group_alive = (first_group + jnp.arange(local_groups, dtype=jnp.int32) < filled[0]).astype(
        jnp.float32
    )
    alive_rows = jnp.repeat(group_alive, GROUP)[:, None]

    chosen = jnp.roll(neighbours, -first_group, axis=0)
    counts = jnp.roll(key_counts, -first_group, axis=0)
    chosen = (chosen - tp_index * table_dev) % table_rows
    log_counts = log_multiplicity(chosen, counts, table_rows)

    def block_rows(array, step):
        return array[step * rows_dev : (step + 1) * rows_dev]

    def table_part(array, step):
        return array[step * table_dev : (step + 1) * table_dev]

    heads_block = self_query.shape[1] // HEAD_DIM
    heads = heads_block * tp_count
    width = heads_block * HEAD_DIM
    model = self_query.shape[0]
    hidden_width = feed_up.shape[1]
    feed_width = min(hidden_width, model)
    cross_first = bits[:1] + bits[2:] + bits[1:2]
    natural = list(reversed(bits))
    order = Order()

    piece_rows = rows_dev // 2 if local_groups % 2 == 0 else rows_dev
    piece_starts = list(range(0, rows_dev, piece_rows))

    def pieces(block):
        return [block[start : start + piece_rows] for start in piece_starts]

    peer_inputs = gather_blocks(inputs)
    own_slice = jnp.stack([self_query, self_key, self_value, stack_output(self_output)], axis=0)
    share = model // lax.axis_size("sets")
    own_slice = lax.dynamic_slice_in_dim(own_slice, lax.axis_index("sets") * share, share, 1)
    peer_slices = [from_peer(own_slice, step) for step in range(1, tp_count)]

    state_rows = latents.astype(jnp.float32)
    grad_final = cotangent.astype(jnp.float32)
    grad_own = (alive_rows * grad_final).astype(jnp.bfloat16)
    unit_cross, inverse_cross, normed_cross = norm_forward(state_rows, cross_gain)
    order.mark(normed_cross)
    log_counts = log_multiplicity(order.hold(chosen), counts, table_rows)
    order.mark(log_counts)
    embedded = jnp.concatenate(order.hold(tuple(peer_inputs)), axis=0)
    order.mark(embedded)
    rows_cross = gather_blocks(order.hold(normed_cross))
    peer_stacks = [
        lax.all_gather(part, "sets", axis=1, tiled=True) for part in order.hold(tuple(peer_slices))
    ]
    key_table = project(order.hold(embedded), cross_key).astype(jnp.bfloat16)
    value_table_t = lax.dot_general(
        cross_value, embedded, (((0,), (1,)), ((), ())), preferred_element_type=jnp.float32
    ).astype(jnp.bfloat16)
    order.mark(key_table, value_table_t)
    grad_pieces = [[] for _ in range(tp_count)]
    queries_cross, attended_cross, logs_cross = [], [], []
    for step in range(tp_count):
        queries = project(order.hold(rows_cross[step]), cross_query).astype(jnp.bfloat16)
        order.mark(queries)
        if step == tp_count - 1:
            for peer in range(1, tp_count):
                grad_pieces[peer].append(from_peer(order.hold(pieces(grad_own)[0]), peer))
        attended, logs = cross_forward(
            log_counts, order.hold(queries), key_table, value_table_t, scale, step * local_groups
        )
        order.mark(attended)
        queries_cross.append(queries)
        attended_cross.append(attended)
        logs_cross.append(logs)
    cross_terms = []
    for step in range(1, tp_count):
        grad_pieces[step][0] = order.hold(grad_pieces[step][0])
        term = project(attended_cross[step], cross_output).astype(jnp.bfloat16)
        cross_terms.append(to_peer(term, step))
        order.mark(term, grad_pieces[step][0])
    branch = project(order.hold(attended_cross[0]), cross_output)
    order.mark(branch)
    key_table_t = lax.dot_general(
        cross_key, order.hold(embedded), (((0,), (1,)), ((), ())), preferred_element_type=jnp.float32
    ).astype(jnp.bfloat16)
    value_table = project(order.hold(embedded), cross_value).astype(jnp.bfloat16)
    order.mark(key_table_t, value_table)
    peer_stacks = order.hold(tuple(peer_stacks))
    mixed_weight = jnp.concatenate(
        [self_query, self_key, self_value]
        + [stack[kind] for stack in peer_stacks for kind in range(3)],
        axis=1,
    )
    output_weight = jnp.concatenate(
        [self_output] + [unstack_output(stack[3]) for stack in peer_stacks], axis=0
    )
    mixed_weight, output_weight = lax.optimization_barrier((mixed_weight, output_weight))
    order.mark(mixed_weight, output_weight)
    for term in order.hold(tuple(cross_terms)):
        branch = branch + term.astype(jnp.float32)
    after_cross = state_rows + alive_rows * branch
    order.mark(after_cross)

    for piece in pieces(grad_own)[1:]:
        for step in range(1, tp_count):
            grad_pieces[step].append(from_peer(order.hold(piece), step))
    unit_self, inverse_self, normed_self = norm_forward(after_cross, self_gain)
    mixed_rows = project(normed_self, mixed_weight).astype(jnp.bfloat16)
    attended_self, logs_self = self_forward(mixed_rows, heads, heads_block, scale)
    order.mark(attended_self)
    for step in range(1, tp_count):
        grad_pieces[step] = list(order.hold(tuple(grad_pieces[step])))
    order.mark(attended_self, *[part for parts in grad_pieces for part in parts])
    after_self = after_cross + alive_rows * project(order.hold(attended_self), output_weight)

    unit_feed, inverse_feed, normed_feed = norm_forward(after_self, feed_gain)
    order.mark(normed_feed)
    feed_pieces = [[] for _ in range(tp_count)]
    for piece in pieces(normed_feed):
        for step in range(1, tp_count):
            feed_pieces[step].append(from_peer(piece, step))
    *filled_parts, grad_normed_feed = feed_block(
        0,
        rows_dev * tp_count,
        order.hold(normed_feed),
        grad_own,
        feed_up,
        feed_down,
        (),
        jnp.float32,
    )
    order.mark(*filled_parts)
    normed_terms = [[] for _ in range(tp_count)]
    for step in range(1, tp_count):
        for place, start in enumerate(piece_starts):
            *filled_parts, term = feed_block(
                step * rows_dev + start,
                rows_dev * tp_count,
                order.hold(feed_pieces[step][place]),
                grad_pieces[step][place],
                feed_up,
                feed_down,
                filled_parts,
                jnp.bfloat16,
            )
            normed_terms[step].append(to_peer(term, step))
            order.mark(term)
    activated, grad_hidden = filled_parts
    feed_all = jnp.concatenate(
        [normed_feed] + [piece for parts in feed_pieces for piece in parts], axis=0
    )
    grad_all = jnp.concatenate(
        [grad_own] + [piece for parts in grad_pieces for piece in parts], axis=0
    )
    received = [[] for _ in range(tp_count)]
    for place in range(len(piece_starts)):
        terms = order.hold(tuple(normed_terms[step][place] for step in range(1, tp_count)))
        for step in range(1, tp_count):
            received[step].append(terms[step - 1])
        order.mark(*terms)
        if place == 0:
            held = order.hold(grad_hidden)
            grad_up = jnp.stack(
                [
                    transposed_times(feed_all, held[:, start : start + feed_width])
                    for start in range(0, hidden_width, feed_width)
                ]
            )
            up_sum = SetSum(order, grad_up, bits, layout=natural, double=False)
    grad_down = transposed_times(order.hold(activated), grad_all).astype(jnp.bfloat16)
    if hidden_width >= model:
        grad_down = grad_down.reshape(hidden_width // model, model, model)
    else:
        grad_down = stack_output(grad_down)[None]
    down_sum = SetSum(order, grad_down, cross_first, layout=natural, double=False)
    up_sum.advance()
    for step in range(1, tp_count):
        term = jnp.concatenate(received[step], axis=0)
        grad_normed_feed = order.hold(grad_normed_feed) + term.astype(jnp.float32)
    order.mark(grad_normed_feed)
    grad_rows, grad_feed_gain = norm_backward(
        order.hold(grad_normed_feed), unit_feed, inverse_feed, feed_gain
    )
    grad_after_self = grad_final + grad_rows

    grad_branch = (alive_rows * grad_after_self).astype(jnp.bfloat16)
    order.mark(grad_branch)
    down_sum.advance()
    grad_attended = times_transposed(order.hold(grad_branch), output_weight).astype(jnp.bfloat16)
    grad_mixed = self_backward(mixed_rows, grad_attended, logs_self, heads, heads_block, scale)
    order.mark(grad_mixed)
    grad_normed_self = times_transposed(order.hold(grad_mixed), mixed_weight)
    grad_rows, grad_self_gain = norm_backward(grad_normed_self, unit_self, inverse_self, self_gain)
    grad_after_cross = grad_after_self + grad_rows
    grad_cross_blocks = gather_blocks((alive_rows * grad_after_cross).astype(jnp.bfloat16))
    order.mark(grad_cross_blocks[0])

    up_sum.advance()
    down_sum.advance()
    late_mixed = order.hold(grad_mixed)
    self_terms = []
    for step in range(tp_count):
        terms = [
            transposed_times(
                normed_self, late_mixed[:, (3 * step + kind) * width : (3 * step + kind + 1) * width]
            ).astype(jnp.bfloat16)
            for kind in range(3)
        ]
        output_term = transposed_times(
            attended_self[:, step * width : (step + 1) * width], grad_branch
        ).astype(jnp.bfloat16)
        self_terms.append(terms + [stack_output(output_term)])
    self_sums = [
        SetSum(
            order,
            order.hold(jnp.stack([jnp.stack(terms[first : first + 2]) for terms in self_terms])),
            halve,
            layout=natural,
            peers_after=peers_after,
            double=False,
        )
        for first, halve, peers_after in ((0, bits, 1), (2, bits, len(bits)))
    ]

    grad_queries, sums = [], ()
    for step in range(tp_count):
        block = order.hold(grad_cross_blocks[step])
        grad_attended = times_transposed(block, cross_output).astype(jnp.bfloat16)
        grad_query, *sums = cross_backward(
            log_counts,
            queries_cross[step],
            grad_attended,
            logs_cross[step],
            key_table,
            key_table_t,
            value_table,
            scale,
            step * local_groups,
            tuple(sums),
            step == tp_count - 1,
        )
        grad_queries.append(grad_query)
        order.mark(grad_query)
        if step == 0:
            up_sum.advance()
            down_sum.advance()
            self_sums[1].advance()
            self_sums[0].advance()
    grad_key_table, grad_value_table = sums
    while up_sum.stages or down_sum.stages:
        up_sum.advance()
        down_sum.advance()
    feed_result = lax.all_gather(
        jnp.concatenate([up_sum.block, down_sum.block], axis=0), "sets", axis=1, tiled=True
    )
    held_keys, held_values = order.hold((grad_key_table, grad_value_table))
    grad_key = transposed_times(embedded, held_keys).astype(jnp.bfloat16)
    grad_value = transposed_times(embedded, held_values).astype(jnp.bfloat16)
    first_sum = SetSum(order, jnp.stack([grad_key, grad_value]), bits)
    self_sums[1].advance()
    output_terms, query_terms = [], []
    for step in range(tp_count):
        output_terms.append(
            transposed_times(attended_cross[step], order.hold(grad_cross_blocks[step]))
        )
        query_terms.append(transposed_times(rows_cross[step], order.hold(grad_queries[step])))
    grad_query = functools.reduce(jnp.add, query_terms).astype(jnp.bfloat16)
    grad_output = functools.reduce(jnp.add, output_terms).astype(jnp.bfloat16)
    second_sum = SetSum(order, jnp.stack([grad_query, stack_output(grad_output)]), cross_first)
    self_sums[0].advance()
    first_sum.advance()
    second_sum.advance()

    def query_term(step):
        return times_transposed(order.hold(grad_queries[step]), cross_query)

    def input_term(step):
        keys, values = order.hold(
            (table_part(grad_key_table, step), table_part(grad_value_table, step))
        )
        return times_transposed(keys, cross_key) + times_transposed(values, cross_value)

    query_sums, input_sums, final_terms = [], [], []
    for step in range(1, tp_count):
        term = query_term(step).astype(jnp.bfloat16)
        query_sums.append(to_peer(term, step))
        order.mark(term)
    grad_normed_cross = query_term(0)
    order.mark(grad_normed_cross)
    def advance_all(*totals):
        for total in totals:
            total.advance()

    final_all = project(order.hold(activated), feed_down)
    for step in range(1, tp_count):
        term = block_rows(final_all, step).astype(jnp.bfloat16)
        final_terms.append(to_peer(term, step))
        order.mark(term)
    advance_all(self_sums[1], self_sums[0], first_sum, second_sum)
    for step in range(1, tp_count):
        term = input_term(step).astype(jnp.bfloat16)
        input_sums.append(to_peer(term, step))
        order.mark(term)
    advance_all(self_sums[1], self_sums[0], first_sum, second_sum)
    for term in order.hold(tuple(query_sums)):
        grad_normed_cross = grad_normed_cross + term.astype(jnp.float32)
    grad_rows, grad_cross_gain = norm_backward(
        grad_normed_cross, unit_cross, inverse_cross, cross_gain
    )
    latent_grad = grad_after_cross + grad_rows
    order.mark(latent_grad)
    while any(total.stages for total in self_sums):
        advance_all(self_sums[1], self_sums[0])
    self_result = lax.all_gather(
        jnp.concatenate([total.block for total in self_sums], axis=0), "sets", axis=1, tiled=True
    )
    final_rows = block_rows(final_all, 0)
    for term in order.hold(tuple(final_terms)):
        final_rows = final_rows + term.astype(jnp.float32)
    final_rows = after_self + alive_rows * final_rows
    group_rms = jnp.sqrt(jnp.mean((final_rows * final_rows).reshape(local_groups, -1), axis=1))
    penalty_term = jnp.sum(group_rms * group_alive)
    order.mark(final_rows)
    small = jnp.stack(
        [
            grad_feed_gain,
            grad_self_gain,
            jnp.full_like(grad_feed_gain, penalty_term),
            grad_cross_gain,
        ],
        axis=0,
    )
    spots = [("sets", 1 << bit) for bit in bits]
    step = 1
    while step < tp_count:
        spots.append(("tp", step))
        step *= 2

    def small_step():
        nonlocal small
        if spots:
            axis, step = spots.pop(0)
            received = lax.ppermute(
                small, axis, [(place, place ^ step) for place in range(lax.axis_size(axis))]
            )
            small = small + order.hold(received)
            order.mark(small)

    running = [first_sum, second_sum]
    advance_all(*running)
    small_step()
    up_blocks = hidden_width // feed_width
    feed_result = order.hold(feed_result)
    grad_feed_up = jnp.concatenate(
        [feed_result[place] for place in range(up_blocks)], axis=1
    ).astype(jnp.float32)
    if hidden_width >= model:
        grad_feed_down = feed_result[up_blocks:].reshape(hidden_width, model).astype(jnp.float32)
    else:
        grad_feed_down = unstack_output(feed_result[up_blocks]).astype(jnp.float32)
    order.mark(grad_feed_up, grad_feed_down)
    advance_all(*running)
    small_step()
    input_grad = input_term(0)
    for term in order.hold(tuple(input_sums)):
        input_grad = input_grad + term.astype(jnp.float32)
    order.mark(input_grad)
    while any(total.stages for total in running) or spots:
        advance_all(*running)
        small_step()
    grad_self_query, grad_self_key, grad_self_value = [
        self_result[kind].astype(jnp.float32) for kind in range(3)
    ]
    grad_self_output = unstack_output(self_result[3]).astype(jnp.float32)
    grad_cross_key, grad_cross_value = first_sum.result(0), first_sum.result(1)
    grad_cross_query = second_sum.result(0)
    grad_cross_output = unstack_output(second_sum.result(1))
    grad_feed_gain, grad_self_gain, _, grad_cross_gain = [small[place] for place in range(4)]
    penalty = small[2, 0] / (group_count * lax.axis_size("sets"))
    return (
        final_rows.astype(jnp.bfloat16),
        latent_grad,
        input_grad,
        grad_cross_gain,
        grad_cross_query,
        grad_cross_key,
        grad_cross_value,
        grad_cross_output,
        grad_self_gain,
        grad_self_query,
        grad_self_key,
        grad_self_value,
        grad_self_output,
        grad_feed_gain,
        grad_feed_up,
        grad_feed_down,
        penalty,
    )


def solution(mesh):
    return jax.shard_map(
        local,
        mesh=mesh,
        in_specs=(
            P(("sets", "tp"), None),
            P(("sets", "tp"), None),
            P("sets", None),
            P("sets"),
            P("sets"),
            P(("sets", "tp"), None),
            P(),
            P(None, "tp"),
            P(None, "tp"),
            P(None, "tp"),
            P("tp", None),
            P(),
            P(None, "tp"),
            P(None, "tp"),
            P(None, "tp"),
            P("tp", None),
            P(),
            P(None, "tp"),
            P("tp", None),
        ),
        out_specs=(
            P(("sets", "tp"), None),
            P(("sets", "tp"), None),
            P(("sets", "tp"), None),
            P(),
            P(None, "tp"),
            P(None, "tp"),
            P(None, "tp"),
            P("tp", None),
            P(),
            P(None, "tp"),
            P(None, "tp"),
            P(None, "tp"),
            P("tp", None),
            P(),
            P(None, "tp"),
            P("tp", None),
            P(),
        ),
        check_vma=False,
    )
```

time: 728 us -> 542 us (0.74)
  waiting for transfers between devices: 342 us -> 139 us
  other arithmetic: 64.6 us -> 78.5 us
  between operations: 5.2 us -> 17.9 us
  matrix products: 101 us -> 91.3 us
    ppermute x60 -> x32, waiting for transfers between devices: 247 us -> 102 us  [swap_sets(): lax.ppermute(block, 'sets', [(source, source ^ 1 << bit) for source in ra...]
    ppermute x7 -> x8, waiting for transfers between devices: 50.2 us -> 16.3 us  [from_peer(): lax.ppermute(block, 'tp', [(source, (source - step) % count) for source i...]
    ppermute x7 -> x8, waiting for transfers between devices: 36.8 us -> 6.2 us  [to_peer(): lax.ppermute(block, 'tp', [(source, (source + step) % count) for source i...]
    dot_general x9, matrix products: 47.2 us -> 33 us  [project(): return jnp.dot(left_rows, right_rows, preferred_element_type=jnp.float32)]
    slice x2 -> x16, local copies, waits for them, and re-layouts: 1.12 us -> 13.5 us  [the longest x2 2.92 us: table_part(): return array[step * table_dev:(step + 1) * table_dev]]
    convert_element_type x33 -> x36, other arithmetic: 30.7 us -> 41.3 us  [the longest x26 18.3 us: advance(): self.block = total.astype(jnp.bfloat16)]
    select_n x26 -> x9, other arithmetic: 14.2 us -> 3.83 us  [the longest x8 3.8 us: join(): jnp.where(first, block, received)]
    ppermute x60 -> x32, starting transfers between devices: 39.9 us -> 29.6 us  [swap_sets(): lax.ppermute(block, 'sets', [(source, source ^ 1 << bit) for source in ra...]
  transfers between devices with their start and end apart: 76 -> 56, of which waited for: 39 -> 20; matrix products, arithmetic and copies ran while one was open for 27% -> 36% of each run, Pallas kernels for 10% -> 16%
where the time goes in v2:
time: 542 us; the launch traced here: 536 us
  waiting for transfers between devices  139 us (26%)
  matrix products  91.3 us (17%)
  Pallas kernels  88.1 us (16%)
  other arithmetic  78.5 us (14%)
  local copies, waits for them, and re-layouts  62.6 us (12%)
  starting transfers between devices  58.9 us (11%)
  between operations  17.9 us (3%)
    ppermute x32, waiting for transfers between devices, swap_sets(): lax.ppermute(block, 'sets', [(source, source ^ 1 << bit) for source in ra...  102 us
    dot_general x9, matrix products, project(): return jnp.dot(left_rows, right_rows, preferred_element_type=jnp.float32)  33 us
    dot_general x17, matrix products, transposed_times(): lax.dot_general(left_rows, right_rows, (((0,), (0,)), ((), ())), preferre...  31.5 us
    ppermute x32, starting transfers between devices, swap_sets(): lax.ppermute(block, 'sets', [(source, source ^ 1 << bit) for source in ra...  29.6 us
    unnamed x184, local copies, waits for them, and re-layouts  29.4 us
    pallas_call x3, Pallas kernels, feed_block(): pl.pallas_call(feed_kernel, grid=(hidden_width // tile,), in_specs=[whole...  28.9 us
    pallas_call x2, Pallas kernels, cross_backward(): pl.pallas_call(functools.partial(cross_backward_kernel, heads=heads, span...  23.9 us
    dot_general x10, matrix products, times_transposed(): lax.dot_general(left_rows, right_rows, (((1,), (1,)), ((), ())), preferre...  19.1 us
  transfers between devices with their start and end apart: 56, of which 20 were waited for; matrix products, arithmetic and copies ran while one was open for 36% of the time, Pallas kernels for 16%

profile of v2, /device:TPU:0, one launch (start us, length us, event | category | flops | bytes accessed | tf_op | source)
XLA Modules:
  0.0 536.3 jit_solution(4852235088094874066)
XLA Ops:
  7.2 3.0 collective-permute-start
  16.0 6.6 %multiplicity.1.counts_ref.refs_0_ = f32[1024,128]{1,0:T(8,128)} custom-call(s32[8,512]{1,0:T(8,128)} %fusion.96.chosen_ref), custom_call_target="tpu_custom_call" | custom-call | tf_op jit(solution)/shard_map/multiplicity/pallas_call | solution.py:227
  22.6 12.0 %collective-permute-done = bf16[512,1024]{1,0:T(8,128)(2,1)} collective-permute-done((bf16[512,1024]{1,0:T(8,128)(2,1)}, bf16[512,1024]{1,0:T(8,128)(2,1)}, u32[]{:S(2)}, u32[]{:S(2)}) %collective-permute-start) | collective-permute-done | bytes 1048608 | tf_op jit(solution)/shard_map/ppermute | solution.py:58
  45.3 3.9 fusion.43.value_t_ref
  49.1 4.0 convolution_convert_fusion.8.key_ref.refs_4_
  53.1 2.7 convolution_convert_fusion.22.query_ref.refs_1_
  55.8 8.9 %cross_forward.2 = (bf16[512,512]{1,0:T(8,128)(2,1)}, f32[2,4,256]{2,1,0:T(4,128)}) custom-call(f32[1024,128]{1,0:T(8,128)} %multiplicity.1.counts_ref.refs_0_, bf16[512,512]{1,0:T(8,128)(2,1)} %convolution_convert_fusion.22.query_ref.refs_1_, bf16[1024,512]{1,0:T(8,128)(2,1)} %convolution_convert_fusion.8.key_ref.refs_4_, bf16[512,1024]{1,0:T(8,128)(2,1)} %fusion.43.value_t_ref), custom_call_target="tpu_custom_call" | custom-call | flops 1000000 | bytes 100000 | tf_op jit(solution)/shard_map/cross_forward/pallas_call | solution.py:283
  67.1 3.4 convolution_convert_fusion.21.query_ref.refs_1_
  74.2 8.4 %cross_forward.3 = (bf16[512,512]{1,0:T(8,128)(2,1)}, f32[2,4,256]{2,1,0:T(4,128)}) custom-call(f32[1024,128]{1,0:T(8,128)} %multiplicity.1.counts_ref.refs_0_, bf16[512,512]{1,0:T(8,128)(2,1)} %convolution_convert_fusion.21.query_ref.refs_1_, bf16[1024,512]{1,0:T(8,128)(2,1)} %convolution_convert_fusion.8.key_ref.refs_4_, bf16[512,1024]{1,0:T(8,128)(2,1)} %fusion.43.value_t_ref), custom_call_target="tpu_custom_call" | custom-call | flops 1000000 | bytes 100000 | tf_op jit(solution)/shard_map/cross_forward/pallas_call | solution.py:283
  82.6 3.2 convolution_convert_fusion.18
  88.4 3.9 convolution_convert_fusion.5.refs_6_
  92.3 3.9 fusion.44.refs_5_
  103.7 4.7 collective-permute-done.3
  114.7 5.0 convolution_convert_fusion.rows_ref
  119.7 4.9 self_forward.1
  125.4 3.9 fusion.114
  134.4 11.8 %feed_hidden.3 = (bf16[1024,2048]{1,0:T(8,128)(2,1)}, bf16[1024,2048]{1,0:T(8,128)(2,1)}, f32[512,1024]{1,0:T(8,128)}) custom-call(bf16[512,1024]{1,0:T(8,128)(2,1)} %copy-done.10, bf16[512,1024]{1,0:T(8,128)(2,1)} %copy-done.12, bf16[1024,2048]{1,0:T(8,128)(2,1)} %up_ref.5, bf16[2048,1024]{1,0:T(8,128)(2,1)} %down_ref.5), custom_call_target="tpu_custom_call" | custom-call | flops 1000000 | bytes 100000 | tf_op jit(solution)/shard_map/feed_hidden/pallas_call | solution.py:544
  148.2 8.4 %feed_hidden.4 = (bf16[1024,2048]{1,0:T(8,128)(2,1)}, bf16[1024,2048]{1,0:T(8,128)(2,1)}, bf16[256,1024]{1,0:T(8,128)(2,1)}) custom-call(bf16[256,1024]{1,0:T(8,128)(2,1)} %copy-done.72, bf16[256,1024]{1,0:T(8,128)(2,1)} %copy-done.66, bf16[1024,2048]{1,0:T(8,128)(2,1)} %up_ref.5, ...), custom_call_target="tpu_custom_call", output_to_operand_aliasing={{0}: (4, {}), {1}: (5, {})} | custom-call | flops 1000000 | bytes 100000 | tf_op jit(solution)/shard_map/feed_hidden/pallas_call | solution.py:544
  157.7 8.7 %feed_hidden.5 = (bf16[1024,2048]{1,0:T(8,128)(2,1)}, bf16[1024,2048]{1,0:T(8,128)(2,1)}, bf16[256,1024]{1,0:T(8,128)(2,1)}) custom-call(bf16[256,1024]{1,0:T(8,128)(2,1)} %collective-permute-done.6.rows_ref, bf16[256,1024]{1,0:T(8,128)(2,1)} %copy-done.68, bf16[1024,2048]{1,0:T(8,128)(2,1)} %up_ref.5, ...), custom_call_target="tpu_custom_call", output_to_operand_aliasing={{0}: (4, {}), {1}: (5, {})} | custom-call | flops 1000000 | bytes 100000 | tf_op jit(solution)/shard_map/feed_hidden/pallas_call | solution.py:544
  169.0 4.6 fusion.40
  173.6 3.4 fusion.37
  181.5 5.2 convolution_convert_fusion.1
  189.2 3.2 fusion.3
  199.6 2.9 fusion.2
  209.6 6.6 %self_backward.1 = bf16[512,3072]{1,0:T(8,128)(2,1)} custom-call(bf16[512,3072]{1,0:T(8,128)(2,1)} %convolution_convert_fusion.rows_ref, bf16[512,1024]{1,0:T(8,128)(2,1)} %convolution_convert_fusion.4.grad_ref, f32[4,8,128]{2,1,0:T(8,128)} %get-tuple-element.176.log_ref), custom_call_target="tpu_custom_call" | custom-call | flops 1000000 | bytes 100000 | tf_op jit(solution)/shard_map/self_backward/pallas_call | solution.py:493
  216.2 8.3 %multiply_reduce_fusion.1 = (f32[1024]{0:T(1024)S(1)}, f32[512]{0:T(512)S(1)}, f32[512]{0:T(512)S(1)}, f32[512,1024]{1,0:T(8,128)S(1)}) fusion(f32[512,1024]{1,0:T(8,128)} %copy-done.4, f32[512]{0:T(512)S(1)} %add_rsqrt_fusion.1, f32[512]{0:T(512)S(1)} %broadcast_multiply_fusion.7, f32[1024]{0:T(1024)S(1)} %copy-done.84, ...), kind=kOutput, calls=%fused_computation.83 | convolution fusion | flops 3225417728 | bytes 13647872 | tf_op jit(solution)/shard_map/dot_general | solution.py:28
  242.7 2.8 collective-permute-start.17
  249.6 2.7 constant_dynamic-slice_fusion.9
  255.2 11.4 %cross_backward.2 = (bf16[512,512]{1,0:T(8,128)(2,1)}, f32[1024,512]{1,0:T(8,128)}, f32[1024,512]{1,0:T(8,128)}) custom-call(f32[1024,128]{1,0:T(8,128)} %multiplicity.1.counts_ref.refs_0_, bf16[512,512]{1,0:T(8,128)(2,1)} %convolution_convert_fusion.22.query_ref.refs_1_, bf16[512,512]{1,0:T(8,128)(2,1)} %convolution_convert_fusion.20.refs_2_, ...), custom_call_target="tpu_custom_call" | custom-call | flops 1000000 | bytes 100000 | tf_op jit(solution)/shard_map/cross_backward/pallas_call | solution.py:376
  277.0 12.5 %cross_backward.3 = (bf16[512,512]{1,0:T(8,128)(2,1)}, bf16[1024,512]{1,0:T(8,128)(2,1)}, bf16[1024,512]{1,0:T(8,128)(2,1)}) custom-call(f32[1024,128]{1,0:T(8,128)} %multiplicity.1.counts_ref.refs_0_, bf16[512,512]{1,0:T(8,128)(2,1)} %convolution_convert_fusion.21.query_ref.refs_1_, bf16[512,512]{1,0:T(8,128)(2,1)} %convolution_convert_fusion.19.refs_2_, ...), custom_call_target="tpu_custom_call" | custom-call | flops 1000000 | bytes 100000 | tf_op jit(solution)/shard_map/cross_backward/pallas_call | solution.py:376
  295.5 3.0 convolution_convert_fusion.2
  300.6 2.9 convolution_convert_fusion.3
  307.7 21.8 %collective-permute-done.19 = bf16[2,2,256,512]{3,2,1,0:T(8,128)(2,1)S(1)} collective-permute-done((bf16[2,2,256,512]{3,2,1,0:T(8,128)(2,1)S(1)}, bf16[2,2,256,512]{3,2,1,0:T(8,128)(2,1)S(1)}, u32[]{:S(2)}, u32[]{:S(2)}) %collective-permute-start.19) | collective-permute-done | bytes 1048608 | tf_op jit(solution)/shard_map/ppermute | solution.py:83
  346.4 4.9 fusion.119
  352.6 10.7 %collective-permute-done.27 = bf16[2,2,128,512]{3,2,1,0:T(8,128)(2,1)S(1)} collective-permute-done((bf16[2,2,128,512]{3,2,1,0:T(8,128)(2,1)S(1)}, bf16[2,2,128,512]{3,2,1,0:T(8,128)(2,1)S(1)}, u32[]{:S(2)}, u32[]{:S(2)}) %collective-permute-start.27) | collective-permute-done | bytes 524320 | tf_op jit(solution)/shard_map/ppermute | solution.py:83
  367.3 7.1 %collective-permute-done.31 = bf16[2,256,512]{2,1,0:T(8,128)(2,1)S(1)} collective-permute-done((bf16[2,256,512]{2,1,0:T(8,128)(2,1)S(1)}, bf16[2,256,512]{2,1,0:T(8,128)(2,1)S(1)}, u32[]{:S(2)}, u32[]{:S(2)}) %collective-permute-start.31) | collective-permute-done | bytes 524320 | tf_op jit(solution)/shard_map/ppermute | solution.py:83
  376.1 20.8 %collective-permute-done.28 = bf16[2,128,512]{2,1,0:T(8,128)(2,1)S(1)} collective-permute-done((bf16[2,128,512]{2,1,0:T(8,128)(2,1)S(1)}, bf16[2,128,512]{2,1,0:T(8,128)(2,1)S(1)}, u32[]{:S(2)}, u32[]{:S(2)}) %collective-permute-start.28) | collective-permute-done | bytes 262176 | tf_op jit(solution)/shard_map/ppermute | solution.py:83
  397.5 7.6 %collective-permute-done.36 = bf16[2,128,512]{2,1,0:T(8,128)(2,1)S(1)} collective-permute-done((bf16[2,128,512]{2,1,0:T(8,128)(2,1)S(1)}, bf16[2,128,512]{2,1,0:T(8,128)(2,1)S(1)}, u32[]{:S(2)}, u32[]{:S(2)}) %collective-permute-start.36) | collective-permute-done | bytes 262176 | tf_op jit(solution)/shard_map/ppermute | solution.py:83
  412.6 11.8 %collective-permute-done.35 = bf16[2,128,512]{2,1,0:T(8,128)(2,1)S(1)} collective-permute-done((bf16[2,128,512]{2,1,0:T(8,128)(2,1)S(1)}, bf16[2,128,512]{2,1,0:T(8,128)(2,1)S(1)}, u32[]{:S(2)}, u32[]{:S(2)}) %collective-permute-start.35) | collective-permute-done | bytes 262176 | tf_op jit(solution)/shard_map/ppermute | solution.py:83
  433.0 3.4 multiply_reduce_fusion
  443.2 3.4 copy-done.9
  448.8 4.7 bitcast_convert_fusion
  453.5 4.4 maximum_convert_fusion
  463.1 3.2 convert_add_fusion.12
  466.2 12.1 %collective-permute-done.46 = bf16[2,128,512]{2,1,0:T(8,128)(2,1)S(1)} collective-permute-done((bf16[2,128,512]{2,1,0:T(8,128)(2,1)S(1)}, bf16[2,128,512]{2,1,0:T(8,128)(2,1)S(1)}, u32[]{:S(2)}, u32[]{:S(2)}) %collective-permute-start.46) | collective-permute-done | bytes 262176 | tf_op jit(solution)/shard_map/ppermute | solution.py:83
  479.3 7.0 %collective-permute-done.45 = bf16[2,128,512]{2,1,0:T(8,128)(2,1)S(1)} collective-permute-done((bf16[2,128,512]{2,1,0:T(8,128)(2,1)S(1)}, bf16[2,128,512]{2,1,0:T(8,128)(2,1)S(1)}, u32[]{:S(2)}, u32[]{:S(2)}) %collective-permute-start.45) | collective-permute-done | bytes 262176 | tf_op jit(solution)/shard_map/ppermute | solution.py:83
  488.7 12.6 %collective-permute-done.44 = f32[4,1024]{1,0:T(4,128)S(1)} collective-permute-done((f32[4,1024]{1,0:T(4,128)S(1)}, f32[4,1024]{1,0:T(4,128)S(1)}, u32[]{:S(2)}, u32[]{:S(2)}) %collective-permute-start.44) | collective-permute-done | bytes 16416 | tf_op jit(solution)/shard_map/ppermute | solution.py:934
  505.7 4.8 fusion.59
  (450 shorter events, 197.4 us)
Async XLA Ops:
  7.2 88.9 %all-gather.4.cloned.1.call-start = ((), (), s32[]{:S(2)}) async-start(), calls=%async_computation | async-start | bytes 4456448 | tf_op jit(solution)/shard_map/all_gather | solution.py:644
  7.2 27.3 %collective-permute-start = (bf16[512,1024]{1,0:T(8,128)(2,1)}, bf16[512,1024]{1,0:T(8,128)(2,1)}, u32[]{:S(2)}, u32[]{:S(2)}) collective-permute-start(bf16[512,1024]{1,0:T(8,128)(2,1)} %param.20), channel_id=1, source_target_pairs={{0,1},{1,0},{2,3},{3,2},{4,5},{5,4},{6,7},{7,6},{8,9},{9,8},{10,11... | collective-permute-start | bytes 3145736 | tf_op jit(solution)/shard_map/ppermute | solution.py:58
  12.8 26.6 %collective-permute-start.4 = (bf16[4,64,512]{2,1,0:T(8,128)(2,1)S(1)}, bf16[4,64,512]{2,1,0:T(8,128)(2,1)}, u32[]{:S(2)}, u32[]{:S(2)}) collective-permute-start(bf16[4,64,512]{2,1,0:T(8,128)(2,1)S(1)} %fusion.88), channel_id=1, source_target_pairs={{0,1},{1,0},{2,3},{3,2},{4,5},{5,4},{6,7},{7,6},{8,9},{9,8},{10,11... | collective-permute-start | bytes 786440 | tf_op jit(solution)/shard_map/ppermute | solution.py:58
  39.4 403.8 %all-gather.6.cloned.1.call-start = ((), (), s32[]{:S(2)}) async-start(), calls=%async_computation.1 | async-start | bytes 8912896 | tf_op jit(solution)/shard_map/all_gather | solution.py:844
  42.4 24.7 %collective-permute-start.1 = (bf16[512,1024]{1,0:T(8,128)(2,1)}, bf16[512,1024]{1,0:T(8,128)(2,1)}, u32[]{:S(2)}, u32[]{:S(2)}) collective-permute-start(bf16[512,1024]{1,0:T(8,128)(2,1)} %fusion.10), channel_id=1, source_target_pairs={{0,1},{1,0},{2,3},{3,2},{4,5},{5,4},{6,7},{7,6},{8,9},{9,8},{10,11... | collective-permute-start | bytes 3145736 | tf_op jit(solution)/shard_map/ppermute | solution.py:58
  70.5 15.8 %collective-permute-start.2 = (bf16[256,1024]{1,0:T(8,128)(2,1)}, bf16[256,1024]{1,0:T(8,128)(2,1)S(1)}, u32[]{:S(2)}, u32[]{:S(2)}) collective-permute-start(bf16[256,1024]{1,0:T(8,128)(2,1)} %get-tuple-element.142), channel_id=1, source_target_pairs={{0,1},{1,0},{2,3},{3,2},{4,5},{5,4},{6,7},{7,6},{8,9},{9,8},{10,11... | collective-permute-start | bytes 1572872 | tf_op jit(solution)/shard_map/ppermute | solution.py:58
  85.8 22.6 %collective-permute-start.3 = (bf16[512,1024]{1,0:T(8,128)(2,1)}, bf16[512,1024]{1,0:T(8,128)(2,1)}, u32[]{:S(2)}, u32[]{:S(2)}) collective-permute-start(bf16[512,1024]{1,0:T(8,128)(2,1)} %convolution_convert_fusion.18), channel_id=1, source_target_pairs={{0,1},{1,0},{2,3},{3,2},{4,5},{5,4},{6,7},{7,6},{8,9},{9,8},{10,11... | collective-permute-start | bytes 3145736 | tf_op jit(solution)/shard_map/ppermute | solution.py:63
  112.3 12.3 %collective-permute-start.5 = (bf16[256,1024]{1,0:T(8,128)(2,1)S(1)}, bf16[256,1024]{1,0:T(8,128)(2,1)S(1)}, u32[]{:S(2)}, u32[]{:S(2)}) collective-permute-start(bf16[256,1024]{1,0:T(8,128)(2,1)S(1)} %copy-done.75), channel_id=1, source_target_pairs={{0,1},{1,0},{2,3},{3,2},{4,5},{5,4},{6,7},{7,6},{8,9},{9,8},{10,11... | collective-permute-start | bytes 1572872 | tf_op jit(solution)/shard_map/ppermute | solution.py:58
  132.3 15.1 %collective-permute-start.7 = (bf16[256,1024]{1,0:T(8,128)(2,1)}, bf16[256,1024]{1,0:T(8,128)(2,1)S(1)}, u32[]{:S(2)}, u32[]{:S(2)}) collective-permute-start(bf16[256,1024]{1,0:T(8,128)(2,1)} %get-tuple-element.315), channel_id=1, source_target_pairs={{0,1},{1,0},{2,3},{3,2},{4,5},{5,4},{6,7},{7,6},{8,9},{9,8},{10,11... | collective-permute-start | bytes 1572872 | tf_op jit(solution)/shard_map/ppermute | solution.py:58
  133.4 24.4 %collective-permute-start.6 = (bf16[256,1024]{1,0:T(8,128)(2,1)}, bf16[256,1024]{1,0:T(8,128)(2,1)}, u32[]{:S(2)}, u32[]{:S(2)}) collective-permute-start(bf16[256,1024]{1,0:T(8,128)(2,1)} %get-tuple-element.316), channel_id=1, source_target_pairs={{0,1},{1,0},{2,3},{3,2},{4,5},{5,4},{6,7},{7,6},{8,9},{9,8},{10,11... | collective-permute-start | bytes 1572872 | tf_op jit(solution)/shard_map/ppermute | solution.py:58
  156.6 12.4 %collective-permute-start.8 = (bf16[256,1024]{1,0:T(8,128)(2,1)}, bf16[256,1024]{1,0:T(8,128)(2,1)}, u32[]{:S(2)}, u32[]{:S(2)}) collective-permute-start(bf16[256,1024]{1,0:T(8,128)(2,1)} %get-tuple-element.160), channel_id=1, source_target_pairs={{0,1},{1,0},{2,3},{3,2},{4,5},{5,4},{6,7},{7,6},{8,9},{9,8},{10,11... | collective-permute-start | bytes 1572872 | tf_op jit(solution)/shard_map/ppermute | solution.py:63
  166.4 13.2 %collective-permute-start.10 = (bf16[256,1024]{1,0:T(8,128)(2,1)}, bf16[256,1024]{1,0:T(8,128)(2,1)S(1)}, u32[]{:S(2)}, u32[]{:S(2)}) collective-permute-start(bf16[256,1024]{1,0:T(8,128)(2,1)} %get-tuple-element.167), channel_id=1, source_target_pairs={{0,1},{1,0},{2,3},{3,2},{4,5},{5,4},{6,7},{7,6},{8,9},{9,8},{10,11... | collective-permute-start | bytes 1572872 | tf_op jit(solution)/shard_map/ppermute | solution.py:63
  179.6 9.6 %collective-permute-start.9 = (bf16[2,512,1024]{2,1,0:T(8,128)(2,1)}, bf16[2,512,1024]{2,1,0:T(8,128)(2,1)}, u32[]{:S(2)}, u32[]{:S(2)}) collective-permute-start(bf16[2,512,1024]{2,1,0:T(8,128)(2,1)} %bitcast.16), channel_id=1, source_target_pairs={{0,2},{2,0},{4,6},{6,4},{8,10},{10,8},{12,14},{14,12},{16,18},{18,... | collective-permute-start | bytes 6291464 | tf_op jit(solution)/shard_map/ppermute | solution.py:83
  189.2 10.4 %collective-permute-start.11 = (bf16[2,512,1024]{2,1,0:T(8,128)(2,1)}, bf16[2,512,1024]{2,1,0:T(8,128)(2,1)}, u32[]{:S(2)}, u32[]{:S(2)}) collective-permute-start(bf16[2,512,1024]{2,1,0:T(8,128)(2,1)} %bitcast.18), channel_id=1, source_target_pairs={{0,2},{2,0},{4,6},{6,4},{8,10},{10,8},{12,14},{14,12},{16,18},{18,... | collective-permute-start | bytes 6291464 | tf_op jit(solution)/shard_map/ppermute | solution.py:83
  194.1 37.1 %collective-permute-start.13 = (bf16[2,256,1024]{2,1,0:T(8,128)(2,1)}, bf16[2,256,1024]{2,1,0:T(8,128)(2,1)}, u32[]{:S(2)}, u32[]{:S(2)}) collective-permute-start(bf16[2,256,1024]{2,1,0:T(8,128)(2,1)} %bitcast.20), channel_id=1, source_target_pairs={{0,4},{2,6},{4,0},{6,2},{8,12},{10,14},{12,8},{14,10},{16,20},{18,... | collective-permute-start | bytes 3145736 | tf_op jit(solution)/shard_map/ppermute | solution.py:83
  204.2 30.9 %collective-permute-start.12 = (bf16[2,256,1024]{2,1,0:T(8,128)(2,1)}, bf16[2,256,1024]{2,1,0:T(8,128)(2,1)}, u32[]{:S(2)}, u32[]{:S(2)}) collective-permute-start(bf16[2,256,1024]{2,1,0:T(8,128)(2,1)} %bitcast.23), channel_id=1, source_target_pairs={{0,8},{2,10},{4,12},{6,14},{8,0},{10,2},{12,4},{14,6},{16,24},{18,... | collective-permute-start | bytes 3145736 | tf_op jit(solution)/shard_map/ppermute | solution.py:83
  228.4 25.8 %collective-permute-start.14 = (bf16[512,1024]{1,0:T(8,128)(2,1)S(1)}, bf16[512,1024]{1,0:T(8,128)(2,1)S(1)}, u32[]{:S(2)}, u32[]{:S(2)}) collective-permute-start(bf16[512,1024]{1,0:T(8,128)(2,1)S(1)} %get-tuple-element.204), channel_id=1, source_target_pairs={{0,1},{1,0},{2,3},{3,2},{4,5},{5,4},{6,7},{7,6},{8,9},{9,8},{10,11... | collective-permute-start | bytes 3145736 | tf_op jit(solution)/shard_map/ppermute | solution.py:58
  242.3 25.0 %collective-permute-start.18 = (bf16[2,128,1024]{2,1,0:T(8,128)(2,1)}, bf16[2,128,1024]{2,1,0:T(8,128)(2,1)S(1)}, u32[]{:S(2)}, u32[]{:S(2)}) collective-permute-start(bf16[2,128,1024]{2,1,0:T(8,128)(2,1)} %bitcast.27), channel_id=1, source_target_pairs={{0,8},{2,10},{4,12},{6,14},{8,0},{10,2},{12,4},{14,6},{16,24},{18,... | collective-permute-start | bytes 1572872 | tf_op jit(solution)/shard_map/ppermute | solution.py:83
  242.7 28.9 %collective-permute-start.17 = (bf16[2,128,1024]{2,1,0:T(8,128)(2,1)}, bf16[2,128,1024]{2,1,0:T(8,128)(2,1)}, u32[]{:S(2)}, u32[]{:S(2)}) collective-permute-start(bf16[2,128,1024]{2,1,0:T(8,128)(2,1)} %dynamic-slice_bitcast_fusion.2), channel_id=1, source_target_pairs={{0,16},{2,18},{4,20},{6,22},{8,24},{10,26},{12,28},{14,30},{16,0},... | collective-permute-start | bytes 1572872 | tf_op jit(solution)/shard_map/ppermute | solution.py:83
  269.7 19.9 %collective-permute-start.21 = (bf16[2,64,1024]{2,1,0:T(8,128)(2,1)S(1)}, bf16[2,64,1024]{2,1,0:T(8,128)(2,1)}, u32[]{:S(2)}, u32[]{:S(2)}) collective-permute-start(bf16[2,64,1024]{2,1,0:T(8,128)(2,1)S(1)} %dynamic-slice_bitcast_fusion.7), channel_id=1, source_target_pairs={{0,16},{2,18},{4,20},{6,22},{8,24},{10,26},{12,28},{14,30},{16,0},... | collective-permute-start | bytes 786440 | tf_op jit(solution)/shard_map/ppermute | solution.py:83
  274.4 16.2 %collective-permute-start.20 = (bf16[2,64,1024]{2,1,0:T(8,128)(2,1)}, bf16[2,64,1024]{2,1,0:T(8,128)(2,1)}, u32[]{:S(2)}, u32[]{:S(2)}) collective-permute-start(bf16[2,64,1024]{2,1,0:T(8,128)(2,1)} %dynamic-slice_bitcast_fusion.6), channel_id=1, source_target_pairs={{0,4},{2,6},{4,0},{6,2},{8,12},{10,14},{12,8},{14,10},{16,20},{18,... | collective-permute-start | bytes 786440 | tf_op jit(solution)/shard_map/ppermute | solution.py:83
  292.6 211.8 %all-gather.8.cloned.1.call-start = ((), (), s32[]{:S(2)}) async-start(), calls=%async_computation.2 | async-start | bytes 4456448 | tf_op jit(solution)/shard_map/all_gather | solution.py:905
  292.9 10.9 %collective-permute-start.15 = (bf16[2,2,512,512]{3,2,1,0:T(8,128)(2,1)}, bf16[2,2,512,512]{3,2,1,0:T(8,128)(2,1)S(1)}, u32[]{:S(2)}, u32[]{:S(2)}) collective-permute-start(bf16[2,2,512,512]{3,2,1,0:T(8,128)(2,1)} %bitcast.357), channel_id=1, source_target_pairs={{0,2},{2,0},{4,6},{6,4},{8,10},{10,8},{12,14},{14,12},{16,18},{18,... | collective-permute-start | bytes 6291464 | tf_op jit(solution)/shard_map/ppermute | solution.py:83
  299.5 30.0 %collective-permute-start.19 = (bf16[2,2,256,512]{3,2,1,0:T(8,128)(2,1)S(1)}, bf16[2,2,256,512]{3,2,1,0:T(8,128)(2,1)S(1)}, u32[]{:S(2)}, u32[]{:S(2)}) collective-permute-start(bf16[2,2,256,512]{3,2,1,0:T(8,128)(2,1)S(1)} %bitcast.372), channel_id=1, source_target_pairs={{0,4},{2,6},{4,0},{6,2},{8,12},{10,14},{12,8},{14,10},{16,20},{18,... | collective-permute-start | bytes 3145736 | tf_op jit(solution)/shard_map/ppermute | solution.py:83
  303.6 36.9 %collective-permute-start.23 = (bf16[2,512,512]{2,1,0:T(8,128)(2,1)S(1)}, bf16[2,512,512]{2,1,0:T(8,128)(2,1)S(1)}, u32[]{:S(2)}, u32[]{:S(2)}) collective-permute-start(bf16[2,512,512]{2,1,0:T(8,128)(2,1)S(1)} %fusion.58), channel_id=1, source_target_pairs={{0,2},{2,0},{4,6},{6,4},{8,10},{10,8},{12,14},{14,12},{16,18},{18,... | collective-permute-start | bytes 3145736 | tf_op jit(solution)/shard_map/ppermute | solution.py:83
  305.8 33.4 %collective-permute-start.24 = (bf16[2,512,512]{2,1,0:T(8,128)(2,1)S(1)}, bf16[2,512,512]{2,1,0:T(8,128)(2,1)S(1)}, u32[]{:S(2)}, u32[]{:S(2)}) collective-permute-start(bf16[2,512,512]{2,1,0:T(8,128)(2,1)S(1)} %slice_bitcast_fusion.12), channel_id=1, source_target_pairs={{0,1},{1,0},{2,3},{3,2},{4,5},{5,4},{6,7},{7,6},{8,9},{9,8},{10,11... | collective-permute-start | bytes 3145736 | tf_op jit(solution)/shard_map/ppermute | solution.py:63
  338.0 25.3 %collective-permute-start.27 = (bf16[2,2,128,512]{3,2,1,0:T(8,128)(2,1)S(1)}, bf16[2,2,128,512]{3,2,1,0:T(8,128)(2,1)S(1)}, u32[]{:S(2)}, u32[]{:S(2)}) collective-permute-start(bf16[2,2,128,512]{3,2,1,0:T(8,128)(2,1)S(1)} %bitcast.379), channel_id=1, source_target_pairs={{0,8},{2,10},{4,12},{6,14},{8,0},{10,2},{12,4},{14,6},{16,24},{18,... | collective-permute-start | bytes 1572872 | tf_op jit(solution)/shard_map/ppermute | solution.py:83
  339.7 25.3 %collective-permute-start.26 = (bf16[2,256,512]{2,1,0:T(8,128)(2,1)S(1)}, bf16[2,256,512]{2,1,0:T(8,128)(2,1)S(1)}, u32[]{:S(2)}, u32[]{:S(2)}) collective-permute-start(bf16[2,256,512]{2,1,0:T(8,128)(2,1)S(1)} %bitcast.380), channel_id=1, source_target_pairs={{0,4},{2,6},{4,0},{6,2},{8,12},{10,14},{12,8},{14,10},{16,20},{18,... | collective-permute-start | bytes 1572872 | tf_op jit(solution)/shard_map/ppermute | solution.py:83
  340.9 33.6 %collective-permute-start.31 = (bf16[2,256,512]{2,1,0:T(8,128)(2,1)S(1)}, bf16[2,256,512]{2,1,0:T(8,128)(2,1)S(1)}, u32[]{:S(2)}, u32[]{:S(2)}) collective-permute-start(bf16[2,256,512]{2,1,0:T(8,128)(2,1)S(1)} %dynamic-slice_bitcast_fusion.1), channel_id=1, source_target_pairs={{0,4},{2,6},{4,0},{6,2},{8,12},{10,14},{12,8},{14,10},{16,20},{18,... | collective-permute-start | bytes 1572872 | tf_op jit(solution)/shard_map/ppermute | solution.py:83
  342.6 65.1 %collective-permute-start.30 = (bf16[2,256,512]{2,1,0:T(8,128)(2,1)S(1)}, bf16[2,256,512]{2,1,0:T(8,128)(2,1)S(1)}, u32[]{:S(2)}, u32[]{:S(2)}) collective-permute-start(bf16[2,256,512]{2,1,0:T(8,128)(2,1)S(1)} %dynamic-slice_bitcast_fusion), channel_id=1, source_target_pairs={{0,8},{2,10},{4,12},{6,14},{8,0},{10,2},{12,4},{14,6},{16,24},{18,... | collective-permute-start | bytes 1572872 | tf_op jit(solution)/shard_map/ppermute | solution.py:83
  344.1 81.2 %collective-permute-start.34 = (bf16[512,1024]{1,0:T(8,128)(2,1)S(1)}, bf16[512,1024]{1,0:T(8,128)(2,1)S(1)}, u32[]{:S(2)}, u32[]{:S(2)}) collective-permute-start(bf16[512,1024]{1,0:T(8,128)(2,1)S(1)} %convolution_convert_fusion.9), channel_id=1, source_target_pairs={{0,1},{1,0},{2,3},{3,2},{4,5},{5,4},{6,7},{7,6},{8,9},{9,8},{10,11... | collective-permute-start | bytes 3145736 | tf_op jit(solution)/shard_map/ppermute | solution.py:63
  363.3 69.7 %collective-permute-start.25 = (bf16[512,1024]{1,0:T(8,128)(2,1)}, bf16[512,1024]{1,0:T(8,128)(2,1)}, u32[]{:S(2)}, u32[]{:S(2)}) collective-permute-start(bf16[512,1024]{1,0:T(8,128)(2,1)} %slice.414), channel_id=1, source_target_pairs={{0,1},{1,0},{2,3},{3,2},{4,5},{5,4},{6,7},{7,6},{8,9},{9,8},{10,11... | collective-permute-start | bytes 3145736 | tf_op jit(solution)/shard_map/ppermute | solution.py:63
  365.0 46.0 %collective-permute-start.29 = (bf16[2,2,64,512]{3,2,1,0:T(8,128)(2,1)S(1)}, bf16[2,2,64,512]{3,2,1,0:T(8,128)(2,1)S(1)}, u32[]{:S(2)}, u32[]{:S(2)}) collective-permute-start(bf16[2,2,64,512]{3,2,1,0:T(8,128)(2,1)S(1)} %dynamic-slice_bitcast_fusion.5), channel_id=1, source_target_pairs={{0,16},{2,18},{4,20},{6,22},{8,24},{10,26},{12,28},{14,30},{16,0},... | collective-permute-start | bytes 786440 | tf_op jit(solution)/shard_map/ppermute | solution.py:83
  374.5 22.5 %collective-permute-start.28 = (bf16[2,128,512]{2,1,0:T(8,128)(2,1)S(1)}, bf16[2,128,512]{2,1,0:T(8,128)(2,1)S(1)}, u32[]{:S(2)}, u32[]{:S(2)}) collective-permute-start(bf16[2,128,512]{2,1,0:T(8,128)(2,1)S(1)} %bitcast.381), channel_id=1, source_target_pairs={{0,8},{2,10},{4,12},{6,14},{8,0},{10,2},{12,4},{14,6},{16,24},{18,... | collective-permute-start | bytes 786440 | tf_op jit(solution)/shard_map/ppermute | solution.py:83
  405.2 23.9 %collective-permute-start.32 = (bf16[2,64,512]{2,1,0:T(8,128)(2,1)S(1)}, bf16[2,64,512]{2,1,0:T(8,128)(2,1)S(1)}, u32[]{:S(2)}, u32[]{:S(2)}) collective-permute-start(bf16[2,64,512]{2,1,0:T(8,128)(2,1)S(1)} %dynamic-slice_bitcast_fusion.10), channel_id=1, source_target_pairs={{0,16},{2,18},{4,20},{6,22},{8,24},{10,26},{12,28},{14,30},{16,0},... | collective-permute-start | bytes 393224 | tf_op jit(solution)/shard_map/ppermute | solution.py:83
  407.9 16.6 %collective-permute-start.35 = (bf16[2,128,512]{2,1,0:T(8,128)(2,1)S(1)}, bf16[2,128,512]{2,1,0:T(8,128)(2,1)S(1)}, u32[]{:S(2)}, u32[]{:S(2)}) collective-permute-start(bf16[2,128,512]{2,1,0:T(8,128)(2,1)S(1)} %dynamic-slice_bitcast_fusion.3), channel_id=1, source_target_pairs={{0,16},{2,18},{4,20},{6,22},{8,24},{10,26},{12,28},{14,30},{16,0},... | collective-permute-start | bytes 786440 | tf_op jit(solution)/shard_map/ppermute | solution.py:83
  411.1 17.9 %collective-permute-start.33 = (bf16[2,64,512]{2,1,0:T(8,128)(2,1)S(1)}, bf16[2,64,512]{2,1,0:T(8,128)(2,1)S(1)}, u32[]{:S(2)}, u32[]{:S(2)}) collective-permute-start(bf16[2,64,512]{2,1,0:T(8,128)(2,1)S(1)} %slice_bitcast_fusion.11), channel_id=1, source_target_pairs={{0,1},{1,0},{2,3},{3,2},{4,5},{5,4},{6,7},{7,6},{8,9},{9,8},{10,11... | collective-permute-start | bytes 393224 | tf_op jit(solution)/shard_map/ppermute | solution.py:63
  429.9 31.6 %collective-permute-start.43 = (bf16[512,1024]{1,0:T(8,128)(2,1)}, bf16[512,1024]{1,0:T(8,128)(2,1)}, u32[]{:S(2)}, u32[]{:S(2)}) collective-permute-start(bf16[512,1024]{1,0:T(8,128)(2,1)} %add_convert_fusion), channel_id=1, source_target_pairs={{0,1},{1,0},{2,3},{3,2},{4,5},{5,4},{6,7},{7,6},{8,9},{9,8},{10,11... | collective-permute-start | bytes 3145736 | tf_op jit(solution)/shard_map/ppermute | solution.py:63
  438.2 19.8 %collective-permute-start.42 = (bf16[2,64,512]{2,1,0:T(8,128)(2,1)S(1)}, bf16[2,64,512]{2,1,0:T(8,128)(2,1)S(1)}, u32[]{:S(2)}, u32[]{:S(2)}) collective-permute-start(bf16[2,64,512]{2,1,0:T(8,128)(2,1)S(1)} %fusion.89), channel_id=1, source_target_pairs={{0,16},{2,18},{4,20},{6,22},{8,24},{10,26},{12,28},{14,30},{16,0},... | collective-permute-start | bytes 393224 | tf_op jit(solution)/shard_map/ppermute | solution.py:83
  441.0 18.8 %collective-permute-start.41 = (bf16[2,64,512]{2,1,0:T(8,128)(2,1)S(1)}, bf16[2,64,512]{2,1,0:T(8,128)(2,1)S(1)}, u32[]{:S(2)}, u32[]{:S(2)}) collective-permute-start(bf16[2,64,512]{2,1,0:T(8,128)(2,1)S(1)} %fusion.90), channel_id=1, source_target_pairs={{0,4},{2,6},{4,0},{6,2},{8,12},{10,14},{12,8},{14,10},{16,20},{18,... | collective-permute-start | bytes 393224 | tf_op jit(solution)/shard_map/ppermute | solution.py:83
  442.2 19.3 %collective-permute-start.40 = (f32[4,1024]{1,0:T(4,128)S(1)}, f32[4,1024]{1,0:T(4,128)S(1)}, u32[]{:S(2)}, u32[]{:S(2)}) collective-permute-start(f32[4,1024]{1,0:T(4,128)S(1)} %fusion.101), channel_id=1, source_target_pairs={{0,4},{2,6},{4,0},{6,2},{8,12},{10,14},{12,8},{14,10},{16,20},{18,... | collective-permute-start | bytes 49160 | tf_op jit(solution)/shard_map/ppermute | solution.py:934
  458.0 20.4 %collective-permute-start.46 = (bf16[2,128,512]{2,1,0:T(8,128)(2,1)S(1)}, bf16[2,128,512]{2,1,0:T(8,128)(2,1)S(1)}, u32[]{:S(2)}, u32[]{:S(2)}) collective-permute-start(bf16[2,128,512]{2,1,0:T(8,128)(2,1)S(1)} %pad_maximum_fusion.12), channel_id=1, source_target_pairs={{0,8},{2,10},{4,12},{6,14},{8,0},{10,2},{12,4},{14,6},{16,24},{18,... | collective-permute-start | bytes 786440 | tf_op jit(solution)/shard_map/ppermute | solution.py:83
  459.9 26.4 %collective-permute-start.45 = (bf16[2,128,512]{2,1,0:T(8,128)(2,1)S(1)}, bf16[2,128,512]{2,1,0:T(8,128)(2,1)S(1)}, u32[]{:S(2)}, u32[]{:S(2)}) collective-permute-start(bf16[2,128,512]{2,1,0:T(8,128)(2,1)S(1)} %pad_maximum_fusion.13), channel_id=1, source_target_pairs={{0,16},{2,18},{4,20},{6,22},{8,24},{10,26},{12,28},{14,30},{16,0},... | collective-permute-start | bytes 786440 | tf_op jit(solution)/shard_map/ppermute | solution.py:83
  478.5 22.8 %collective-permute-start.49 = (bf16[2,256,512]{2,1,0:T(8,128)(2,1)S(1)}, bf16[2,256,512]{2,1,0:T(8,128)(2,1)S(1)}, u32[]{:S(2)}, u32[]{:S(2)}) collective-permute-start(bf16[2,256,512]{2,1,0:T(8,128)(2,1)S(1)} %pad_maximum_fusion.10), channel_id=1, source_target_pairs={{0,4},{2,6},{4,0},{6,2},{8,12},{10,14},{12,8},{14,10},{16,20},{18,... | collective-permute-start | bytes 1572872 | tf_op jit(solution)/shard_map/ppermute | solution.py:83
  486.4 16.2 %collective-permute-start.48 = (bf16[2,256,512]{2,1,0:T(8,128)(2,1)S(1)}, bf16[2,256,512]{2,1,0:T(8,128)(2,1)S(1)}, u32[]{:S(2)}, u32[]{:S(2)}) collective-permute-start(bf16[2,256,512]{2,1,0:T(8,128)(2,1)S(1)} %pad_maximum_fusion.11), channel_id=1, source_target_pairs={{0,8},{2,10},{4,12},{6,14},{8,0},{10,2},{12,4},{14,6},{16,24},{18,... | collective-permute-start | bytes 1572872 | tf_op jit(solution)/shard_map/ppermute | solution.py:83
  486.5 14.8 %collective-permute-start.44 = (f32[4,1024]{1,0:T(4,128)S(1)}, f32[4,1024]{1,0:T(4,128)S(1)}, u32[]{:S(2)}, u32[]{:S(2)}) collective-permute-start(f32[4,1024]{1,0:T(4,128)S(1)} %fusion.186), channel_id=1, source_target_pairs={{0,8},{2,10},{4,12},{6,14},{8,0},{10,2},{12,4},{14,6},{16,24},{18,... | collective-permute-start | bytes 49160 | tf_op jit(solution)/shard_map/ppermute | solution.py:934
  502.6 14.2 %collective-permute-start.52 = (bf16[2,512,512]{2,1,0:T(8,128)(2,1)}, bf16[2,512,512]{2,1,0:T(8,128)(2,1)}, u32[]{:S(2)}, u32[]{:S(2)}) collective-permute-start(bf16[2,512,512]{2,1,0:T(8,128)(2,1)} %pad_maximum_fusion.4), channel_id=1, source_target_pairs={{0,2},{2,0},{4,6},{6,4},{8,10},{10,8},{12,14},{14,12},{16,18},{18,... | collective-permute-start | bytes 3145736 | tf_op jit(solution)/shard_map/ppermute | solution.py:83
  503.9 12.9 %collective-permute-start.51 = (bf16[2,512,512]{2,1,0:T(8,128)(2,1)}, bf16[2,512,512]{2,1,0:T(8,128)(2,1)}, u32[]{:S(2)}, u32[]{:S(2)}) collective-permute-start(bf16[2,512,512]{2,1,0:T(8,128)(2,1)} %pad_maximum_fusion.5), channel_id=1, source_target_pairs={{0,2},{2,0},{4,6},{6,4},{8,10},{10,8},{12,14},{14,12},{16,18},{18,... | collective-permute-start | bytes 3145736 | tf_op jit(solution)/shard_map/ppermute | solution.py:83
  (98 other events, 460.8 us)
Sparse Core Ops, SparseCore 0:
  39.5 52.0 all-gather.3
  292.7 96.8 all-gather.5
  430.0 62.9 all-gather.7

commit v3 on v2

--- a/solution.py
+++ b/solution.py
@@ -150,10 +150,11 @@
             self.kept, sent = halves(self.block, bit, before)
             self.received = [swap_sets(sent, bit)]
         elif kind == "peers":
-            self.kept, sent = self.block[0], self.block[1:]
-            self.received = [
-                to_peer(sent[step], step + 1) for step in range(sent.shape[0])
-            ]
+            self.kept = self.block[0]
+            sent = [self.block[step] for step in range(1, self.block.shape[0])]
+            self.received = [to_peer(part, step + 1) for step, part in enumerate(sent)]
+            self.order.mark(*sent)
+            return
         else:
             self.kept = sent = self.block
             self.received = [swap_sets(sent, bit)]
@@ -248,11 +249,15 @@
 
 def cross_forward_kernel(
     counts_ref,
-    query_ref,
+    rows_ref,
     key_ref,
     value_t_ref,
+    query_weight_ref,
+    output_weight_ref,
+    query_ref,
     out_ref,
     log_ref,
+    branch_ref,
     bias_ref,
     *,
     heads,
@@ -261,6 +266,7 @@
     first_group,
 ):
     fill_bias(counts_ref, bias_ref, span, first_group)
+    query_ref[...] = project(rows_ref[...], query_weight_ref[...]).astype(jnp.bfloat16)
     for head in range(heads):
         cols = slice(head * HEAD_DIM, (head + 1) * HEAD_DIM)
         scores = times_transposed(key_ref[:, cols], query_ref[:, cols])
@@ -271,15 +277,28 @@
         mixed = project(value_t_ref[cols, :], raised.astype(jnp.bfloat16)) / total
         out_ref[:, cols] = mixed.T.astype(jnp.bfloat16)
         log_ref[0, head : head + 1, :] = top + jnp.log2(total)
-
-
-def cross_forward(log_counts, queries, key_table, value_table_t, scale, first_group):
-    row_count, width = queries.shape
-    table_rows = key_table.shape[0]
+    branch_ref[...] = project(out_ref[...], output_weight_ref[...]).astype(branch_ref.dtype)
+
+
+def cross_forward(
+    log_counts,
+    normed,
+    key_table,
+    value_table_t,
+    query_weight,
+    output_weight,
+    scale,
+    first_group,
+    branch_type,
+):
+    row_count, model = normed.shape
+    table_rows, width = key_table.shape
     heads = width // HEAD_DIM
     groups = row_count // GROUP
     span = 2 if groups % 2 == 0 else 1
     rows = span * GROUP
+    block = pl.BlockSpec((rows, width), lambda i: (i, 0))
+    wide_block = pl.BlockSpec((rows, model), lambda i: (i, 0))
     return pl.pallas_call(
         functools.partial(
             cross_forward_kernel, heads=heads, span=span, scale=scale, first_group=first_group
@@ -287,23 +306,24 @@
         grid=(groups // span,),
         in_specs=[
             pl.BlockSpec((table_rows, 128), lambda i: (0, 0)),
-            pl.BlockSpec((rows, width), lambda i: (i, 0)),
+            wide_block,
             pl.BlockSpec((table_rows, width), lambda i: (0, 0)),
             pl.BlockSpec((width, table_rows), lambda i: (0, 0)),
+            pl.BlockSpec((model, width), lambda i: (0, 0)),
+            pl.BlockSpec((width, model), lambda i: (0, 0)),
         ],
-        out_specs=[
-            pl.BlockSpec((rows, width), lambda i: (i, 0)),
-            pl.BlockSpec((1, heads, rows), lambda i: (i, 0, 0)),
-        ],
+        out_specs=[block, block, pl.BlockSpec((1, heads, rows), lambda i: (i, 0, 0)), wide_block],
         out_shape=[
             jax.ShapeDtypeStruct((row_count, width), jnp.bfloat16),
+            jax.ShapeDtypeStruct((row_count, width), jnp.bfloat16),
             jax.ShapeDtypeStruct((groups // span, heads, rows), jnp.float32),
+            jax.ShapeDtypeStruct((row_count, model), branch_type),
         ],
         scratch_shapes=[pltpu.VMEM((table_rows, rows), jnp.float32)],
         compiler_params=pltpu.CompilerParams(vmem_limit_bytes=vmem_bytes),
         cost_estimate=small_cost,
         name="cross_forward",
-    )(log_counts, queries, key_table, value_table_t)
+    )(log_counts, normed, key_table, value_table_t, query_weight, output_weight)
 
 
 def cross_backward_kernel(*refs, heads, span, scale, first_group, start, finish):
@@ -416,45 +436,114 @@
     ]
 
 
-def self_forward_kernel(rows_ref, out_ref, log_ref, *, heads, heads_block, scale):
+def norm_block(values, gain, average_ref, inverse_ref):
+    average = jnp.mean(values, axis=1, keepdims=True)
+    centred = values - average
+    variance = jnp.mean(centred * centred, axis=1, keepdims=True)
+    inverse = lax.rsqrt(variance + epsilon)
+    average_ref[...] = average
+    inverse_ref[...] = inverse
+    return (centred * inverse * gain).astype(jnp.bfloat16)
+
+
+def self_forward_kernel(
+    state_ref,
+    alive_ref,
+    self_gain_ref,
+    feed_gain_ref,
+    mixed_weight_ref,
+    output_weight_ref,
+    normed_ref,
+    rows_ref,
+    out_ref,
+    log_ref,
+    after_ref,
+    feed_ref,
+    self_average_ref,
+    self_inverse_ref,
+    feed_average_ref,
+    feed_inverse_ref,
+    *,
+    heads,
+    heads_block,
+    scale,
+):
+    normed_ref[...] = norm_block(
+        state_ref[...], self_gain_ref[...], self_average_ref, self_inverse_ref
+    )
+    rows_ref[...] = project(normed_ref[...], mixed_weight_ref[...]).astype(jnp.bfloat16)
     columns = [head_columns(head, heads_block) for head in range(heads)]
-    scores = [
-        times_transposed(rows_ref[:, key_cols], rows_ref[:, query_cols])
-        for query_cols, key_cols, _ in columns
-    ]
-    weights = []
-    for head in range(heads):
-        scaled = scores[head] * (scale * log2_e)
-        top = jnp.max(scaled, axis=0, keepdims=True)
-        raised = jnp.exp2(scaled - top)
-        total = jnp.sum(raised, axis=0, keepdims=True)
-        weights.append((raised * (1.0 / total)).astype(jnp.bfloat16))
-        log_ref[0, head : head + 1, :] = top + jnp.log2(total)
-    for head in range(heads):
-        mixed = transposed_times(weights[head], rows_ref[:, columns[head][2]])
-        out_ref[:, head * HEAD_DIM : (head + 1) * HEAD_DIM] = mixed.astype(jnp.bfloat16)
-
-
-def self_forward(mixed_rows, heads, heads_block, scale):
-    row_count, width = mixed_rows.shape
+    for group in range(state_ref.shape[0] // GROUP):
+        rows = slice(group * GROUP, (group + 1) * GROUP)
+        scores = [
+            times_transposed(rows_ref[rows, key_cols], rows_ref[rows, query_cols])
+            for query_cols, key_cols, _ in columns
+        ]
+        weights = []
+        for head in range(heads):
+            scaled = scores[head] * (scale * log2_e)
+            top = jnp.max(scaled, axis=0, keepdims=True)
+            raised = jnp.exp2(scaled - top)
+            total = jnp.sum(raised, axis=0, keepdims=True)
+            weights.append((raised * (1.0 / total)).astype(jnp.bfloat16))
+            log_ref[group, head : head + 1, :] = top + jnp.log2(total)
+        for head in range(heads):
+            mixed = transposed_times(weights[head], rows_ref[rows, columns[head][2]])
+            out_ref[rows, head * HEAD_DIM : (head + 1) * HEAD_DIM] = mixed.astype(jnp.bfloat16)
+    branch = project(out_ref[...], output_weight_ref[...])
+    after_ref[...] = state_ref[...] + alive_ref[...] * branch
+    feed_ref[...] = norm_block(
+        after_ref[...], feed_gain_ref[...], feed_average_ref, feed_inverse_ref
+    )
+
+
+def self_forward(
+    state_rows, alive_rows, self_gain, feed_gain, mixed_weight, output_weight, heads, heads_block, scale
+):
+    row_count, model = state_rows.shape
     groups = row_count // GROUP
+    span = 2 if groups % 2 == 0 else 1
+    rows = span * GROUP
+    mixed_width = mixed_weight.shape[1]
+
+    def block(width):
+        return pl.BlockSpec((rows, width), lambda i: (i, 0))
+
+    def whole(array):
+        return pl.BlockSpec(array.shape, lambda i: (0, 0))
+
+    def result(width, kind):
+        return jax.ShapeDtypeStruct((row_count, width), kind)
+
+    weights = (self_gain[None], feed_gain[None], mixed_weight, output_weight)
     return pl.pallas_call(
         functools.partial(
             self_forward_kernel, heads=heads, heads_block=heads_block, scale=scale
         ),
-        grid=(groups,),
-        in_specs=[pl.BlockSpec((GROUP, width), lambda i: (i, 0))],
+        grid=(groups // span,),
+        in_specs=[block(model), block(1)] + [whole(array) for array in weights],
         out_specs=[
-            pl.BlockSpec((GROUP, heads * HEAD_DIM), lambda i: (i, 0)),
-            pl.BlockSpec((1, heads, GROUP), lambda i: (i, 0, 0)),
-        ],
+            block(model),
+            block(mixed_width),
+            block(heads * HEAD_DIM),
+            pl.BlockSpec((span, heads, GROUP), lambda i: (i, 0, 0)),
+            block(model),
+            block(model),
+        ]
+        + [block(1)] * 4,
         out_shape=[
-            jax.ShapeDtypeStruct((row_count, heads * HEAD_DIM), jnp.bfloat16),
+            result(model, jnp.bfloat16),
+            result(mixed_width, jnp.bfloat16),
+            result(heads * HEAD_DIM, jnp.bfloat16),
             jax.ShapeDtypeStruct((groups, heads, GROUP), jnp.float32),
-        ],
+            result(model, jnp.float32),
+            result(model, jnp.bfloat16),
+        ]
+        + [result(1, jnp.float32)] * 4,
+        compiler_params=pltpu.CompilerParams(vmem_limit_bytes=vmem_bytes),
         cost_estimate=small_cost,
         name="self_forward",
-    )(mixed_rows)
+    )(state_rows, alive_rows, *weights)
 
 
 def self_backward_kernel(rows_ref, grad_ref, log_ref, out_ref, *, heads, heads_block, scale):
@@ -637,9 +726,11 @@
     order.mark(normed_cross)
     log_counts = log_multiplicity(order.hold(chosen), counts, table_rows)
     order.mark(log_counts)
-    embedded = jnp.concatenate(order.hold(tuple(peer_inputs)), axis=0)
+    peer_inputs = order.hold(tuple(peer_inputs))
+    order.mark(*peer_inputs)
+    rows_cross = gather_blocks(order.hold(normed_cross))
+    embedded = jnp.concatenate(peer_inputs, axis=0)
     order.mark(embedded)
-    rows_cross = gather_blocks(order.hold(normed_cross))
     peer_stacks = [
         lax.all_gather(part, "sets", axis=1, tiled=True) for part in order.hold(tuple(peer_slices))
     ]
@@ -649,28 +740,37 @@
     ).astype(jnp.bfloat16)
     order.mark(key_table, value_table_t)
     grad_pieces = [[] for _ in range(tp_count)]
-    queries_cross, attended_cross, logs_cross = [], [], []
+    queries_cross, attended_cross, logs_cross, cross_terms = [], [], [], []
     for step in range(tp_count):
-        queries = project(order.hold(rows_cross[step]), cross_query).astype(jnp.bfloat16)
-        order.mark(queries)
+        rows = order.hold(rows_cross[step])
+        order.mark(rows)
         if step == tp_count - 1:
             for peer in range(1, tp_count):
                 grad_pieces[peer].append(from_peer(order.hold(pieces(grad_own)[0]), peer))
-        attended, logs = cross_forward(
-            log_counts, order.hold(queries), key_table, value_table_t, scale, step * local_groups
+        queries, attended, logs, term = cross_forward(
+            log_counts,
+            rows,
+            key_table,
+            value_table_t,
+            cross_query,
+            cross_output,
+            scale,
+            step * local_groups,
+            jnp.bfloat16 if step else jnp.float32,
         )
-        order.mark(attended)
         queries_cross.append(queries)
         attended_cross.append(attended)
         logs_cross.append(logs)
-    cross_terms = []
-    for step in range(1, tp_count):
-        grad_pieces[step][0] = order.hold(grad_pieces[step][0])
-        term = project(attended_cross[step], cross_output).astype(jnp.bfloat16)
-        cross_terms.append(to_peer(term, step))
-        order.mark(term, grad_pieces[step][0])
-    branch = project(order.hold(attended_cross[0]), cross_output)
-    order.mark(branch)
+        if step == 0:
+            branch = term
+            order.mark(attended)
+        else:
+            cross_terms.append(to_peer(term, step))
+            order.mark(term)
+        if step == tp_count - 1:
+            for peer in range(1, tp_count):
+                grad_pieces[peer][0] = order.hold(grad_pieces[peer][0])
+            order.mark(term, *[parts[0] for parts in grad_pieces[1:]])
     key_table_t = lax.dot_general(
         cross_key, order.hold(embedded), (((0,), (1,)), ((), ())), preferred_element_type=jnp.float32
     ).astype(jnp.bfloat16)
@@ -695,19 +795,35 @@
     for piece in pieces(grad_own)[1:]:
         for step in range(1, tp_count):
             grad_pieces[step].append(from_peer(order.hold(piece), step))
-    unit_self, inverse_self, normed_self = norm_forward(after_cross, self_gain)
-    mixed_rows = project(normed_self, mixed_weight).astype(jnp.bfloat16)
-    attended_self, logs_self = self_forward(mixed_rows, heads, heads_block, scale)
-    order.mark(attended_self)
+    (
+        normed_self,
+        mixed_rows,
+        attended_self,
+        logs_self,
+        after_self,
+        normed_feed,
+        average_self,
+        inverse_self,
+        average_feed,
+        inverse_feed,
+    ) = self_forward(
+        after_cross,
+        alive_rows,
+        self_gain,
+        feed_gain,
+        mixed_weight,
+        output_weight,
+        heads,
+        heads_block,
+        scale,
+    )
+    order.mark(normed_feed)
     for step in range(1, tp_count):
         grad_pieces[step] = list(order.hold(tuple(grad_pieces[step])))
-    order.mark(attended_self, *[part for parts in grad_pieces for part in parts])
-    after_self = after_cross + alive_rows * project(order.hold(attended_self), output_weight)
-
-    unit_feed, inverse_feed, normed_feed = norm_forward(after_self, feed_gain)
-    order.mark(normed_feed)
+    order.mark(normed_feed, *[part for parts in grad_pieces for part in parts])
+
     feed_pieces = [[] for _ in range(tp_count)]
-    for piece in pieces(normed_feed):
+    for piece in pieces(order.hold(normed_feed)):
         for step in range(1, tp_count):
             feed_pieces[step].append(from_peer(piece, step))
     *filled_parts, grad_normed_feed = feed_block(
@@ -751,33 +867,35 @@
         order.mark(*terms)
         if place == 0:
             held = order.hold(grad_hidden)
-            grad_up = jnp.stack(
-                [
-                    transposed_times(feed_all, held[:, start : start + feed_width])
-                    for start in range(0, hidden_width, feed_width)
-                ]
-            )
-            up_sum = SetSum(order, grad_up, bits, layout=natural, double=False)
+            grad_up = [
+                transposed_times(feed_all, held[:, start : start + feed_width]).astype(jnp.bfloat16)
+                for start in range(0, hidden_width, feed_width)
+            ]
+            order.mark(*grad_up)
     grad_down = transposed_times(order.hold(activated), grad_all).astype(jnp.bfloat16)
     if hidden_width >= model:
         grad_down = grad_down.reshape(hidden_width // model, model, model)
     else:
         grad_down = stack_output(grad_down)[None]
-    down_sum = SetSum(order, grad_down, cross_first, layout=natural, double=False)
-    up_sum.advance()
+    feed_term = jnp.concatenate([jnp.stack(grad_up), grad_down], axis=0)
+    order.mark(feed_term)
+    feed_share = lax.psum_scatter(feed_term, "sets", scatter_dimension=1, tiled=True)
     for step in range(1, tp_count):
         term = jnp.concatenate(received[step], axis=0)
         grad_normed_feed = order.hold(grad_normed_feed) + term.astype(jnp.float32)
     order.mark(grad_normed_feed)
+    average_self, inverse_self, average_feed, inverse_feed = order.hold(
+        (average_self, inverse_self, average_feed, inverse_feed)
+    )
+    unit_feed = (after_self - average_feed) * inverse_feed
+    unit_self = (after_cross - average_self) * inverse_self
     grad_rows, grad_feed_gain = norm_backward(
         order.hold(grad_normed_feed), unit_feed, inverse_feed, feed_gain
     )
     grad_after_self = grad_final + grad_rows
 
     grad_branch = (alive_rows * grad_after_self).astype(jnp.bfloat16)
-    order.mark(grad_branch)
-    down_sum.advance()
-    grad_attended = times_transposed(order.hold(grad_branch), output_weight).astype(jnp.bfloat16)
+    grad_attended = times_transposed(grad_branch, output_weight).astype(jnp.bfloat16)
     grad_mixed = self_backward(mixed_rows, grad_attended, logs_self, heads, heads_block, scale)
     order.mark(grad_mixed)
     grad_normed_self = times_transposed(order.hold(grad_mixed), mixed_weight)
@@ -786,8 +904,6 @@
     grad_cross_blocks = gather_blocks((alive_rows * grad_after_cross).astype(jnp.bfloat16))
     order.mark(grad_cross_blocks[0])
 
-    up_sum.advance()
-    down_sum.advance()
     late_mixed = order.hold(grad_mixed)
     self_terms = []
     for step in range(tp_count):
@@ -833,22 +949,15 @@
         grad_queries.append(grad_query)
         order.mark(grad_query)
         if step == 0:
-            up_sum.advance()
-            down_sum.advance()
             self_sums[1].advance()
             self_sums[0].advance()
     grad_key_table, grad_value_table = sums
-    while up_sum.stages or down_sum.stages:
-        up_sum.advance()
-        down_sum.advance()
-    feed_result = lax.all_gather(
-        jnp.concatenate([up_sum.block, down_sum.block], axis=0), "sets", axis=1, tiled=True
-    )
     held_keys, held_values = order.hold((grad_key_table, grad_value_table))
     grad_key = transposed_times(embedded, held_keys).astype(jnp.bfloat16)
     grad_value = transposed_times(embedded, held_values).astype(jnp.bfloat16)
     first_sum = SetSum(order, jnp.stack([grad_key, grad_value]), bits)
     self_sums[1].advance()
+    self_sums[0].advance()
     output_terms, query_terms = [], []
     for step in range(tp_count):
         output_terms.append(
@@ -857,9 +966,13 @@
         query_terms.append(transposed_times(rows_cross[step], order.hold(grad_queries[step])))
     grad_query = functools.reduce(jnp.add, query_terms).astype(jnp.bfloat16)
     grad_output = functools.reduce(jnp.add, output_terms).astype(jnp.bfloat16)
-    second_sum = SetSum(order, jnp.stack([grad_query, stack_output(grad_output)]), cross_first)
-    self_sums[0].advance()
+    second_sum = SetSum(
+        order, order.hold(jnp.stack([grad_query, stack_output(grad_output)])), cross_first
+    )
     first_sum.advance()
+    feed_share = order.hold(feed_share)
+    order.mark(feed_share, *order.last)
+    feed_result = lax.all_gather(feed_share, "sets", axis=1, tiled=True)
     second_sum.advance()
 
     def query_term(step):

time: 542 us -> 519 us (0.958)
  matrix products: 91.3 us -> 73.4 us
  Pallas kernels: 88.1 us -> 102 us
  waiting for transfers between devices: 139 us -> 130 us
  local copies, waits for them, and re-layouts: 62.6 us -> 55.6 us
  starting transfers between devices: 58.9 us -> 53.4 us
    dot_general x9 -> x3, matrix products: 33 us -> 12.4 us  [project(): return jnp.dot(left_rows, right_rows, preferred_element_type=jnp.float32)]
    ppermute x32 -> x24, waiting for transfers between devices: 102 us -> 91.9 us  [swap_sets(): lax.ppermute(block, 'sets', [(source, source ^ 1 << bit) for source in ra...]
    unnamed x184 -> x170, local copies, waits for them, and re-layouts: 29.4 us -> 20 us
    pallas_call x1, Pallas kernels: 4.92 us -> 13.9 us  [self_forward(): pl.pallas_call(functools.partial(self_forward_kernel, heads=heads, heads_...]
    convert_element_type x26 -> x18, other arithmetic: 18.3 us -> 11.5 us  [advance(): self.block = total.astype(jnp.bfloat16)]
    dynamic_slice x10 -> x6, local copies, waits for them, and re-layouts: 12.4 us -> 8.34 us  [halves(): lax.dynamic_slice_in_dim(view, place, 1, axis)]
    ppermute x32 -> x24, starting transfers between devices: 29.6 us -> 28.3 us  [swap_sets(): lax.ppermute(block, 'sets', [(source, source ^ 1 << bit) for source in ra...]
  transfers between devices with their start and end apart: 56 -> 49, of which waited for: 20 -> 18; matrix products, arithmetic and copies ran while one was open for 36% -> 34% of each run, Pallas kernels for 16% -> 20%
where the time goes in v3:
time: 519 us; the launch traced here: 513 us
  waiting for transfers between devices  130 us (25%)
  Pallas kernels  102 us (20%)
  other arithmetic  80.8 us (16%)
  matrix products  73.4 us (14%)
  local copies, waits for them, and re-layouts  55.6 us (11%)
  starting transfers between devices  53.4 us (10%)
  between operations  17.8 us (3%)
    ppermute x24, waiting for transfers between devices, swap_sets(): lax.ppermute(block, 'sets', [(source, source ^ 1 << bit) for source in ra...  91.9 us
    dot_general x17, matrix products, transposed_times(): lax.dot_general(left_rows, right_rows, (((0,), (0,)), ((), ())), preferre...  31 us
    pallas_call x3, Pallas kernels, feed_block(): pl.pallas_call(feed_kernel, grid=(hidden_width // tile,), in_specs=[whole...  29 us
    ppermute x24, starting transfers between devices, swap_sets(): lax.ppermute(block, 'sets', [(source, source ^ 1 << bit) for source in ra...  28.3 us
    pallas_call x2, Pallas kernels, cross_backward(): pl.pallas_call(functools.partial(cross_backward_kernel, heads=heads, span...  23.8 us
    dot_general x10, matrix products, times_transposed(): lax.dot_general(left_rows, right_rows, (((1,), (1,)), ((), ())), preferre...  22.2 us
    pallas_call x2, Pallas kernels, cross_forward(): pl.pallas_call(functools.partial(cross_forward_kernel, heads=heads, span=...  22.1 us
    unnamed x170, local copies, waits for them, and re-layouts  20 us
  transfers between devices with their start and end apart: 49, of which 18 were waited for; matrix products, arithmetic and copies ran while one was open for 34% of the time, Pallas kernels for 20%

profile of v3, /device:TPU:0, one launch (start us, length us, event | category | flops | bytes accessed | tf_op | source)
XLA Modules:
  0.0 513.5 jit_solution(8550109590885932979)
XLA Ops:
  7.2 3.0 collective-permute-start
  16.0 6.6 %multiplicity.1.counts_ref.refs_0_ = f32[1024,128]{1,0:T(8,128)} custom-call(s32[8,512]{1,0:T(8,128)} %fusion.83.chosen_ref), custom_call_target="tpu_custom_call" | custom-call | tf_op jit(solution)/shard_map/multiplicity/pallas_call | solution.py:228
  22.6 12.0 %collective-permute-done = bf16[512,1024]{1,0:T(8,128)(2,1)} collective-permute-done((bf16[512,1024]{1,0:T(8,128)(2,1)}, bf16[512,1024]{1,0:T(8,128)(2,1)}, u32[]{:S(2)}, u32[]{:S(2)}) %collective-permute-start) | collective-permute-done | bytes 1048608 | tf_op jit(solution)/shard_map/ppermute | solution.py:58
  44.5 3.9 fusion.37.value_t_ref
  48.4 3.9 convolution_convert_fusion.7.key_ref.refs_4_
  52.3 11.2 %cross_forward.2 = (bf16[512,512]{1,0:T(8,128)(2,1)}, bf16[512,512]{1,0:T(8,128)(2,1)}, f32[2,4,256]{2,1,0:T(4,128)}, f32[512,1024]{1,0:T(8,128)}) custom-call(f32[1024,128]{1,0:T(8,128)} %multiplicity.1.counts_ref.refs_0_, bf16[512,1024]{1,0:T(8,128)(2,1)} %fusion.8.rows_ref, bf16[1024,512]{1,0:T(8,128)(2,1)} %convolution_convert_fusion.7.key_ref.refs_4_, ...), custom_call_target="tpu_custom_call" | custom-call | flops 1000000 | bytes 100000 | tf_op jit(solution)/shard_map/cross_forward/pallas_call | solution.py:302
  69.4 10.8 %cross_forward.3 = (bf16[512,512]{1,0:T(8,128)(2,1)}, bf16[512,512]{1,0:T(8,128)(2,1)}, f32[2,4,256]{2,1,0:T(4,128)}, bf16[512,1024]{1,0:T(8,128)(2,1)}) custom-call(f32[1024,128]{1,0:T(8,128)} %multiplicity.1.counts_ref.refs_0_, bf16[512,1024]{1,0:T(8,128)(2,1)} %collective-permute-done.1.rows_ref, ...), custom_call_target="tpu_custom_call" | custom-call | flops 1000000 | bytes 100000 | tf_op jit(solution)/shard_map/cross_forward/pallas_call | solution.py:302
  80.8 4.1 convolution_convert_fusion.4.refs_6_
  84.9 3.9 fusion.38.refs_5_
  88.8 2.8 all-gather.4.cloned.1.call-done
  98.9 4.9 collective-permute-done.2
  103.8 3.0 convert_add_fusion.2.state_ref
  108.8 13.9 %self_forward.1 = (bf16[512,1024]{1,0:T(8,128)(2,1)}, bf16[512,3072]{1,0:T(8,128)(2,1)}, bf16[512,1024]{1,0:T(8,128)(2,1)}, f32[4,8,128]{2,1,0:T(8,128)}, f32[51...) custom-call(f32[512,1024]{1,0:T(8,128)} %convert_add_fusion.2.state_, ...), custom_call_target="tpu_custom_call" | custom-call | flops 1000000 | bytes 100000 | tf_op jit(solution)/shard_map/self_forward/pallas_call | solution.py:519
  127.0 11.8 %feed_hidden.3 = (bf16[1024,2048]{1,0:T(8,128)(2,1)}, bf16[1024,2048]{1,0:T(8,128)(2,1)}, f32[512,1024]{1,0:T(8,128)}) custom-call(bf16[512,1024]{1,0:T(8,128)(2,1)} %get-tuple-element.160.rows_ref, bf16[512,1024]{1,0:T(8,128)(2,1)} %copy-done.10, bf16[1024,2048]{1,0:T(8,128)(2,1)} %up_ref.5, bf16[2048,1024]{1,0:T(8,128)(2,1)} %down_ref.5), custom_call_target="tpu_custom_call" | custom-call | flops 1000000 | bytes 100000 | tf_op jit(solution)/shard_map/feed_hidden/pallas_call | solution.py:633
  140.6 8.5 %feed_hidden.4 = (bf16[1024,2048]{1,0:T(8,128)(2,1)}, bf16[1024,2048]{1,0:T(8,128)(2,1)}, bf16[256,1024]{1,0:T(8,128)(2,1)}) custom-call(bf16[256,1024]{1,0:T(8,128)(2,1)} %copy-done.39, bf16[256,1024]{1,0:T(8,128)(2,1)} %copy-done.54, bf16[1024,2048]{1,0:T(8,128)(2,1)} %up_ref.5, ...), custom_call_target="tpu_custom_call", output_to_operand_aliasing={{0}: (4, {}), {1}: (5, {})} | custom-call | flops 1000000 | bytes 100000 | tf_op jit(solution)/shard_map/feed_hidden/pallas_call | solution.py:633
  151.3 8.7 %feed_hidden.5 = (bf16[1024,2048]{1,0:T(8,128)(2,1)}, bf16[1024,2048]{1,0:T(8,128)(2,1)}, bf16[256,1024]{1,0:T(8,128)(2,1)}) custom-call(bf16[256,1024]{1,0:T(8,128)(2,1)} %collective-permute-done.6.rows_ref, bf16[256,1024]{1,0:T(8,128)(2,1)} %copy-done.58, bf16[1024,2048]{1,0:T(8,128)(2,1)} %up_ref.5, ...), custom_call_target="tpu_custom_call", output_to_operand_aliasing={{0}: (4, {}), {1}: (5, {})} | custom-call | flops 1000000 | bytes 100000 | tf_op jit(solution)/shard_map/feed_hidden/pallas_call | solution.py:633
  163.8 4.8 fusion.34
  171.9 5.0 convolution_convert_fusion
  176.9 3.8 pad_maximum_fusion
  180.7 3.7 convert_add_fusion.10
  185.7 3.5 multiply_reduce_fusion.2
  194.2 6.8 %self_backward.1 = bf16[512,3072]{1,0:T(8,128)(2,1)} custom-call(bf16[512,3072]{1,0:T(8,128)(2,1)} %get-tuple-element.186.rows_ref, bf16[512,1024]{1,0:T(8,128)(2,1)} %convolution_convert_fusion.3.grad_ref, f32[4,8,128]{2,1,0:T(8,128)} %get-tuple-element.187.log_ref), custom_call_target="tpu_custom_call" | custom-call | flops 1000000 | bytes 100000 | tf_op jit(solution)/shard_map/self_backward/pallas_call | solution.py:582
  201.4 8.8 %multiply_reduce_fusion.1 = (f32[1024]{0:T(1024)S(1)}, f32[512]{0:T(512)S(1)}, f32[512]{0:T(512)S(1)}, f32[512,1024]{1,0:T(8,128)S(1)}) fusion(f32[512,1024]{1,0:T(8,128)} %convert_add_fusion.2.state_ref, f32[512]{0:T(512)S(1)} %reduce.5, f32[512]{0:T(512)S(1)} %reduce.4, f32[1024]{0:T(1024)S(1)} %copy-done.76, bf16[512,3072]{1,0:T(8,128)(2,1)} %self_backward.1, ...), kind=kOutput, calls=%fused_computation.65 | convolution fusion | flops 3225417728 | bytes 13647872 | tf_op jit(solution)/shard_map/dot_general | solution.py:28
  229.1 3.0 convolution_convert_fusion.18.refs_2_
  232.0 11.4 %cross_backward.2 = (bf16[512,512]{1,0:T(8,128)(2,1)}, f32[1024,512]{1,0:T(8,128)}, f32[1024,512]{1,0:T(8,128)}) custom-call(f32[1024,128]{1,0:T(8,128)} %multiplicity.1.counts_ref.refs_0_, bf16[512,512]{1,0:T(8,128)(2,1)} %get-tuple-element.169.refs_1_, bf16[512,512]{1,0:T(8,128)(2,1)} %convolution_convert_fusion.18.refs_2_, ...), custom_call_target="tpu_custom_call" | custom-call | flops 1000000 | bytes 100000 | tf_op jit(solution)/shard_map/cross_backward/pallas_call | solution.py:396
  243.4 2.8 fusion
  253.5 2.8 convolution_convert_fusion.17.refs_2_
  256.2 12.5 %cross_backward.3 = (bf16[512,512]{1,0:T(8,128)(2,1)}, bf16[1024,512]{1,0:T(8,128)(2,1)}, bf16[1024,512]{1,0:T(8,128)(2,1)}) custom-call(f32[1024,128]{1,0:T(8,128)} %multiplicity.1.counts_ref.refs_0_, bf16[512,512]{1,0:T(8,128)(2,1)} %get-tuple-element.198.refs_1_, bf16[512,512]{1,0:T(8,128)(2,1)} %convolution_convert_fusion.17.refs_2_, ...), custom_call_target="tpu_custom_call" | custom-call | flops 1000000 | bytes 100000 | tf_op jit(solution)/shard_map/cross_backward/pallas_call | solution.py:396
  268.7 3.2 convolution_convert_fusion.1
  272.0 2.9 convolution_convert_fusion.2
  275.1 7.8 %collective-permute-done.14 = bf16[2,2,256,512]{3,2,1,0:T(8,128)(2,1)} collective-permute-done((bf16[2,2,256,512]{3,2,1,0:T(8,128)(2,1)}, bf16[2,2,256,512]{3,2,1,0:T(8,128)(2,1)}, u32[]{:S(2)}, u32[]{:S(2)}) %collective-permute-start.14) | collective-permute-done | bytes 1048608 | tf_op jit(solution)/shard_map/ppermute | solution.py:83
  313.0 4.5 fusion.101
  318.7 15.2 %collective-permute-done.19 = bf16[2,2,128,512]{3,2,1,0:T(8,128)(2,1)S(1)} collective-permute-done((bf16[2,2,128,512]{3,2,1,0:T(8,128)(2,1)S(1)}, bf16[2,2,128,512]{3,2,1,0:T(8,128)(2,1)S(1)}, u32[]{:S(2)}, u32[]{:S(2)}) %collective-permute-start.19) | collective-permute-done | bytes 524320 | tf_op jit(solution)/shard_map/ppermute | solution.py:83
  337.6 3.3 collective-permute-start.20
  341.0 13.0 %collective-permute-done.22 = bf16[2,256,512]{2,1,0:T(8,128)(2,1)S(1)} collective-permute-done((bf16[2,256,512]{2,1,0:T(8,128)(2,1)S(1)}, bf16[2,256,512]{2,1,0:T(8,128)(2,1)S(1)}, u32[]{:S(2)}, u32[]{:S(2)}) %collective-permute-start.22) | collective-permute-done | bytes 524320 | tf_op jit(solution)/shard_map/ppermute | solution.py:83
  357.2 7.9 %collective-permute-start.27 = (bf16[2,128,512]{2,1,0:T(8,128)(2,1)S(1)}, bf16[2,128,512]{2,1,0:T(8,128)(2,1)S(1)}, u32[]{:S(2)}, u32[]{:S(2)}) collective-permute-start(bf16[2,128,512]{2,1,0:T(8,128)(2,1)S(1)} %dynamic-slice_bitcast_fusion.3), channel_id=1, source_target_pairs={{0,16},{2,18},{4,20},{6,22},{8,24},{10,26},{12,28},{14,30},{16,0},... | collective-permute-start | bytes 786440 | tf_op jit(solution)/shard_map/ppermute | solution.py:83
  365.2 16.2 %collective-permute-done.20 = bf16[2,128,512]{2,1,0:T(8,128)(2,1)S(1)} collective-permute-done((bf16[2,128,512]{2,1,0:T(8,128)(2,1)S(1)}, bf16[2,128,512]{2,1,0:T(8,128)(2,1)S(1)}, u32[]{:S(2)}, u32[]{:S(2)}) %collective-permute-start.20) | collective-permute-done | bytes 262176 | tf_op jit(solution)/shard_map/ppermute | solution.py:83
  382.7 15.2 %collective-permute-done.28 = bf16[2,128,512]{2,1,0:T(8,128)(2,1)S(1)} collective-permute-done((bf16[2,128,512]{2,1,0:T(8,128)(2,1)S(1)}, bf16[2,128,512]{2,1,0:T(8,128)(2,1)S(1)}, u32[]{:S(2)}, u32[]{:S(2)}) %collective-permute-start.28) | collective-permute-done | bytes 262176 | tf_op jit(solution)/shard_map/ppermute | solution.py:83
  404.0 3.0 collective-permute-done.24
  409.8 4.0 multiply_reduce_fusion
  421.1 3.4 copy-done.9
  426.7 4.9 bitcast_convert_fusion
  431.5 4.4 maximum_convert_fusion
  440.6 3.2 convert_add_fusion.8
  443.8 14.7 %collective-permute-done.38 = bf16[2,128,512]{2,1,0:T(8,128)(2,1)S(1)} collective-permute-done((bf16[2,128,512]{2,1,0:T(8,128)(2,1)S(1)}, bf16[2,128,512]{2,1,0:T(8,128)(2,1)S(1)}, u32[]{:S(2)}, u32[]{:S(2)}) %collective-permute-start.38) | collective-permute-done | bytes 262176 | tf_op jit(solution)/shard_map/ppermute | solution.py:83
  458.7 5.4 %collective-permute-done.37 = bf16[2,128,512]{2,1,0:T(8,128)(2,1)S(1)} collective-permute-done((bf16[2,128,512]{2,1,0:T(8,128)(2,1)S(1)}, bf16[2,128,512]{2,1,0:T(8,128)(2,1)S(1)}, u32[]{:S(2)}, u32[]{:S(2)}) %collective-permute-start.37) | collective-permute-done | bytes 262176 | tf_op jit(solution)/shard_map/ppermute | solution.py:83
  466.4 12.0 %collective-permute-done.36 = f32[4,1024]{1,0:T(4,128)S(1)} collective-permute-done((f32[4,1024]{1,0:T(4,128)S(1)}, f32[4,1024]{1,0:T(4,128)S(1)}, u32[]{:S(2)}, u32[]{:S(2)}) %collective-permute-start.36) | collective-permute-done | bytes 16416 | tf_op jit(solution)/shard_map/ppermute | solution.py:1047
  482.7 4.8 fusion.50
  (401 shorter events, 164.8 us)
Async XLA Ops:
  7.2 84.4 %all-gather.4.cloned.1.call-start = ((), (), s32[]{:S(2)}) async-start(), calls=%async_computation.1 | async-start | bytes 4456448 | tf_op jit(solution)/shard_map/all_gather | solution.py:735
  7.2 27.3 %collective-permute-start = (bf16[512,1024]{1,0:T(8,128)(2,1)}, bf16[512,1024]{1,0:T(8,128)(2,1)}, u32[]{:S(2)}, u32[]{:S(2)}) collective-permute-start(bf16[512,1024]{1,0:T(8,128)(2,1)} %param.20), channel_id=1, source_target_pairs={{0,1},{1,0},{2,3},{3,2},{4,5},{5,4},{6,7},{7,6},{8,9},{9,8},{10,11... | collective-permute-start | bytes 3145736 | tf_op jit(solution)/shard_map/ppermute | solution.py:58
  12.8 26.6 %collective-permute-start.3 = (bf16[4,64,512]{2,1,0:T(8,128)(2,1)S(1)}, bf16[4,64,512]{2,1,0:T(8,128)(2,1)}, u32[]{:S(2)}, u32[]{:S(2)}) collective-permute-start(bf16[4,64,512]{2,1,0:T(8,128)(2,1)S(1)} %fusion.75), channel_id=1, source_target_pairs={{0,1},{1,0},{2,3},{3,2},{4,5},{5,4},{6,7},{7,6},{8,9},{9,8},{10,11... | collective-permute-start | bytes 786440 | tf_op jit(solution)/shard_map/ppermute | solution.py:58
  39.4 259.8 %reduce-scatter.2.cloned.1.call-start = ((), (), s32[]{:S(2)}) async-start(), calls=%async_computation.2 | async-start | bytes 8912896 | tf_op jit(solution)/shard_map/reduce_scatter | solution.py:882
  40.2 24.7 %collective-permute-start.1 = (bf16[512,1024]{1,0:T(8,128)(2,1)}, bf16[512,1024]{1,0:T(8,128)(2,1)}, u32[]{:S(2)}, u32[]{:S(2)}) collective-permute-start(bf16[512,1024]{1,0:T(8,128)(2,1)} %fusion.8.rows_ref), channel_id=1, source_target_pairs={{0,1},{1,0},{2,3},{3,2},{4,5},{5,4},{6,7},{7,6},{8,9},{9,8},{10,11... | collective-permute-start | bytes 3145736 | tf_op jit(solution)/shard_map/ppermute | solution.py:58
  64.9 16.0 %collective-permute-start.4 = (bf16[256,1024]{1,0:T(8,128)(2,1)}, bf16[256,1024]{1,0:T(8,128)(2,1)S(1)}, u32[]{:S(2)}, u32[]{:S(2)}) collective-permute-start(bf16[256,1024]{1,0:T(8,128)(2,1)} %get-tuple-element.148), channel_id=1, source_target_pairs={{0,1},{1,0},{2,3},{3,2},{4,5},{5,4},{6,7},{7,6},{8,9},{9,8},{10,11... | collective-permute-start | bytes 1572872 | tf_op jit(solution)/shard_map/ppermute | solution.py:58
  80.2 23.6 %collective-permute-start.2 = (bf16[512,1024]{1,0:T(8,128)(2,1)}, bf16[512,1024]{1,0:T(8,128)(2,1)}, u32[]{:S(2)}, u32[]{:S(2)}) collective-permute-start(bf16[512,1024]{1,0:T(8,128)(2,1)} %get-tuple-element.146), channel_id=1, source_target_pairs={{0,1},{1,0},{2,3},{3,2},{4,5},{5,4},{6,7},{7,6},{8,9},{9,8},{10,11... | collective-permute-start | bytes 3145736 | tf_op jit(solution)/shard_map/ppermute | solution.py:63
  106.9 15.8 %collective-permute-start.5 = (bf16[256,1024]{1,0:T(8,128)(2,1)S(1)}, bf16[256,1024]{1,0:T(8,128)(2,1)S(1)}, u32[]{:S(2)}, u32[]{:S(2)}) collective-permute-start(bf16[256,1024]{1,0:T(8,128)(2,1)S(1)} %copy-done.65), channel_id=1, source_target_pairs={{0,1},{1,0},{2,3},{3,2},{4,5},{5,4},{6,7},{7,6},{8,9},{9,8},{10,11... | collective-permute-start | bytes 1572872 | tf_op jit(solution)/shard_map/ppermute | solution.py:58
  125.0 14.9 %collective-permute-start.7 = (bf16[256,1024]{1,0:T(8,128)(2,1)S(1)}, bf16[256,1024]{1,0:T(8,128)(2,1)S(1)}, u32[]{:S(2)}, u32[]{:S(2)}) collective-permute-start(bf16[256,1024]{1,0:T(8,128)(2,1)S(1)} %get-tuple-element.315), channel_id=1, source_target_pairs={{0,1},{1,0},{2,3},{3,2},{4,5},{5,4},{6,7},{7,6},{8,9},{9,8},{10,11... | collective-permute-start | bytes 1572872 | tf_op jit(solution)/shard_map/ppermute | solution.py:58
  126.0 25.3 %collective-permute-start.6 = (bf16[256,1024]{1,0:T(8,128)(2,1)}, bf16[256,1024]{1,0:T(8,128)(2,1)}, u32[]{:S(2)}, u32[]{:S(2)}) collective-permute-start(bf16[256,1024]{1,0:T(8,128)(2,1)} %get-tuple-element.316), channel_id=1, source_target_pairs={{0,1},{1,0},{2,3},{3,2},{4,5},{5,4},{6,7},{7,6},{8,9},{9,8},{10,11... | collective-permute-start | bytes 1572872 | tf_op jit(solution)/shard_map/ppermute | solution.py:58
  149.2 14.6 %collective-permute-start.8 = (bf16[256,1024]{1,0:T(8,128)(2,1)}, bf16[256,1024]{1,0:T(8,128)(2,1)}, u32[]{:S(2)}, u32[]{:S(2)}) collective-permute-start(bf16[256,1024]{1,0:T(8,128)(2,1)} %get-tuple-element.164), channel_id=1, source_target_pairs={{0,1},{1,0},{2,3},{3,2},{4,5},{5,4},{6,7},{7,6},{8,9},{9,8},{10,11... | collective-permute-start | bytes 1572872 | tf_op jit(solution)/shard_map/ppermute | solution.py:63
  160.0 11.0 %collective-permute-start.9 = (bf16[256,1024]{1,0:T(8,128)(2,1)}, bf16[256,1024]{1,0:T(8,128)(2,1)S(1)}, u32[]{:S(2)}, u32[]{:S(2)}) collective-permute-start(bf16[256,1024]{1,0:T(8,128)(2,1)} %get-tuple-element.176), channel_id=1, source_target_pairs={{0,1},{1,0},{2,3},{3,2},{4,5},{5,4},{6,7},{7,6},{8,9},{9,8},{10,11... | collective-permute-start | bytes 1572872 | tf_op jit(solution)/shard_map/ppermute | solution.py:63
  180.6 240.4 %all-gather.6.cloned.1.call-start = ((), (), s32[]{:S(2)}) async-start(), calls=%async_computation.3 | async-start | bytes 8912896 | tf_op jit(solution)/shard_map/all_gather | solution.py:975
  227.6 15.9 %collective-permute-start.12 = (bf16[2,2,512,512]{3,2,1,0:T(8,128)(2,1)}, bf16[2,2,512,512]{3,2,1,0:T(8,128)(2,1)}, u32[]{:S(2)}, u32[]{:S(2)}) collective-permute-start(bf16[2,2,512,512]{3,2,1,0:T(8,128)(2,1)} %bitcast.34), channel_id=1, source_target_pairs={{0,2},{2,0},{4,6},{6,4},{8,10},{10,8},{12,14},{14,12},{16,18},{18,... | collective-permute-start | bytes 6291464 | tf_op jit(solution)/shard_map/ppermute | solution.py:83
  227.6 21.4 %collective-permute-start.11 = (bf16[2,2,512,512]{3,2,1,0:T(8,128)(2,1)}, bf16[2,2,512,512]{3,2,1,0:T(8,128)(2,1)}, u32[]{:S(2)}, u32[]{:S(2)}) collective-permute-start(bf16[2,2,512,512]{3,2,1,0:T(8,128)(2,1)} %bitcast.32), channel_id=1, source_target_pairs={{0,2},{2,0},{4,6},{6,4},{8,10},{10,8},{12,14},{14,12},{16,18},{18,... | collective-permute-start | bytes 6291464 | tf_op jit(solution)/shard_map/ppermute | solution.py:83
  228.1 25.4 %collective-permute-start.10 = (bf16[512,1024]{1,0:T(8,128)(2,1)}, bf16[512,1024]{1,0:T(8,128)(2,1)}, u32[]{:S(2)}, u32[]{:S(2)}) collective-permute-start(bf16[512,1024]{1,0:T(8,128)(2,1)} %get-tuple-element.214), channel_id=1, source_target_pairs={{0,1},{1,0},{2,3},{3,2},{4,5},{5,4},{6,7},{7,6},{8,9},{9,8},{10,11... | collective-permute-start | bytes 3145736 | tf_op jit(solution)/shard_map/ppermute | solution.py:58
  247.4 35.5 %collective-permute-start.14 = (bf16[2,2,256,512]{3,2,1,0:T(8,128)(2,1)}, bf16[2,2,256,512]{3,2,1,0:T(8,128)(2,1)}, u32[]{:S(2)}, u32[]{:S(2)}) collective-permute-start(bf16[2,2,256,512]{3,2,1,0:T(8,128)(2,1)} %bitcast.38), channel_id=1, source_target_pairs={{0,4},{2,6},{4,0},{6,2},{8,12},{10,14},{12,8},{14,10},{16,20},{18,... | collective-permute-start | bytes 3145736 | tf_op jit(solution)/shard_map/ppermute | solution.py:83
  252.2 33.4 %collective-permute-start.13 = (bf16[2,512,512]{2,1,0:T(8,128)(2,1)}, bf16[2,512,512]{2,1,0:T(8,128)(2,1)}, u32[]{:S(2)}, u32[]{:S(2)}) collective-permute-start(bf16[2,512,512]{2,1,0:T(8,128)(2,1)} %slice_bitcast_fusion.6), channel_id=1, source_target_pairs={{0,1},{1,0},{2,3},{3,2},{4,5},{5,4},{6,7},{7,6},{8,9},{9,8},{10,11... | collective-permute-start | bytes 3145736 | tf_op jit(solution)/shard_map/ppermute | solution.py:63
  275.0 22.8 %collective-permute-start.16 = (bf16[2,512,512]{2,1,0:T(8,128)(2,1)S(1)}, bf16[2,512,512]{2,1,0:T(8,128)(2,1)S(1)}, u32[]{:S(2)}, u32[]{:S(2)}) collective-permute-start(bf16[2,512,512]{2,1,0:T(8,128)(2,1)S(1)} %fusion.49), channel_id=1, source_target_pairs={{0,2},{2,0},{4,6},{6,4},{8,10},{10,8},{12,14},{14,12},{16,18},{18,... | collective-permute-start | bytes 3145736 | tf_op jit(solution)/shard_map/ppermute | solution.py:83
  299.2 182.2 %all-gather.8.cloned.1.call-start = ((), (), s32[]{:S(2)}) async-start(), calls=%async_computation.4 | async-start | bytes 4456448 | tf_op jit(solution)/shard_map/all_gather | solution.py:1018
  299.7 6.6 %collective-permute-start.15 = (bf16[2,512,512]{2,1,0:T(8,128)(2,1)}, bf16[2,512,512]{2,1,0:T(8,128)(2,1)}, u32[]{:S(2)}, u32[]{:S(2)}) collective-permute-start(bf16[2,512,512]{2,1,0:T(8,128)(2,1)} %dynamic-slice_bitcast_fusion), channel_id=1, source_target_pairs={{0,2},{2,0},{4,6},{6,4},{8,10},{10,8},{12,14},{14,12},{16,18},{18,... | collective-permute-start | bytes 3145736 | tf_op jit(solution)/shard_map/ppermute | solution.py:83
  304.1 29.9 %collective-permute-start.19 = (bf16[2,2,128,512]{3,2,1,0:T(8,128)(2,1)S(1)}, bf16[2,2,128,512]{3,2,1,0:T(8,128)(2,1)S(1)}, u32[]{:S(2)}, u32[]{:S(2)}) collective-permute-start(bf16[2,2,128,512]{3,2,1,0:T(8,128)(2,1)S(1)} %bitcast.315), channel_id=1, source_target_pairs={{0,8},{2,10},{4,12},{6,14},{8,0},{10,2},{12,4},{14,6},{16,24},{18,... | collective-permute-start | bytes 1572872 | tf_op jit(solution)/shard_map/ppermute | solution.py:83
  304.2 31.1 %collective-permute-start.18 = (bf16[2,256,512]{2,1,0:T(8,128)(2,1)S(1)}, bf16[2,256,512]{2,1,0:T(8,128)(2,1)S(1)}, u32[]{:S(2)}, u32[]{:S(2)}) collective-permute-start(bf16[2,256,512]{2,1,0:T(8,128)(2,1)S(1)} %bitcast.314), channel_id=1, source_target_pairs={{0,4},{2,6},{4,0},{6,2},{8,12},{10,14},{12,8},{14,10},{16,20},{18,... | collective-permute-start | bytes 1572872 | tf_op jit(solution)/shard_map/ppermute | solution.py:83
  305.0 32.6 %collective-permute-start.23 = (bf16[2,256,512]{2,1,0:T(8,128)(2,1)S(1)}, bf16[2,256,512]{2,1,0:T(8,128)(2,1)S(1)}, u32[]{:S(2)}, u32[]{:S(2)}) collective-permute-start(bf16[2,256,512]{2,1,0:T(8,128)(2,1)S(1)} %copy-done.62), channel_id=1, source_target_pairs={{0,4},{2,6},{4,0},{6,2},{8,12},{10,14},{12,8},{14,10},{16,20},{18,... | collective-permute-start | bytes 1572872 | tf_op jit(solution)/shard_map/ppermute | solution.py:83
  308.0 46.0 %collective-permute-start.22 = (bf16[2,256,512]{2,1,0:T(8,128)(2,1)S(1)}, bf16[2,256,512]{2,1,0:T(8,128)(2,1)S(1)}, u32[]{:S(2)}, u32[]{:S(2)}) collective-permute-start(bf16[2,256,512]{2,1,0:T(8,128)(2,1)S(1)} %dynamic-slice_bitcast_fusion.1), channel_id=1, source_target_pairs={{0,8},{2,10},{4,12},{6,14},{8,0},{10,2},{12,4},{14,6},{16,24},{18,... | collective-permute-start | bytes 1572872 | tf_op jit(solution)/shard_map/ppermute | solution.py:83
  310.8 89.3 %collective-permute-start.26 = (bf16[512,1024]{1,0:T(8,128)(2,1)S(1)}, bf16[512,1024]{1,0:T(8,128)(2,1)S(1)}, u32[]{:S(2)}, u32[]{:S(2)}) collective-permute-start(bf16[512,1024]{1,0:T(8,128)(2,1)S(1)} %convolution_convert_fusion.8), channel_id=1, source_target_pairs={{0,1},{1,0},{2,3},{3,2},{4,5},{5,4},{6,7},{7,6},{8,9},{9,8},{10,11... | collective-permute-start | bytes 3145736 | tf_op jit(solution)/shard_map/ppermute | solution.py:63
  334.0 75.8 %collective-permute-start.17 = (bf16[512,1024]{1,0:T(8,128)(2,1)}, bf16[512,1024]{1,0:T(8,128)(2,1)}, u32[]{:S(2)}, u32[]{:S(2)}) collective-permute-start(bf16[512,1024]{1,0:T(8,128)(2,1)} %slice.412), channel_id=1, source_target_pairs={{0,1},{1,0},{2,3},{3,2},{4,5},{5,4},{6,7},{7,6},{8,9},{9,8},{10,11... | collective-permute-start | bytes 3145736 | tf_op jit(solution)/shard_map/ppermute | solution.py:63
  335.2 22.0 %collective-permute-start.21 = (bf16[2,2,64,512]{3,2,1,0:T(8,128)(2,1)S(1)}, bf16[2,2,64,512]{3,2,1,0:T(8,128)(2,1)S(1)}, u32[]{:S(2)}, u32[]{:S(2)}) collective-permute-start(bf16[2,2,64,512]{3,2,1,0:T(8,128)(2,1)S(1)} %dynamic-slice_bitcast_fusion.5), channel_id=1, source_target_pairs={{0,16},{2,18},{4,20},{6,22},{8,24},{10,26},{12,28},{14,30},{16,0},... | collective-permute-start | bytes 786440 | tf_op jit(solution)/shard_map/ppermute | solution.py:83
  337.6 43.9 %collective-permute-start.20 = (bf16[2,128,512]{2,1,0:T(8,128)(2,1)S(1)}, bf16[2,128,512]{2,1,0:T(8,128)(2,1)S(1)}, u32[]{:S(2)}, u32[]{:S(2)}) collective-permute-start(bf16[2,128,512]{2,1,0:T(8,128)(2,1)S(1)} %bitcast.316), channel_id=1, source_target_pairs={{0,8},{2,10},{4,12},{6,14},{8,0},{10,2},{12,4},{14,6},{16,24},{18,... | collective-permute-start | bytes 786440 | tf_op jit(solution)/shard_map/ppermute | solution.py:83
  354.1 43.8 %collective-permute-start.28 = (bf16[2,128,512]{2,1,0:T(8,128)(2,1)S(1)}, bf16[2,128,512]{2,1,0:T(8,128)(2,1)S(1)}, u32[]{:S(2)}, u32[]{:S(2)}) collective-permute-start(bf16[2,128,512]{2,1,0:T(8,128)(2,1)S(1)} %dynamic-slice_bitcast_fusion.4), channel_id=1, source_target_pairs={{0,8},{2,10},{4,12},{6,14},{8,0},{10,2},{12,4},{14,6},{16,24},{18,... | collective-permute-start | bytes 786440 | tf_op jit(solution)/shard_map/ppermute | solution.py:83
  357.2 42.8 %collective-permute-start.27 = (bf16[2,128,512]{2,1,0:T(8,128)(2,1)S(1)}, bf16[2,128,512]{2,1,0:T(8,128)(2,1)S(1)}, u32[]{:S(2)}, u32[]{:S(2)}) collective-permute-start(bf16[2,128,512]{2,1,0:T(8,128)(2,1)S(1)} %dynamic-slice_bitcast_fusion.3), channel_id=1, source_target_pairs={{0,16},{2,18},{4,20},{6,22},{8,24},{10,26},{12,28},{14,30},{16,0},... | collective-permute-start | bytes 786440 | tf_op jit(solution)/shard_map/ppermute | solution.py:83
  381.4 22.5 %collective-permute-start.25 = (bf16[2,64,512]{2,1,0:T(8,128)(2,1)S(1)}, bf16[2,64,512]{2,1,0:T(8,128)(2,1)S(1)}, u32[]{:S(2)}, u32[]{:S(2)}) collective-permute-start(bf16[2,64,512]{2,1,0:T(8,128)(2,1)S(1)} %slice_bitcast_fusion.12), channel_id=1, source_target_pairs={{0,1},{1,0},{2,3},{3,2},{4,5},{5,4},{6,7},{7,6},{8,9},{9,8},{10,11... | collective-permute-start | bytes 393224 | tf_op jit(solution)/shard_map/ppermute | solution.py:63
  397.9 9.0 %collective-permute-start.24 = (bf16[2,64,512]{2,1,0:T(8,128)(2,1)S(1)}, bf16[2,64,512]{2,1,0:T(8,128)(2,1)S(1)}, u32[]{:S(2)}, u32[]{:S(2)}) collective-permute-start(bf16[2,64,512]{2,1,0:T(8,128)(2,1)S(1)} %dynamic-slice_bitcast_fusion.8), channel_id=1, source_target_pairs={{0,16},{2,18},{4,20},{6,22},{8,24},{10,26},{12,28},{14,30},{16,0},... | collective-permute-start | bytes 393224 | tf_op jit(solution)/shard_map/ppermute | solution.py:83
  407.8 7.3 %collective-permute-start.31 = (bf16[2,64,512]{2,1,0:T(8,128)(2,1)}, bf16[2,64,512]{2,1,0:T(8,128)(2,1)S(1)}, u32[]{:S(2)}, u32[]{:S(2)}) collective-permute-start(bf16[2,64,512]{2,1,0:T(8,128)(2,1)} %dynamic-slice_bitcast_fusion.7), channel_id=1, source_target_pairs={{0,16},{2,18},{4,20},{6,22},{8,24},{10,26},{12,28},{14,30},{16,0},... | collective-permute-start | bytes 393224 | tf_op jit(solution)/shard_map/ppermute | solution.py:83
  407.8 31.3 %collective-permute-start.35 = (bf16[512,1024]{1,0:T(8,128)(2,1)}, bf16[512,1024]{1,0:T(8,128)(2,1)}, u32[]{:S(2)}, u32[]{:S(2)}) collective-permute-start(bf16[512,1024]{1,0:T(8,128)(2,1)} %add_convert_fusion), channel_id=1, source_target_pairs={{0,1},{1,0},{2,3},{3,2},{4,5},{5,4},{6,7},{7,6},{8,9},{9,8},{10,11... | collective-permute-start | bytes 3145736 | tf_op jit(solution)/shard_map/ppermute | solution.py:63
  409.3 7.0 %collective-permute-start.30 = (bf16[2,64,512]{2,1,0:T(8,128)(2,1)S(1)}, bf16[2,64,512]{2,1,0:T(8,128)(2,1)S(1)}, u32[]{:S(2)}, u32[]{:S(2)}) collective-permute-start(bf16[2,64,512]{2,1,0:T(8,128)(2,1)S(1)} %dynamic-slice_bitcast_fusion.6), channel_id=1, source_target_pairs={{0,4},{2,6},{4,0},{6,2},{8,12},{10,14},{12,8},{14,10},{16,20},{18,... | collective-permute-start | bytes 393224 | tf_op jit(solution)/shard_map/ppermute | solution.py:83
  415.1 20.9 %collective-permute-start.34 = (bf16[2,64,512]{2,1,0:T(8,128)(2,1)S(1)}, bf16[2,64,512]{2,1,0:T(8,128)(2,1)S(1)}, u32[]{:S(2)}, u32[]{:S(2)}) collective-permute-start(bf16[2,64,512]{2,1,0:T(8,128)(2,1)S(1)} %fusion.76), channel_id=1, source_target_pairs={{0,16},{2,18},{4,20},{6,22},{8,24},{10,26},{12,28},{14,30},{16,0},... | collective-permute-start | bytes 393224 | tf_op jit(solution)/shard_map/ppermute | solution.py:83
  417.8 19.0 %collective-permute-start.33 = (bf16[2,64,512]{2,1,0:T(8,128)(2,1)S(1)}, bf16[2,64,512]{2,1,0:T(8,128)(2,1)S(1)}, u32[]{:S(2)}, u32[]{:S(2)}) collective-permute-start(bf16[2,64,512]{2,1,0:T(8,128)(2,1)S(1)} %fusion.77), channel_id=1, source_target_pairs={{0,4},{2,6},{4,0},{6,2},{8,12},{10,14},{12,8},{14,10},{16,20},{18,... | collective-permute-start | bytes 393224 | tf_op jit(solution)/shard_map/ppermute | solution.py:83
  420.0 19.1 %collective-permute-start.32 = (f32[4,1024]{1,0:T(4,128)S(1)}, f32[4,1024]{1,0:T(4,128)S(1)}, u32[]{:S(2)}, u32[]{:S(2)}) collective-permute-start(f32[4,1024]{1,0:T(4,128)S(1)} %fusion.86), channel_id=1, source_target_pairs={{0,4},{2,6},{4,0},{6,2},{8,12},{10,14},{12,8},{14,10},{16,20},{18,... | collective-permute-start | bytes 49160 | tf_op jit(solution)/shard_map/ppermute | solution.py:1047
  436.0 22.5 %collective-permute-start.38 = (bf16[2,128,512]{2,1,0:T(8,128)(2,1)S(1)}, bf16[2,128,512]{2,1,0:T(8,128)(2,1)S(1)}, u32[]{:S(2)}, u32[]{:S(2)}) collective-permute-start(bf16[2,128,512]{2,1,0:T(8,128)(2,1)S(1)} %pad_maximum_fusion.9), channel_id=1, source_target_pairs={{0,8},{2,10},{4,12},{6,14},{8,0},{10,2},{12,4},{14,6},{16,24},{18,... | collective-permute-start | bytes 786440 | tf_op jit(solution)/shard_map/ppermute | solution.py:83
  436.9 27.3 %collective-permute-start.37 = (bf16[2,128,512]{2,1,0:T(8,128)(2,1)S(1)}, bf16[2,128,512]{2,1,0:T(8,128)(2,1)S(1)}, u32[]{:S(2)}, u32[]{:S(2)}) collective-permute-start(bf16[2,128,512]{2,1,0:T(8,128)(2,1)S(1)} %pad_maximum_fusion.10), channel_id=1, source_target_pairs={{0,16},{2,18},{4,20},{6,22},{8,24},{10,26},{12,28},{14,30},{16,0},... | collective-permute-start | bytes 786440 | tf_op jit(solution)/shard_map/ppermute | solution.py:83
  458.7 19.7 %collective-permute-start.41 = (bf16[2,256,512]{2,1,0:T(8,128)(2,1)S(1)}, bf16[2,256,512]{2,1,0:T(8,128)(2,1)S(1)}, u32[]{:S(2)}, u32[]{:S(2)}) collective-permute-start(bf16[2,256,512]{2,1,0:T(8,128)(2,1)S(1)} %pad_maximum_fusion.7), channel_id=1, source_target_pairs={{0,4},{2,6},{4,0},{6,2},{8,12},{10,14},{12,8},{14,10},{16,20},{18,... | collective-permute-start | bytes 1572872 | tf_op jit(solution)/shard_map/ppermute | solution.py:83
  464.3 15.3 %collective-permute-start.40 = (bf16[2,256,512]{2,1,0:T(8,128)(2,1)S(1)}, bf16[2,256,512]{2,1,0:T(8,128)(2,1)S(1)}, u32[]{:S(2)}, u32[]{:S(2)}) collective-permute-start(bf16[2,256,512]{2,1,0:T(8,128)(2,1)S(1)} %pad_maximum_fusion.8), channel_id=1, source_target_pairs={{0,8},{2,10},{4,12},{6,14},{8,0},{10,2},{12,4},{14,6},{16,24},{18,... | collective-permute-start | bytes 1572872 | tf_op jit(solution)/shard_map/ppermute | solution.py:83
  464.4 14.0 %collective-permute-start.36 = (f32[4,1024]{1,0:T(4,128)S(1)}, f32[4,1024]{1,0:T(4,128)S(1)}, u32[]{:S(2)}, u32[]{:S(2)}) collective-permute-start(f32[4,1024]{1,0:T(4,128)S(1)} %fusion.158), channel_id=1, source_target_pairs={{0,8},{2,10},{4,12},{6,14},{8,0},{10,2},{12,4},{14,6},{16,24},{18,... | collective-permute-start | bytes 49160 | tf_op jit(solution)/shard_map/ppermute | solution.py:1047
  479.7 14.2 %collective-permute-start.44 = (bf16[2,512,512]{2,1,0:T(8,128)(2,1)}, bf16[2,512,512]{2,1,0:T(8,128)(2,1)}, u32[]{:S(2)}, u32[]{:S(2)}) collective-permute-start(bf16[2,512,512]{2,1,0:T(8,128)(2,1)} %pad_maximum_fusion.5), channel_id=1, source_target_pairs={{0,2},{2,0},{4,6},{6,4},{8,10},{10,8},{12,14},{14,12},{16,18},{18,... | collective-permute-start | bytes 3145736 | tf_op jit(solution)/shard_map/ppermute | solution.py:83
  480.9 13.0 %collective-permute-start.43 = (bf16[2,512,512]{2,1,0:T(8,128)(2,1)}, bf16[2,512,512]{2,1,0:T(8,128)(2,1)}, u32[]{:S(2)}, u32[]{:S(2)}) collective-permute-start(bf16[2,512,512]{2,1,0:T(8,128)(2,1)} %pad_maximum_fusion.6), channel_id=1, source_target_pairs={{0,2},{2,0},{4,6},{6,4},{8,10},{10,8},{12,14},{14,12},{16,18},{18,... | collective-permute-start | bytes 3145736 | tf_op jit(solution)/shard_map/ppermute | solution.py:83
  487.6 4.8 collective-permute-start.39
  492.4 4.7 collective-permute-start.42
  (83 other events, 581.9 us)
Sparse Core Ops, SparseCore 0:
  39.5 52.0 all-gather.3
  180.8 113.7 reduce-scatter.1
  299.3 106.7 all-gather.5
  408.8 61.1 all-gather.7

commit v4 on v3

--- a/solution.py
+++ b/solution.py
@@ -728,7 +728,7 @@
     order.mark(log_counts)
     peer_inputs = order.hold(tuple(peer_inputs))
     order.mark(*peer_inputs)
-    rows_cross = gather_blocks(order.hold(normed_cross))
+    rows_cross = gather_blocks(normed_cross)
     embedded = jnp.concatenate(peer_inputs, axis=0)
     order.mark(embedded)
     peer_stacks = [

time: 519 us -> 519 us (level)
  transfers between devices with their start and end apart: 49 -> 49, of which waited for: 18 -> 17; matrix products, arithmetic and copies ran while one was open for 34% -> 34% of each run, Pallas kernels for 20% -> 20%
where the time goes in v4:
time: 519 us; the launch traced here: 513 us
  waiting for transfers between devices  129 us (25%)
  Pallas kernels  102 us (20%)
  other arithmetic  80.9 us (16%)
  matrix products  73.8 us (14%)
  local copies, waits for them, and re-layouts  55.6 us (11%)
  starting transfers between devices  54.3 us (10%)
  between operations  17.8 us (3%)
    ppermute x24, waiting for transfers between devices, swap_sets(): lax.ppermute(block, 'sets', [(source, source ^ 1 << bit) for source in ra...  91.5 us
    dot_general x17, matrix products, transposed_times(): lax.dot_general(left_rows, right_rows, (((0,), (0,)), ((), ())), preferre...  31.2 us
    pallas_call x3, Pallas kernels, feed_block(): pl.pallas_call(feed_kernel, grid=(hidden_width // tile,), in_specs=[whole...  29 us
    ppermute x24, starting transfers between devices, swap_sets(): lax.ppermute(block, 'sets', [(source, source ^ 1 << bit) for source in ra...  26.3 us
    pallas_call x2, Pallas kernels, cross_backward(): pl.pallas_call(functools.partial(cross_backward_kernel, heads=heads, span...  23.8 us
    dot_general x10, matrix products, times_transposed(): lax.dot_general(left_rows, right_rows, (((1,), (1,)), ((), ())), preferre...  22.5 us
    pallas_call x2, Pallas kernels, cross_forward(): pl.pallas_call(functools.partial(cross_forward_kernel, heads=heads, span=...  22.1 us
    unnamed x170, local copies, waits for them, and re-layouts  20 us
  transfers between devices with their start and end apart: 49, of which 17 were waited for; matrix products, arithmetic and copies ran while one was open for 34% of the time, Pallas kernels for 20%

profile of v4, /device:TPU:0, one launch (start us, length us, event | category | flops | bytes accessed | tf_op | source)
XLA Modules:
  0.0 513.1 jit_solution(2487360001852049528)
XLA Ops:
  7.2 3.0 collective-permute-start
  16.0 6.6 %multiplicity.1.counts_ref.refs_0_ = f32[1024,128]{1,0:T(8,128)} custom-call(s32[8,512]{1,0:T(8,128)} %fusion.83.chosen_ref), custom_call_target="tpu_custom_call" | custom-call | tf_op jit(solution)/shard_map/multiplicity/pallas_call | solution.py:228
  22.6 12.0 %collective-permute-done = bf16[512,1024]{1,0:T(8,128)(2,1)} collective-permute-done((bf16[512,1024]{1,0:T(8,128)(2,1)}, bf16[512,1024]{1,0:T(8,128)(2,1)}, u32[]{:S(2)}, u32[]{:S(2)}) %collective-permute-start) | collective-permute-done | bytes 1048608 | tf_op jit(solution)/shard_map/ppermute | solution.py:58
  44.7 3.9 fusion.37.value_t_ref
  48.5 3.9 convolution_convert_fusion.7.key_ref.refs_4_
  52.4 11.2 %cross_forward.2 = (bf16[512,512]{1,0:T(8,128)(2,1)}, bf16[512,512]{1,0:T(8,128)(2,1)}, f32[2,4,256]{2,1,0:T(4,128)}, f32[512,1024]{1,0:T(8,128)}) custom-call(f32[1024,128]{1,0:T(8,128)} %multiplicity.1.counts_ref.refs_0_, bf16[512,1024]{1,0:T(8,128)(2,1)} %fusion.8.rows_ref, bf16[1024,512]{1,0:T(8,128)(2,1)} %convolution_convert_fusion.7.key_ref.refs_4_, ...), custom_call_target="tpu_custom_call" | custom-call | flops 1000000 | bytes 100000 | tf_op jit(solution)/shard_map/cross_forward/pallas_call | solution.py:302
  68.7 10.8 %cross_forward.3 = (bf16[512,512]{1,0:T(8,128)(2,1)}, bf16[512,512]{1,0:T(8,128)(2,1)}, f32[2,4,256]{2,1,0:T(4,128)}, bf16[512,1024]{1,0:T(8,128)(2,1)}) custom-call(f32[1024,128]{1,0:T(8,128)} %multiplicity.1.counts_ref.refs_0_, bf16[512,1024]{1,0:T(8,128)(2,1)} %collective-permute-done.1.rows_ref, ...), custom_call_target="tpu_custom_call" | custom-call | flops 1000000 | bytes 100000 | tf_op jit(solution)/shard_map/cross_forward/pallas_call | solution.py:302
  80.2 4.0 convolution_convert_fusion.4.refs_6_
  84.2 3.9 fusion.38.refs_5_
  88.1 3.7 all-gather.4.cloned.1.call-done
  99.1 4.1 collective-permute-done.2
  103.2 3.0 convert_add_fusion.2.state_ref
  107.6 13.9 %self_forward.1 = (bf16[512,1024]{1,0:T(8,128)(2,1)}, bf16[512,3072]{1,0:T(8,128)(2,1)}, bf16[512,1024]{1,0:T(8,128)(2,1)}, f32[4,8,128]{2,1,0:T(8,128)}, f32[51...) custom-call(f32[512,1024]{1,0:T(8,128)} %convert_add_fusion.2.state_, ...), custom_call_target="tpu_custom_call" | custom-call | flops 1000000 | bytes 100000 | tf_op jit(solution)/shard_map/self_forward/pallas_call | solution.py:519
  125.8 11.8 %feed_hidden.3 = (bf16[1024,2048]{1,0:T(8,128)(2,1)}, bf16[1024,2048]{1,0:T(8,128)(2,1)}, f32[512,1024]{1,0:T(8,128)}) custom-call(bf16[512,1024]{1,0:T(8,128)(2,1)} %get-tuple-element.158.rows_ref, bf16[512,1024]{1,0:T(8,128)(2,1)} %copy-done.10, bf16[1024,2048]{1,0:T(8,128)(2,1)} %up_ref.5, bf16[2048,1024]{1,0:T(8,128)(2,1)} %down_ref.5), custom_call_target="tpu_custom_call" | custom-call | flops 1000000 | bytes 100000 | tf_op jit(solution)/shard_map/feed_hidden/pallas_call | solution.py:633
  139.5 8.5 %feed_hidden.4 = (bf16[1024,2048]{1,0:T(8,128)(2,1)}, bf16[1024,2048]{1,0:T(8,128)(2,1)}, bf16[256,1024]{1,0:T(8,128)(2,1)}) custom-call(bf16[256,1024]{1,0:T(8,128)(2,1)} %copy-done.39, bf16[256,1024]{1,0:T(8,128)(2,1)} %copy-done.54, bf16[1024,2048]{1,0:T(8,128)(2,1)} %up_ref.5, ...), custom_call_target="tpu_custom_call", output_to_operand_aliasing={{0}: (4, {}), {1}: (5, {})} | custom-call | flops 1000000 | bytes 100000 | tf_op jit(solution)/shard_map/feed_hidden/pallas_call | solution.py:633
  150.7 8.7 %feed_hidden.5 = (bf16[1024,2048]{1,0:T(8,128)(2,1)}, bf16[1024,2048]{1,0:T(8,128)(2,1)}, bf16[256,1024]{1,0:T(8,128)(2,1)}) custom-call(bf16[256,1024]{1,0:T(8,128)(2,1)} %collective-permute-done.6.rows_ref, bf16[256,1024]{1,0:T(8,128)(2,1)} %copy-done.58, bf16[1024,2048]{1,0:T(8,128)(2,1)} %up_ref.5, ...), custom_call_target="tpu_custom_call", output_to_operand_aliasing={{0}: (4, {}), {1}: (5, {})} | custom-call | flops 1000000 | bytes 100000 | tf_op jit(solution)/shard_map/feed_hidden/pallas_call | solution.py:633
  162.6 4.8 fusion.34
  170.7 5.0 convolution_convert_fusion
  175.7 3.8 pad_maximum_fusion
  179.5 3.7 convert_add_fusion.10
  184.5 3.5 multiply_reduce_fusion.2
  192.8 6.7 %self_backward.1 = bf16[512,3072]{1,0:T(8,128)(2,1)} custom-call(bf16[512,3072]{1,0:T(8,128)(2,1)} %get-tuple-element.184.rows_ref, bf16[512,1024]{1,0:T(8,128)(2,1)} %convolution_convert_fusion.3.grad_ref, f32[4,8,128]{2,1,0:T(8,128)} %get-tuple-element.185.log_ref), custom_call_target="tpu_custom_call" | custom-call | flops 1000000 | bytes 100000 | tf_op jit(solution)/shard_map/self_backward/pallas_call | solution.py:582
  199.9 9.0 %multiply_reduce_fusion.1 = (f32[1024]{0:T(1024)S(1)}, f32[512]{0:T(512)S(1)}, f32[512]{0:T(512)S(1)}, f32[512,1024]{1,0:T(8,128)S(1)}) fusion(f32[512,1024]{1,0:T(8,128)} %convert_add_fusion.2.state_ref, f32[512]{0:T(512)S(1)} %reduce.5, f32[512]{0:T(512)S(1)} %reduce.4, f32[1024]{0:T(1024)S(1)} %copy-done.76, bf16[512,3072]{1,0:T(8,128)(2,1)} %self_backward.1, ...), kind=kOutput, calls=%fused_computation.65 | convolution fusion | flops 3225417728 | bytes 13647872 | tf_op jit(solution)/shard_map/dot_general | solution.py:28
  228.5 3.0 convolution_convert_fusion.18.refs_2_
  231.4 11.4 %cross_backward.2 = (bf16[512,512]{1,0:T(8,128)(2,1)}, f32[1024,512]{1,0:T(8,128)}, f32[1024,512]{1,0:T(8,128)}) custom-call(f32[1024,128]{1,0:T(8,128)} %multiplicity.1.counts_ref.refs_0_, bf16[512,512]{1,0:T(8,128)(2,1)} %get-tuple-element.167.refs_1_, bf16[512,512]{1,0:T(8,128)(2,1)} %convolution_convert_fusion.18.refs_2_, ...), custom_call_target="tpu_custom_call" | custom-call | flops 1000000 | bytes 100000 | tf_op jit(solution)/shard_map/cross_backward/pallas_call | solution.py:396
  242.8 2.8 fusion
  252.6 2.8 convolution_convert_fusion.17.refs_2_
  255.3 12.5 %cross_backward.3 = (bf16[512,512]{1,0:T(8,128)(2,1)}, bf16[1024,512]{1,0:T(8,128)(2,1)}, bf16[1024,512]{1,0:T(8,128)(2,1)}) custom-call(f32[1024,128]{1,0:T(8,128)} %multiplicity.1.counts_ref.refs_0_, bf16[512,512]{1,0:T(8,128)(2,1)} %get-tuple-element.196.refs_1_, bf16[512,512]{1,0:T(8,128)(2,1)} %convolution_convert_fusion.17.refs_2_, ...), custom_call_target="tpu_custom_call" | custom-call | flops 1000000 | bytes 100000 | tf_op jit(solution)/shard_map/cross_backward/pallas_call | solution.py:396
  267.8 3.2 convolution_convert_fusion.1
  271.0 3.1 convolution_convert_fusion.2
  274.4 7.6 %collective-permute-done.14 = bf16[2,2,256,512]{3,2,1,0:T(8,128)(2,1)} collective-permute-done((bf16[2,2,256,512]{3,2,1,0:T(8,128)(2,1)}, bf16[2,2,256,512]{3,2,1,0:T(8,128)(2,1)}, u32[]{:S(2)}, u32[]{:S(2)}) %collective-permute-start.14) | collective-permute-done | bytes 1048608 | tf_op jit(solution)/shard_map/ppermute | solution.py:83
  312.4 4.5 fusion.101
  318.1 14.7 %collective-permute-done.19 = bf16[2,2,128,512]{3,2,1,0:T(8,128)(2,1)S(1)} collective-permute-done((bf16[2,2,128,512]{3,2,1,0:T(8,128)(2,1)S(1)}, bf16[2,2,128,512]{3,2,1,0:T(8,128)(2,1)S(1)}, u32[]{:S(2)}, u32[]{:S(2)}) %collective-permute-start.19) | collective-permute-done | bytes 524320 | tf_op jit(solution)/shard_map/ppermute | solution.py:83
  336.7 3.1 collective-permute-start.20
  340.0 13.4 %collective-permute-done.22 = bf16[2,256,512]{2,1,0:T(8,128)(2,1)S(1)} collective-permute-done((bf16[2,256,512]{2,1,0:T(8,128)(2,1)S(1)}, bf16[2,256,512]{2,1,0:T(8,128)(2,1)S(1)}, u32[]{:S(2)}, u32[]{:S(2)}) %collective-permute-start.22) | collective-permute-done | bytes 524320 | tf_op jit(solution)/shard_map/ppermute | solution.py:83
  356.5 7.0 %collective-permute-start.27 = (bf16[2,128,512]{2,1,0:T(8,128)(2,1)S(1)}, bf16[2,128,512]{2,1,0:T(8,128)(2,1)S(1)}, u32[]{:S(2)}, u32[]{:S(2)}) collective-permute-start(bf16[2,128,512]{2,1,0:T(8,128)(2,1)S(1)} %dynamic-slice_bitcast_fusion.3), channel_id=1, source_target_pairs={{0,16},{2,18},{4,20},{6,22},{8,24},{10,26},{12,28},{14,30},{16,0},... | collective-permute-start | bytes 786440 | tf_op jit(solution)/shard_map/ppermute | solution.py:83
  363.6 16.6 %collective-permute-done.20 = bf16[2,128,512]{2,1,0:T(8,128)(2,1)S(1)} collective-permute-done((bf16[2,128,512]{2,1,0:T(8,128)(2,1)S(1)}, bf16[2,128,512]{2,1,0:T(8,128)(2,1)S(1)}, u32[]{:S(2)}, u32[]{:S(2)}) %collective-permute-start.20) | collective-permute-done | bytes 262176 | tf_op jit(solution)/shard_map/ppermute | solution.py:83
  382.4 14.6 %collective-permute-done.28 = bf16[2,128,512]{2,1,0:T(8,128)(2,1)S(1)} collective-permute-done((bf16[2,128,512]{2,1,0:T(8,128)(2,1)S(1)}, bf16[2,128,512]{2,1,0:T(8,128)(2,1)S(1)}, u32[]{:S(2)}, u32[]{:S(2)}) %collective-permute-start.28) | collective-permute-done | bytes 262176 | tf_op jit(solution)/shard_map/ppermute | solution.py:83
  402.6 3.3 collective-permute-done.24
  408.9 4.0 multiply_reduce_fusion
  420.5 3.4 copy-done.9
  426.1 4.9 bitcast_convert_fusion
  431.0 4.4 maximum_convert_fusion
  440.0 3.2 convert_add_fusion.8
  443.2 14.9 %collective-permute-done.38 = bf16[2,128,512]{2,1,0:T(8,128)(2,1)S(1)} collective-permute-done((bf16[2,128,512]{2,1,0:T(8,128)(2,1)S(1)}, bf16[2,128,512]{2,1,0:T(8,128)(2,1)S(1)}, u32[]{:S(2)}, u32[]{:S(2)}) %collective-permute-start.38) | collective-permute-done | bytes 262176 | tf_op jit(solution)/shard_map/ppermute | solution.py:83
  458.5 5.0 collective-permute-done.37
  465.7 12.0 %collective-permute-done.36 = f32[4,1024]{1,0:T(4,128)S(1)} collective-permute-done((f32[4,1024]{1,0:T(4,128)S(1)}, f32[4,1024]{1,0:T(4,128)S(1)}, u32[]{:S(2)}, u32[]{:S(2)}) %collective-permute-start.36) | collective-permute-done | bytes 16416 | tf_op jit(solution)/shard_map/ppermute | solution.py:1047
  482.1 4.8 fusion.50
  (401 shorter events, 165.7 us)
Async XLA Ops:
  7.2 84.6 %all-gather.4.cloned.1.call-start = ((), (), s32[]{:S(2)}) async-start(), calls=%async_computation.1 | async-start | bytes 4456448 | tf_op jit(solution)/shard_map/all_gather | solution.py:735
  7.2 27.3 %collective-permute-start = (bf16[512,1024]{1,0:T(8,128)(2,1)}, bf16[512,1024]{1,0:T(8,128)(2,1)}, u32[]{:S(2)}, u32[]{:S(2)}) collective-permute-start(bf16[512,1024]{1,0:T(8,128)(2,1)} %param.20), channel_id=1, source_target_pairs={{0,1},{1,0},{2,3},{3,2},{4,5},{5,4},{6,7},{7,6},{8,9},{9,8},{10,11... | collective-permute-start | bytes 3145736 | tf_op jit(solution)/shard_map/ppermute | solution.py:58
  12.8 26.6 %collective-permute-start.3 = (bf16[4,64,512]{2,1,0:T(8,128)(2,1)S(1)}, bf16[4,64,512]{2,1,0:T(8,128)(2,1)}, u32[]{:S(2)}, u32[]{:S(2)}) collective-permute-start(bf16[4,64,512]{2,1,0:T(8,128)(2,1)S(1)} %fusion.75), channel_id=1, source_target_pairs={{0,1},{1,0},{2,3},{3,2},{4,5},{5,4},{6,7},{7,6},{8,9},{9,8},{10,11... | collective-permute-start | bytes 786440 | tf_op jit(solution)/shard_map/ppermute | solution.py:58
  39.4 258.9 %reduce-scatter.2.cloned.1.call-start = ((), (), s32[]{:S(2)}) async-start(), calls=%async_computation.2 | async-start | bytes 8912896 | tf_op jit(solution)/shard_map/reduce_scatter | solution.py:882
  39.5 24.7 %collective-permute-start.1 = (bf16[512,1024]{1,0:T(8,128)(2,1)}, bf16[512,1024]{1,0:T(8,128)(2,1)}, u32[]{:S(2)}, u32[]{:S(2)}) collective-permute-start(bf16[512,1024]{1,0:T(8,128)(2,1)} %fusion.8.rows_ref), channel_id=1, source_target_pairs={{0,1},{1,0},{2,3},{3,2},{4,5},{5,4},{6,7},{7,6},{8,9},{9,8},{10,11... | collective-permute-start | bytes 3145736 | tf_op jit(solution)/shard_map/ppermute | solution.py:58
  64.2 16.0 %collective-permute-start.4 = (bf16[256,1024]{1,0:T(8,128)(2,1)}, bf16[256,1024]{1,0:T(8,128)(2,1)S(1)}, u32[]{:S(2)}, u32[]{:S(2)}) collective-permute-start(bf16[256,1024]{1,0:T(8,128)(2,1)} %get-tuple-element.146), channel_id=1, source_target_pairs={{0,1},{1,0},{2,3},{3,2},{4,5},{5,4},{6,7},{7,6},{8,9},{9,8},{10,11... | collective-permute-start | bytes 1572872 | tf_op jit(solution)/shard_map/ppermute | solution.py:58
  79.5 23.7 %collective-permute-start.2 = (bf16[512,1024]{1,0:T(8,128)(2,1)}, bf16[512,1024]{1,0:T(8,128)(2,1)}, u32[]{:S(2)}, u32[]{:S(2)}) collective-permute-start(bf16[512,1024]{1,0:T(8,128)(2,1)} %get-tuple-element.144), channel_id=1, source_target_pairs={{0,1},{1,0},{2,3},{3,2},{4,5},{5,4},{6,7},{7,6},{8,9},{9,8},{10,11... | collective-permute-start | bytes 3145736 | tf_op jit(solution)/shard_map/ppermute | solution.py:63
  106.2 15.2 %collective-permute-start.5 = (bf16[256,1024]{1,0:T(8,128)(2,1)S(1)}, bf16[256,1024]{1,0:T(8,128)(2,1)S(1)}, u32[]{:S(2)}, u32[]{:S(2)}) collective-permute-start(bf16[256,1024]{1,0:T(8,128)(2,1)S(1)} %copy-done.65), channel_id=1, source_target_pairs={{0,1},{1,0},{2,3},{3,2},{4,5},{5,4},{6,7},{7,6},{8,9},{9,8},{10,11... | collective-permute-start | bytes 1572872 | tf_op jit(solution)/shard_map/ppermute | solution.py:58
  123.8 14.9 %collective-permute-start.7 = (bf16[256,1024]{1,0:T(8,128)(2,1)S(1)}, bf16[256,1024]{1,0:T(8,128)(2,1)S(1)}, u32[]{:S(2)}, u32[]{:S(2)}) collective-permute-start(bf16[256,1024]{1,0:T(8,128)(2,1)S(1)} %get-tuple-element.313), channel_id=1, source_target_pairs={{0,1},{1,0},{2,3},{3,2},{4,5},{5,4},{6,7},{7,6},{8,9},{9,8},{10,11... | collective-permute-start | bytes 1572872 | tf_op jit(solution)/shard_map/ppermute | solution.py:58
  125.4 25.3 %collective-permute-start.6 = (bf16[256,1024]{1,0:T(8,128)(2,1)}, bf16[256,1024]{1,0:T(8,128)(2,1)}, u32[]{:S(2)}, u32[]{:S(2)}) collective-permute-start(bf16[256,1024]{1,0:T(8,128)(2,1)} %get-tuple-element.314), channel_id=1, source_target_pairs={{0,1},{1,0},{2,3},{3,2},{4,5},{5,4},{6,7},{7,6},{8,9},{9,8},{10,11... | collective-permute-start | bytes 1572872 | tf_op jit(solution)/shard_map/ppermute | solution.py:58
  148.0 14.6 %collective-permute-start.8 = (bf16[256,1024]{1,0:T(8,128)(2,1)}, bf16[256,1024]{1,0:T(8,128)(2,1)}, u32[]{:S(2)}, u32[]{:S(2)}) collective-permute-start(bf16[256,1024]{1,0:T(8,128)(2,1)} %get-tuple-element.162), channel_id=1, source_target_pairs={{0,1},{1,0},{2,3},{3,2},{4,5},{5,4},{6,7},{7,6},{8,9},{9,8},{10,11... | collective-permute-start | bytes 1572872 | tf_op jit(solution)/shard_map/ppermute | solution.py:63
  159.4 10.5 %collective-permute-start.9 = (bf16[256,1024]{1,0:T(8,128)(2,1)}, bf16[256,1024]{1,0:T(8,128)(2,1)S(1)}, u32[]{:S(2)}, u32[]{:S(2)}) collective-permute-start(bf16[256,1024]{1,0:T(8,128)(2,1)} %get-tuple-element.174), channel_id=1, source_target_pairs={{0,1},{1,0},{2,3},{3,2},{4,5},{5,4},{6,7},{7,6},{8,9},{9,8},{10,11... | collective-permute-start | bytes 1572872 | tf_op jit(solution)/shard_map/ppermute | solution.py:63
  179.5 241.1 %all-gather.6.cloned.1.call-start = ((), (), s32[]{:S(2)}) async-start(), calls=%async_computation.3 | async-start | bytes 8912896 | tf_op jit(solution)/shard_map/all_gather | solution.py:975
  226.2 16.6 %collective-permute-start.12 = (bf16[2,2,512,512]{3,2,1,0:T(8,128)(2,1)}, bf16[2,2,512,512]{3,2,1,0:T(8,128)(2,1)}, u32[]{:S(2)}, u32[]{:S(2)}) collective-permute-start(bf16[2,2,512,512]{3,2,1,0:T(8,128)(2,1)} %bitcast.34), channel_id=1, source_target_pairs={{0,2},{2,0},{4,6},{6,4},{8,10},{10,8},{12,14},{14,12},{16,18},{18,... | collective-permute-start | bytes 6291464 | tf_op jit(solution)/shard_map/ppermute | solution.py:83
  226.2 22.1 %collective-permute-start.11 = (bf16[2,2,512,512]{3,2,1,0:T(8,128)(2,1)}, bf16[2,2,512,512]{3,2,1,0:T(8,128)(2,1)}, u32[]{:S(2)}, u32[]{:S(2)}) collective-permute-start(bf16[2,2,512,512]{3,2,1,0:T(8,128)(2,1)} %bitcast.32), channel_id=1, source_target_pairs={{0,2},{2,0},{4,6},{6,4},{8,10},{10,8},{12,14},{14,12},{16,18},{18,... | collective-permute-start | bytes 6291464 | tf_op jit(solution)/shard_map/ppermute | solution.py:83
  226.8 25.4 %collective-permute-start.10 = (bf16[512,1024]{1,0:T(8,128)(2,1)}, bf16[512,1024]{1,0:T(8,128)(2,1)}, u32[]{:S(2)}, u32[]{:S(2)}) collective-permute-start(bf16[512,1024]{1,0:T(8,128)(2,1)} %get-tuple-element.212), channel_id=1, source_target_pairs={{0,1},{1,0},{2,3},{3,2},{4,5},{5,4},{6,7},{7,6},{8,9},{9,8},{10,11... | collective-permute-start | bytes 3145736 | tf_op jit(solution)/shard_map/ppermute | solution.py:58
  246.8 35.2 %collective-permute-start.14 = (bf16[2,2,256,512]{3,2,1,0:T(8,128)(2,1)}, bf16[2,2,256,512]{3,2,1,0:T(8,128)(2,1)}, u32[]{:S(2)}, u32[]{:S(2)}) collective-permute-start(bf16[2,2,256,512]{3,2,1,0:T(8,128)(2,1)} %bitcast.38), channel_id=1, source_target_pairs={{0,4},{2,6},{4,0},{6,2},{8,12},{10,14},{12,8},{14,10},{16,20},{18,... | collective-permute-start | bytes 3145736 | tf_op jit(solution)/shard_map/ppermute | solution.py:83
  251.6 33.2 %collective-permute-start.13 = (bf16[2,512,512]{2,1,0:T(8,128)(2,1)}, bf16[2,512,512]{2,1,0:T(8,128)(2,1)}, u32[]{:S(2)}, u32[]{:S(2)}) collective-permute-start(bf16[2,512,512]{2,1,0:T(8,128)(2,1)} %slice_bitcast_fusion.6), channel_id=1, source_target_pairs={{0,1},{1,0},{2,3},{3,2},{4,5},{5,4},{6,7},{7,6},{8,9},{9,8},{10,11... | collective-permute-start | bytes 3145736 | tf_op jit(solution)/shard_map/ppermute | solution.py:63
  274.3 22.7 %collective-permute-start.16 = (bf16[2,512,512]{2,1,0:T(8,128)(2,1)S(1)}, bf16[2,512,512]{2,1,0:T(8,128)(2,1)S(1)}, u32[]{:S(2)}, u32[]{:S(2)}) collective-permute-start(bf16[2,512,512]{2,1,0:T(8,128)(2,1)S(1)} %fusion.49), channel_id=1, source_target_pairs={{0,2},{2,0},{4,6},{6,4},{8,10},{10,8},{12,14},{14,12},{16,18},{18,... | collective-permute-start | bytes 3145736 | tf_op jit(solution)/shard_map/ppermute | solution.py:83
  298.4 182.4 %all-gather.8.cloned.1.call-start = ((), (), s32[]{:S(2)}) async-start(), calls=%async_computation.4 | async-start | bytes 4456448 | tf_op jit(solution)/shard_map/all_gather | solution.py:1018
  298.8 6.6 %collective-permute-start.15 = (bf16[2,512,512]{2,1,0:T(8,128)(2,1)}, bf16[2,512,512]{2,1,0:T(8,128)(2,1)}, u32[]{:S(2)}, u32[]{:S(2)}) collective-permute-start(bf16[2,512,512]{2,1,0:T(8,128)(2,1)} %dynamic-slice_bitcast_fusion), channel_id=1, source_target_pairs={{0,2},{2,0},{4,6},{6,4},{8,10},{10,8},{12,14},{14,12},{16,18},{18,... | collective-permute-start | bytes 3145736 | tf_op jit(solution)/shard_map/ppermute | solution.py:83
  303.2 29.5 %collective-permute-start.19 = (bf16[2,2,128,512]{3,2,1,0:T(8,128)(2,1)S(1)}, bf16[2,2,128,512]{3,2,1,0:T(8,128)(2,1)S(1)}, u32[]{:S(2)}, u32[]{:S(2)}) collective-permute-start(bf16[2,2,128,512]{3,2,1,0:T(8,128)(2,1)S(1)} %bitcast.315), channel_id=1, source_target_pairs={{0,8},{2,10},{4,12},{6,14},{8,0},{10,2},{12,4},{14,6},{16,24},{18,... | collective-permute-start | bytes 1572872 | tf_op jit(solution)/shard_map/ppermute | solution.py:83
  303.3 31.7 %collective-permute-start.18 = (bf16[2,256,512]{2,1,0:T(8,128)(2,1)S(1)}, bf16[2,256,512]{2,1,0:T(8,128)(2,1)S(1)}, u32[]{:S(2)}, u32[]{:S(2)}) collective-permute-start(bf16[2,256,512]{2,1,0:T(8,128)(2,1)S(1)} %bitcast.314), channel_id=1, source_target_pairs={{0,4},{2,6},{4,0},{6,2},{8,12},{10,14},{12,8},{14,10},{16,20},{18,... | collective-permute-start | bytes 1572872 | tf_op jit(solution)/shard_map/ppermute | solution.py:83
  304.1 32.6 %collective-permute-start.23 = (bf16[2,256,512]{2,1,0:T(8,128)(2,1)S(1)}, bf16[2,256,512]{2,1,0:T(8,128)(2,1)S(1)}, u32[]{:S(2)}, u32[]{:S(2)}) collective-permute-start(bf16[2,256,512]{2,1,0:T(8,128)(2,1)S(1)} %copy-done.62), channel_id=1, source_target_pairs={{0,4},{2,6},{4,0},{6,2},{8,12},{10,14},{12,8},{14,10},{16,20},{18,... | collective-permute-start | bytes 1572872 | tf_op jit(solution)/shard_map/ppermute | solution.py:83
  307.2 46.2 %collective-permute-start.22 = (bf16[2,256,512]{2,1,0:T(8,128)(2,1)S(1)}, bf16[2,256,512]{2,1,0:T(8,128)(2,1)S(1)}, u32[]{:S(2)}, u32[]{:S(2)}) collective-permute-start(bf16[2,256,512]{2,1,0:T(8,128)(2,1)S(1)} %dynamic-slice_bitcast_fusion.1), channel_id=1, source_target_pairs={{0,8},{2,10},{4,12},{6,14},{8,0},{10,2},{12,4},{14,6},{16,24},{18,... | collective-permute-start | bytes 1572872 | tf_op jit(solution)/shard_map/ppermute | solution.py:83
  310.0 88.9 %collective-permute-start.26 = (bf16[512,1024]{1,0:T(8,128)(2,1)S(1)}, bf16[512,1024]{1,0:T(8,128)(2,1)S(1)}, u32[]{:S(2)}, u32[]{:S(2)}) collective-permute-start(bf16[512,1024]{1,0:T(8,128)(2,1)S(1)} %convolution_convert_fusion.8), channel_id=1, source_target_pairs={{0,1},{1,0},{2,3},{3,2},{4,5},{5,4},{6,7},{7,6},{8,9},{9,8},{10,11... | collective-permute-start | bytes 3145736 | tf_op jit(solution)/shard_map/ppermute | solution.py:63
  332.7 76.2 %collective-permute-start.17 = (bf16[512,1024]{1,0:T(8,128)(2,1)}, bf16[512,1024]{1,0:T(8,128)(2,1)}, u32[]{:S(2)}, u32[]{:S(2)}) collective-permute-start(bf16[512,1024]{1,0:T(8,128)(2,1)} %slice.412), channel_id=1, source_target_pairs={{0,1},{1,0},{2,3},{3,2},{4,5},{5,4},{6,7},{7,6},{8,9},{9,8},{10,11... | collective-permute-start | bytes 3145736 | tf_op jit(solution)/shard_map/ppermute | solution.py:63
  335.0 21.5 %collective-permute-start.21 = (bf16[2,2,64,512]{3,2,1,0:T(8,128)(2,1)S(1)}, bf16[2,2,64,512]{3,2,1,0:T(8,128)(2,1)S(1)}, u32[]{:S(2)}, u32[]{:S(2)}) collective-permute-start(bf16[2,2,64,512]{3,2,1,0:T(8,128)(2,1)S(1)} %dynamic-slice_bitcast_fusion.5), channel_id=1, source_target_pairs={{0,16},{2,18},{4,20},{6,22},{8,24},{10,26},{12,28},{14,30},{16,0},... | collective-permute-start | bytes 786440 | tf_op jit(solution)/shard_map/ppermute | solution.py:83
  336.7 43.5 %collective-permute-start.20 = (bf16[2,128,512]{2,1,0:T(8,128)(2,1)S(1)}, bf16[2,128,512]{2,1,0:T(8,128)(2,1)S(1)}, u32[]{:S(2)}, u32[]{:S(2)}) collective-permute-start(bf16[2,128,512]{2,1,0:T(8,128)(2,1)S(1)} %bitcast.316), channel_id=1, source_target_pairs={{0,8},{2,10},{4,12},{6,14},{8,0},{10,2},{12,4},{14,6},{16,24},{18,... | collective-permute-start | bytes 786440 | tf_op jit(solution)/shard_map/ppermute | solution.py:83
  353.4 43.6 %collective-permute-start.28 = (bf16[2,128,512]{2,1,0:T(8,128)(2,1)S(1)}, bf16[2,128,512]{2,1,0:T(8,128)(2,1)S(1)}, u32[]{:S(2)}, u32[]{:S(2)}) collective-permute-start(bf16[2,128,512]{2,1,0:T(8,128)(2,1)S(1)} %dynamic-slice_bitcast_fusion.4), channel_id=1, source_target_pairs={{0,8},{2,10},{4,12},{6,14},{8,0},{10,2},{12,4},{14,6},{16,24},{18,... | collective-permute-start | bytes 786440 | tf_op jit(solution)/shard_map/ppermute | solution.py:83
  356.5 42.2 %collective-permute-start.27 = (bf16[2,128,512]{2,1,0:T(8,128)(2,1)S(1)}, bf16[2,128,512]{2,1,0:T(8,128)(2,1)S(1)}, u32[]{:S(2)}, u32[]{:S(2)}) collective-permute-start(bf16[2,128,512]{2,1,0:T(8,128)(2,1)S(1)} %dynamic-slice_bitcast_fusion.3), channel_id=1, source_target_pairs={{0,16},{2,18},{4,20},{6,22},{8,24},{10,26},{12,28},{14,30},{16,0},... | collective-permute-start | bytes 786440 | tf_op jit(solution)/shard_map/ppermute | solution.py:83
  380.2 22.4 %collective-permute-start.25 = (bf16[2,64,512]{2,1,0:T(8,128)(2,1)S(1)}, bf16[2,64,512]{2,1,0:T(8,128)(2,1)S(1)}, u32[]{:S(2)}, u32[]{:S(2)}) collective-permute-start(bf16[2,64,512]{2,1,0:T(8,128)(2,1)S(1)} %slice_bitcast_fusion.12), channel_id=1, source_target_pairs={{0,1},{1,0},{2,3},{3,2},{4,5},{5,4},{6,7},{7,6},{8,9},{9,8},{10,11... | collective-permute-start | bytes 393224 | tf_op jit(solution)/shard_map/ppermute | solution.py:63
  397.0 9.0 %collective-permute-start.24 = (bf16[2,64,512]{2,1,0:T(8,128)(2,1)S(1)}, bf16[2,64,512]{2,1,0:T(8,128)(2,1)S(1)}, u32[]{:S(2)}, u32[]{:S(2)}) collective-permute-start(bf16[2,64,512]{2,1,0:T(8,128)(2,1)S(1)} %dynamic-slice_bitcast_fusion.8), channel_id=1, source_target_pairs={{0,16},{2,18},{4,20},{6,22},{8,24},{10,26},{12,28},{14,30},{16,0},... | collective-permute-start | bytes 393224 | tf_op jit(solution)/shard_map/ppermute | solution.py:83
  406.8 7.5 %collective-permute-start.31 = (bf16[2,64,512]{2,1,0:T(8,128)(2,1)}, bf16[2,64,512]{2,1,0:T(8,128)(2,1)S(1)}, u32[]{:S(2)}, u32[]{:S(2)}) collective-permute-start(bf16[2,64,512]{2,1,0:T(8,128)(2,1)} %dynamic-slice_bitcast_fusion.7), channel_id=1, source_target_pairs={{0,16},{2,18},{4,20},{6,22},{8,24},{10,26},{12,28},{14,30},{16,0},... | collective-permute-start | bytes 393224 | tf_op jit(solution)/shard_map/ppermute | solution.py:83
  406.9 31.6 %collective-permute-start.35 = (bf16[512,1024]{1,0:T(8,128)(2,1)}, bf16[512,1024]{1,0:T(8,128)(2,1)}, u32[]{:S(2)}, u32[]{:S(2)}) collective-permute-start(bf16[512,1024]{1,0:T(8,128)(2,1)} %add_convert_fusion), channel_id=1, source_target_pairs={{0,1},{1,0},{2,3},{3,2},{4,5},{5,4},{6,7},{7,6},{8,9},{9,8},{10,11... | collective-permute-start | bytes 3145736 | tf_op jit(solution)/shard_map/ppermute | solution.py:63
  408.7 7.0 %collective-permute-start.30 = (bf16[2,64,512]{2,1,0:T(8,128)(2,1)S(1)}, bf16[2,64,512]{2,1,0:T(8,128)(2,1)S(1)}, u32[]{:S(2)}, u32[]{:S(2)}) collective-permute-start(bf16[2,64,512]{2,1,0:T(8,128)(2,1)S(1)} %dynamic-slice_bitcast_fusion.6), channel_id=1, source_target_pairs={{0,4},{2,6},{4,0},{6,2},{8,12},{10,14},{12,8},{14,10},{16,20},{18,... | collective-permute-start | bytes 393224 | tf_op jit(solution)/shard_map/ppermute | solution.py:83
  414.3 21.1 %collective-permute-start.34 = (bf16[2,64,512]{2,1,0:T(8,128)(2,1)S(1)}, bf16[2,64,512]{2,1,0:T(8,128)(2,1)S(1)}, u32[]{:S(2)}, u32[]{:S(2)}) collective-permute-start(bf16[2,64,512]{2,1,0:T(8,128)(2,1)S(1)} %fusion.76), channel_id=1, source_target_pairs={{0,16},{2,18},{4,20},{6,22},{8,24},{10,26},{12,28},{14,30},{16,0},... | collective-permute-start | bytes 393224 | tf_op jit(solution)/shard_map/ppermute | solution.py:83
  417.3 18.9 %collective-permute-start.33 = (bf16[2,64,512]{2,1,0:T(8,128)(2,1)S(1)}, bf16[2,64,512]{2,1,0:T(8,128)(2,1)S(1)}, u32[]{:S(2)}, u32[]{:S(2)}) collective-permute-start(bf16[2,64,512]{2,1,0:T(8,128)(2,1)S(1)} %fusion.77), channel_id=1, source_target_pairs={{0,4},{2,6},{4,0},{6,2},{8,12},{10,14},{12,8},{14,10},{16,20},{18,... | collective-permute-start | bytes 393224 | tf_op jit(solution)/shard_map/ppermute | solution.py:83
  419.4 19.0 %collective-permute-start.32 = (f32[4,1024]{1,0:T(4,128)S(1)}, f32[4,1024]{1,0:T(4,128)S(1)}, u32[]{:S(2)}, u32[]{:S(2)}) collective-permute-start(f32[4,1024]{1,0:T(4,128)S(1)} %fusion.86), channel_id=1, source_target_pairs={{0,4},{2,6},{4,0},{6,2},{8,12},{10,14},{12,8},{14,10},{16,20},{18,... | collective-permute-start | bytes 49160 | tf_op jit(solution)/shard_map/ppermute | solution.py:1047
  435.5 22.6 %collective-permute-start.38 = (bf16[2,128,512]{2,1,0:T(8,128)(2,1)S(1)}, bf16[2,128,512]{2,1,0:T(8,128)(2,1)S(1)}, u32[]{:S(2)}, u32[]{:S(2)}) collective-permute-start(bf16[2,128,512]{2,1,0:T(8,128)(2,1)S(1)} %pad_maximum_fusion.9), channel_id=1, source_target_pairs={{0,8},{2,10},{4,12},{6,14},{8,0},{10,2},{12,4},{14,6},{16,24},{18,... | collective-permute-start | bytes 786440 | tf_op jit(solution)/shard_map/ppermute | solution.py:83
  436.2 27.3 %collective-permute-start.37 = (bf16[2,128,512]{2,1,0:T(8,128)(2,1)S(1)}, bf16[2,128,512]{2,1,0:T(8,128)(2,1)S(1)}, u32[]{:S(2)}, u32[]{:S(2)}) collective-permute-start(bf16[2,128,512]{2,1,0:T(8,128)(2,1)S(1)} %pad_maximum_fusion.10), channel_id=1, source_target_pairs={{0,16},{2,18},{4,20},{6,22},{8,24},{10,26},{12,28},{14,30},{16,0},... | collective-permute-start | bytes 786440 | tf_op jit(solution)/shard_map/ppermute | solution.py:83
  458.2 19.6 %collective-permute-start.41 = (bf16[2,256,512]{2,1,0:T(8,128)(2,1)S(1)}, bf16[2,256,512]{2,1,0:T(8,128)(2,1)S(1)}, u32[]{:S(2)}, u32[]{:S(2)}) collective-permute-start(bf16[2,256,512]{2,1,0:T(8,128)(2,1)S(1)} %pad_maximum_fusion.7), channel_id=1, source_target_pairs={{0,4},{2,6},{4,0},{6,2},{8,12},{10,14},{12,8},{14,10},{16,20},{18,... | collective-permute-start | bytes 1572872 | tf_op jit(solution)/shard_map/ppermute | solution.py:83
  463.7 15.4 %collective-permute-start.40 = (bf16[2,256,512]{2,1,0:T(8,128)(2,1)S(1)}, bf16[2,256,512]{2,1,0:T(8,128)(2,1)S(1)}, u32[]{:S(2)}, u32[]{:S(2)}) collective-permute-start(bf16[2,256,512]{2,1,0:T(8,128)(2,1)S(1)} %pad_maximum_fusion.8), channel_id=1, source_target_pairs={{0,8},{2,10},{4,12},{6,14},{8,0},{10,2},{12,4},{14,6},{16,24},{18,... | collective-permute-start | bytes 1572872 | tf_op jit(solution)/shard_map/ppermute | solution.py:83
  463.7 14.0 %collective-permute-start.36 = (f32[4,1024]{1,0:T(4,128)S(1)}, f32[4,1024]{1,0:T(4,128)S(1)}, u32[]{:S(2)}, u32[]{:S(2)}) collective-permute-start(f32[4,1024]{1,0:T(4,128)S(1)} %fusion.158), channel_id=1, source_target_pairs={{0,8},{2,10},{4,12},{6,14},{8,0},{10,2},{12,4},{14,6},{16,24},{18,... | collective-permute-start | bytes 49160 | tf_op jit(solution)/shard_map/ppermute | solution.py:1047
  479.0 14.5 %collective-permute-start.44 = (bf16[2,512,512]{2,1,0:T(8,128)(2,1)}, bf16[2,512,512]{2,1,0:T(8,128)(2,1)}, u32[]{:S(2)}, u32[]{:S(2)}) collective-permute-start(bf16[2,512,512]{2,1,0:T(8,128)(2,1)} %pad_maximum_fusion.5), channel_id=1, source_target_pairs={{0,2},{2,0},{4,6},{6,4},{8,10},{10,8},{12,14},{14,12},{16,18},{18,... | collective-permute-start | bytes 3145736 | tf_op jit(solution)/shard_map/ppermute | solution.py:83
  480.3 13.2 %collective-permute-start.43 = (bf16[2,512,512]{2,1,0:T(8,128)(2,1)}, bf16[2,512,512]{2,1,0:T(8,128)(2,1)}, u32[]{:S(2)}, u32[]{:S(2)}) collective-permute-start(bf16[2,512,512]{2,1,0:T(8,128)(2,1)} %pad_maximum_fusion.6), channel_id=1, source_target_pairs={{0,2},{2,0},{4,6},{6,4},{8,10},{10,8},{12,14},{14,12},{16,18},{18,... | collective-permute-start | bytes 3145736 | tf_op jit(solution)/shard_map/ppermute | solution.py:83
  486.9 4.8 collective-permute-start.39
  491.7 4.9 collective-permute-start.42
  (83 other events, 578.3 us)
Sparse Core Ops, SparseCore 0:
  39.5 52.1 all-gather.3
  179.6 114.2 reduce-scatter.1
  298.5 106.6 all-gather.5
  407.8 61.5 all-gather.7
